TPU v7x, 32 devices: a whole 2x2x4 slice. The times are simulated.
32 devices in a mesh: dp: 8 (over z, y), space: 4 (over x, core).
Axes of the slice: x: 2, y: 2, z: 4, core: 2. Of those that a mesh axis runs over, the one named last changes fastest.
Arguments:
- section_three: bfloat16 [8, 16, 32, 768], P('dp', 'space'), may hold values from -6 to 6
- dw_kernel: float32 [7, 7, 768], replicated, may hold values from -0.875 to 0.875
- dw_bias: float32 [768], replicated, may hold values from -3 to 3
- mix_gain: float32 [768], replicated, may hold values from 0.1 to 1.9
- w_expand: bfloat16 [768, 1536], replicated, may hold values from -0.21875 to 0.21875
- w_reduce: bfloat16 [1536, 768], replicated, may hold values from -0.15625 to 0.15625
- layer_scale: float32 [768], replicated, may hold values from 0.3 to 1.5
- down_gain: float32 [768], replicated, may hold values from 0.1 to 1.9
- w_down: bfloat16 [3072, 1536], P(None, 'space'), may hold values from -0.109375 to 0.109375
- owner_table: int32 [8, 128, 1], P('dp'), may hold values from 0 to 7; in each aligned block of 128 rows (0 to 127, 128 to 255, ..., all dimensions but the last counted through in order) at most 16 rows name the same one
- grad_packed: bfloat16 [8, 128, 1536], P('dp', None, 'space'), may hold values from -6 to 6
Outputs:
- packed_tokens: bfloat16 [8, 128, 1536], P('dp', None, 'space')
- grad_mixed: bfloat16 [8, 16, 32, 768], P('dp', 'space')
Inputs may be any that keep to these rules, and one draw needn't show every extreme that they name: `owner_table`: among the 128 tokens of one screenshot no owner is named more than 16 times, a bound that some block reaches.
All inputs are finite; a program needn't handle non-finite values.
Results may differ from a plain program's by a relative error of at most 0.018.
Values may be sent and summed in bfloat16 or wider, within the bound.
No kernel may reach another device: no remote copies, remote signals or barrier semaphores. Data moves between devices by JAX's collectives and lax.ppermute only.
A program may use at most 64 MiB of HBM per device.

v0:
```python
import jax
import jax.numpy as jnp
from jax import lax
from jax.sharding import PartitionSpec as P

KS = 7


def padded_2(cells, sides, width):
    for axis, dim in sides:
        count = lax.axis_size(axis)
        ends = count - 1
        head = lax.slice_in_dim(cells, 0, width, axis=dim)
        tail = lax.slice_in_dim(cells, cells.shape[dim] - width, cells.shape[dim], axis=dim)
        cells = jnp.concatenate(
            [
                lax.ppermute(tail, axis, [(i, (i + 1) % count) for i in range(ends)]),
                cells,
                lax.ppermute(head, axis, [((i + 1) % count, i) for i in range(ends)]),
            ],
            axis=dim,
        )
    return cells


def depthwise(padded, kernel, height, width):
    total = jnp.zeros((height, width, kernel.shape[2]), jnp.float32)
    for offset_y in range(KS):
        for offset_x in range(KS):
            total = (
                total
                + padded[offset_y : offset_y + height, offset_x : offset_x + width]
                * kernel[offset_y, offset_x]
            )
    return total


def layer_norm(values):
    center = values - jnp.mean(values, axis=-1, keepdims=True)
    inv_std = lax.rsqrt(jnp.mean(center * center, axis=-1, keepdims=True) + 1e-06)
    return (center * inv_std, inv_std)


def norm_back(grad, normed, inv_std, gain):
    scaled = grad * gain
    return inv_std * (
        scaled
        - jnp.mean(scaled, axis=-1, keepdims=True)
        - normed * jnp.mean(scaled * normed, axis=-1, keepdims=True)
    )


def gelu_slope(pre):
    cumulative = 0.5 * (1.0 + lax.erf(pre * 0.7071067811865476))
    density = jnp.exp(-0.5 * pre * pre) * 0.3989422804014327
    return cumulative + pre * density


def to_patches(grid):
    height, width, channels = grid.shape
    return (
        grid.reshape(height // 2, 2, width // 2, 2, channels)
        .transpose(0, 2, 1, 3, 4)
        .reshape(height // 2 * (width // 2), 4 * channels)
    )


def from_patches(flat, height, width, channels):
    return (
        flat.reshape(height // 2, width // 2, 2, 2, channels)
        .transpose(0, 2, 1, 3, 4)
        .reshape(height, width, channels)
    )


def slot_index(targets, owners_count, capacity):
    onehot = (targets[:, None] == jnp.arange(owners_count, dtype=jnp.int32)[None, :]).astype(
        jnp.int32
    )
    earlier = jnp.cumsum(onehot, axis=0) - onehot
    ranking = jnp.sum(earlier * onehot, axis=1)
    return targets * capacity + ranking


def on_device(
    section_three,
    dw_kernel,
    dw_bias,
    mix_gain,
    w_expand,
    w_reduce,
    layer_scale,
    down_gain,
    w_down,
    owner_table,
    grad_packed,
):
    owners_count = lax.axis_size("dp")
    slot_count = grad_packed.shape[1]
    capacity = slot_count // owners_count
    band_height = section_three.shape[1]
    band_width = section_three.shape[2]
    channels = section_three.shape[3]
    half = KS // 2
    extended = padded_2(section_three, (("space", 1),), half)
    padded = jnp.pad(extended[0].astype(jnp.float32), ((0, 0), (half, half), (0, 0)))
    mixed = (depthwise(padded, dw_kernel, band_height, band_width) + dw_bias).reshape(
        band_height * band_width, channels
    )
    normed_one, inv_one = layer_norm(mixed)
    first = (normed_one * mix_gain).astype(jnp.bfloat16)
    pre = jnp.dot(first, w_expand, preferred_element_type=jnp.float32)
    hidden = jax.nn.gelu(pre, approximate=False).astype(jnp.bfloat16)
    residual = section_three[0].astype(jnp.float32).reshape(band_height * band_width, channels)
    block_out = residual + layer_scale * jnp.dot(
        hidden, w_reduce, preferred_element_type=jnp.float32
    )
    normed_two, inv_two = layer_norm(block_out)
    second = (normed_two * down_gain).astype(jnp.bfloat16)
    patches = to_patches(second.reshape(band_height, band_width, channels))
    tokens = jnp.dot(
        lax.all_gather(patches, "space", axis=0, tiled=True),
        w_down,
        preferred_element_type=jnp.float32,
    ).astype(jnp.bfloat16)
    targets = owner_table[0, :, 0]
    send_pos = slot_index(targets, owners_count, capacity)
    send_buffer = jnp.zeros((slot_count, tokens.shape[1]), jnp.bfloat16).at[send_pos].set(tokens)
    arrived = lax.all_to_all(send_buffer, "dp", split_axis=0, concat_axis=0, tiled=True)
    returned = lax.all_to_all(grad_packed[0], "dp", split_axis=0, concat_axis=0, tiled=True)
    grad_tokens = returned[send_pos]
    grad_patches = lax.psum_scatter(
        lax.dot_general(
            grad_tokens, w_down, (((1,), (1,)), ((), ())), preferred_element_type=jnp.float32
        ).astype(jnp.bfloat16),
        "space",
        scatter_dimension=0,
        tiled=True,
    ).astype(jnp.float32)
    grad_second = from_patches(grad_patches, band_height, band_width, channels).reshape(
        band_height * band_width, channels
    )
    grad_block = norm_back(grad_second, normed_two, inv_two, down_gain)
    grad_scaled = (grad_block * layer_scale).astype(jnp.bfloat16)
    grad_hidden = lax.dot_general(
        grad_scaled, w_reduce, (((1,), (1,)), ((), ())), preferred_element_type=jnp.float32
    )
    grad_pre = (grad_hidden * gelu_slope(pre)).astype(jnp.bfloat16)
    grad_first = lax.dot_general(
        grad_pre, w_expand, (((1,), (1,)), ((), ())), preferred_element_type=jnp.float32
    )
    grad_mixed = norm_back(grad_first, normed_one, inv_one, mix_gain).astype(jnp.bfloat16)
    return (arrived[None], grad_mixed.reshape(1, band_height, band_width, channels))


def solution(mesh):
    in_specs = (
        P("dp", "space", None, None),
        P(),
        P(),
        P(),
        P(),
        P(),
        P(),
        P(),
        P(None, "space"),
        P("dp", None, None),
        P("dp", None, "space"),
    )
    out_specs = (P("dp", None, "space"), P("dp", "space", None, None))
    return jax.shard_map(
        on_device, mesh=mesh, in_specs=in_specs, out_specs=out_specs, check_vma=False
    )
```

profile of v0, /device:TPU:0, one launch (start us, length us, event | category | flops | bytes accessed | tf_op | source)
XLA Modules:
  0.0 97.8 jit_solution(6100218620952280234)
XLA Ops:
  7.2 0.0 copy-start
  7.2 1.2 %fusion.213 = (bf16[1,3,32,768]{3,2,1,0:T(8,128)(2,1)S(1)}, bf16[1,3,32,768]{3,2,1,0:T(8,128)(2,1)S(1)}) fusion(bf16[1,4,32,768]{3,2,1,0:T(8,128)(2,1)} %param.11), kind=kLoop, calls=%fused_computation.345 | loop fusion | bytes 589824 | tf_op jit(solution)/shard_map/slice | solution.py:14
  8.3 2.4 %collective-permute-start = (bf16[1,3,32,768]{3,2,1,0:T(8,128)(2,1)S(1)}, bf16[1,3,32,768]{3,2,1,0:T(8,128)(2,1)S(1)}, u32[]{:S(2)}, u32[]{:S(2)}) collective-permute-start(bf16[1,3,32,768]{3,2,1,0:T(8,128)(2,1)S(1)} %get-tuple-element.59), channel_id=1, source_target_pairs={{0,1},{1,2},{2,3},{4,5},{5,6},{6,7},{8,9},{9,10},{10,11},{12,13},{... | collective-permute-start | bytes 442376 | tf_op jit(solution)/shard_map/ppermute | solution.py:17
  10.8 1.3 %collective-permute-start.1 = (bf16[1,3,32,768]{3,2,1,0:T(8,128)(2,1)S(1)}, bf16[1,3,32,768]{3,2,1,0:T(8,128)(2,1)S(1)}, u32[]{:S(2)}, u32[]{:S(2)}) collective-permute-start(bf16[1,3,32,768]{3,2,1,0:T(8,128)(2,1)S(1)} %get-tuple-element.60), channel_id=1, source_target_pairs={{1,0},{2,1},{3,2},{5,4},{6,5},{7,6},{9,8},{10,9},{11,10},{13,12},{... | collective-permute-start | bytes 442376 | tf_op jit(solution)/shard_map/ppermute | solution.py:19
  12.1 6.7 %all-to-all-start.1 = ((bf16[8,16,384]{2,1,0:T(8,128)(2,1)}), bf16[8,16,384]{2,1,0:T(8,128)(2,1)S(1)}, u32[]{:S(2)}, u32[]{:S(2)}) async-start(bf16[8,16,384]{2,1,0:T(8,128)(2,1)} %bitcast.116), calls=%async_computation.1 | async-start | bytes 196608 | tf_op jit(solution)/shard_map/all_to_all | solution.py:130
  18.7 0.0 reduce-scatter.2.cloned.1.call-start
  18.8 1.3 %slice_reduce_fusion.48 = (f32[768]{0:T(1024)S(1)}, f32[768]{0:T(1024)S(1)}, f32[768]{0:T(1024)S(1)}, f32[768]{0:T(1024)S(1)}, f32[768]{0:T(1024)S(1)}, /*index=...) fusion(f32[7,7,768]{2,1,0:T(8,128)} %param.12), kind=kLoop, calls=%fused_computation.296 | loop fusion | bytes 116736 | tf_op jit(solution)/shard_map/slice | solution.py:33
  20.1 1.1 %slice_reduce_fusion.46 = (f32[768]{0:T(1024)S(1)}, f32[768]{0:T(1024)S(1)}, f32[768]{0:T(1024)S(1)}, f32[768]{0:T(1024)S(1)}, f32[768]{0:T(1024)S(1)}, /*index=...) fusion(f32[7,7,768]{2,1,0:T(8,128)} %param.12), kind=kLoop, calls=%fused_computation.294 | loop fusion | bytes 67584 | tf_op jit(solution)/shard_map/slice | solution.py:33
  21.2 0.7 fusion.170
  22.0 0.2 reduce_window_sum.11
  22.2 0.8 select_reduce_fusion
  23.0 0.7 fusion.173
  23.7 1.4 %slice_reduce_fusion.47 = (f32[768]{0:T(1024)S(1)}, f32[768]{0:T(1024)S(1)}, f32[768]{0:T(1024)S(1)}, f32[768]{0:T(1024)S(1)}, f32[768]{0:T(1024)S(1)}, /*index=...) fusion(f32[7,7,768]{2,1,0:T(8,128)} %param.12), kind=kLoop, calls=%fused_computation.295 | loop fusion | bytes 116736 | tf_op jit(solution)/shard_map/slice | solution.py:33
  25.1 0.0 collective-permute-done
  25.1 1.1 %fusion.209 = (f32[10,32,768]{2,1,0:T(8,128)S(1)}, f32[1,10,32,768]{3,2,1,0:T(8,128)S(1)}) fusion(bf16[1,3,32,768]{3,2,1,0:T(8,128)(2,1)S(1)} %collective-permute-done.1, bf16[1,4,32,768]{3,2,1,0:T(8,128)(2,1)} %param.11, bf16[1,3,32,768]{3,2,1,0:T(8,128)(2,1)S(1)} %collective-permute-done), kind=kLoop, calls=%fused_computation.342 | loop fusion | flops 737280 | bytes 2457600 | tf_op jit(solution)/shard_map/convert_element_type | solution.py:106
  26.2 0.0 copy-start.5
  26.2 4.5 %fusion.211 = (f32[4,32]{1,0:T(4,128)S(1)}, f32[4,32,768]{2,1,0:T(8,128)S(1)}) fusion(f32[768]{0:T(1024)S(1)} %copy-done.6, f32[768]{0:T(1024)S(1)} %get-tuple-element.51, f32[768]{0:T(1024)S(1)} %get-tuple-element.52, f32[768]{0:T(1024)S(1)} %get-tuple-element.5, f32[768]{0:T(1024)S(1)} %get-tuple-element.6, f32[1,10,32,768]{3,2,1,0:T(8,128)S(1)} %get-tuple-element.56, ...), kind=kLoop, calls=%fused_computation.344 | loop fusion | flops 9731968 | bytes 4282880 | tf_op jit(solution)/shard_map/reduce_sum | solution.py:39
  30.7 0.1 div.29
  30.8 0.2 multiply_reduce_fusion.4
  31.0 0.1 rsqrt.20
  31.0 0.1 multiply_convert_fusion.3
  31.2 0.0 all-to-all-done.1
  31.2 0.9 gather_fusion
  32.1 1.8 %convolution_convert_fusion = bf16[128,3072]{1,0:T(8,128)(2,1)} fusion(bf16[128,384]{1,0:T(8,128)(2,1)S(1)} %gather_fusion, bf16[3072,384]{1,0:T(8,128)(2,1)S(1)} %copy-done), kind=kOutput, calls=%fused_computation.2 | convolution fusion | flops 302383104 | bytes 3244032 | tf_op jit(solution)/shard_map/dot_general | solution.py:133
  33.8 0.0 reduce-scatter.2.cloned.1.call-update
  33.9 0.0 copy-start.7
  33.9 2.3 %fusion.215 = f32[128,1536]{1,0:T(8,128)S(1)} fusion(bf16[128,768]{1,0:T(8,128)(2,1)S(1)} %multiply_convert_fusion.3, bf16[768,1536]{1,0:T(8,128)(2,1)} %param.15), kind=kOutput, calls=%fused_computation.347 | convolution fusion | flops 301989888 | bytes 3342336 | tf_op jit(solution)/shard_map/dot_general | solution.py:112
  36.2 0.1 copy-done.7
  36.4 2.8 %fusion.214 = (f32[128]{0:T(128)S(1)}, f32[128,768]{1,0:T(8,128)}) fusion(bf16[1536,768]{1,0:T(8,128)(2,1)S(1)} %copy-done.7, f32[128,1536]{1,0:T(8,128)S(1)} %fusion.215, f32[768]{0:T(1024)S(1)} %copy-done.8, bf16[128,768]{1,0:T(8,128)(2,1)S(1)} %bitcast.112), kind=kOutput, calls=%fused_computation.346 | convolution fusion | flops 315162496 | bytes 3739136 | tf_op jit(solution)/shard_map/dot_general | solution.py:115
  39.2 1.2 %multiply_reduce_fusion.3 = f32[128]{0:T(128)S(1)} fusion(f32[128,768]{1,0:T(8,128)} %get-tuple-element.62, f32[128]{0:T(128)S(1)} %broadcast_multiply_fusion.5), kind=kLoop, calls=%fused_computation.197 | loop fusion | flops 294784 | bytes 394240 | tf_op jit(solution)/shard_map/reduce_sum | solution.py:40
  40.4 20.8 %reduce-scatter.2.cloned.1.call-done = bf16[32,3072]{1,0:T(8,128)(2,1)} async-done(((bf16[128,3072]{1,0:T(8,128)(2,1)}), bf16[32,3072]{1,0:T(8,128)(2,1)}) %reduce-scatter.2.cloned.1.call-update) | async-done | bytes 196624 | tf_op jit(solution)/shard_map/reduce_scatter | solution.py:132
  61.1 1.3 %reshape.143 = f32[2,16,2,2,768]{4,3,2,1,0:T(2,128)S(1)} reshape(bf16[32,3072]{1,0:T(8,128)(2,1)} %reduce-scatter.2.cloned.1.call-done) | data formatting | bytes 589824 | tf_op jit(solution)/shard_map/transpose | solution.py:71
  62.4 0.8 copy.20
  63.2 2.0 %reshape_reshape.7 = f32[128,768]{1,0:T(8,128)} reshape(f32[2,2,16,2,768]{4,3,2,1,0:T(2,128)} %bitcast.111) | data formatting | bytes 786432 | tf_op jit(solution)/shard_map/reshape;reshape | solution.py:140
  65.3 0.2 multiply_reduce_fusion.2
  65.5 1.3 %multiply_reduce_fusion.1 = (f32[128]{0:T(128)S(1)}, bf16[128,768]{1,0:T(8,128)(2,1)S(1)}) fusion(f32[128,768]{1,0:T(8,128)} %reshape_reshape.7, f32[128,768]{1,0:T(8,128)} %get-tuple-element.62, f32[768]{0:T(1024)S(1)} %copy-done.4, f32[128]{0:T(128)S(1)} %add_rsqrt_fusion.1, f32[128]{0:T(128)S(1)} %broadcast_multiply_fusion.5), kind=kLoop, calls=%fused_computation.194 | loop fusion | flops 688000 | bytes 987648 | tf_op jit(solution)/shard_map/reduce_sum | solution.py:49
  66.8 0.1 div.34
  67.0 0.1 reshape_reshape.6
  67.1 0.1 copy.21
  67.2 0.1 reshape.139
  67.4 8.1 %all_gather.3 = bf16[128,3072]{1,0:T(8,128)(2,1)S(1)} all-gather(bf16[32,3072]{1,0:T(8,128)(2,1)S(1)} %reshape.139), channel_id=1, replica_groups=mesh['dp'=8,'space'=4] {'space'}, dimensions={0}, use_global_device_ids=true | all-gather | bytes 983040 | tf_op jit(solution)/shard_map/all_gather | solution.py:122
  75.5 0.6 convolution_convert_fusion.1
  76.1 1.6 %scatter_custom_fusion = bf16[128,384]{1,0:T(8,128)(2,1)} fusion(s32[128]{0:T(128)S(1)} %fusion.173, bf16[128,384]{1,0:T(8,128)(2,1)S(1)} %convolution_convert_fusion.1, bf16[]{:T(256)} %constant.38.clone.1), kind=kCustom, calls=%fused_computation.244 | custom fusion | bytes 98306 | tf_op jit(solution)/shard_map/scatter | solution.py:128
  77.7 5.5 %all-to-all-start = ((bf16[8,16,384]{2,1,0:T(8,128)(2,1)}), bf16[8,16,384]{2,1,0:T(8,128)(2,1)S(1)}, u32[]{:S(2)}, u32[]{:S(2)}) async-start(bf16[8,16,384]{2,1,0:T(8,128)(2,1)} %bitcast.15), calls=%async_computation | async-start | bytes 196608 | tf_op jit(solution)/shard_map/all_to_all | solution.py:129
  83.2 5.2 %fusion.210 = (f32[128]{0:T(128)S(1)}, f32[128]{0:T(128)S(1)}, f32[128,768]{1,0:T(8,128)}) fusion(f32[128]{0:T(128)S(1)} %rsqrt.20, f32[128]{0:T(128)S(1)} %div.29, f32[4,32,768]{2,1,0:T(8,128)S(1)} %get-tuple-element.54, f32[768]{0:T(1024)S(1)} %copy-done.5, bf16[768,1536]{1,0:T(8,128)(2,1)} %param.15, bf16[1536,768]{1,0:T(8,128)(2,1)} %param.16, ...), kind=kOutput, calls=%fused_computation.343 | convolution fusion | flops 607420160 | bytes 7091200 | tf_op jit(solution)/shard_map/dot_general | solution.py:149
  88.4 1.8 %multiply_convert_fusion = bf16[128,768]{1,0:T(8,128)(2,1)} fusion(f32[128,768]{1,0:T(8,128)} %get-tuple-element.63, f32[4,32,768]{2,1,0:T(8,128)S(1)} %get-tuple-element.54, f32[128]{0:T(128)S(1)} %get-tuple-element.64, f32[128]{0:T(128)S(1)} %get-tuple-element.65, f32[128]{0:T(128)S(1)} %rsqrt.20, f32[128]{0:T(128)S(1)} %div.29), kind=kLoop, calls=%fused_computation.189 | loop fusion | flops 688128 | bytes 985088 | tf_op jit(solution)/shard_map/convert_element_type | solution.py:152
  90.3 0.1 all-to-all-done
  90.4 0.6 copy.23
  (23 shorter events, 0.1 us)
Async XLA Ops:
  7.2 24.9 %copy-start = (bf16[3072,384]{1,0:T(8,128)(2,1)S(1)}, bf16[3072,384]{1,0:T(8,128)(2,1)}, u32[]{:S(2)}) copy-start(bf16[3072,384]{1,0:T(8,128)(2,1)} %param.19) | copy-start | bytes 7077892
  7.2 19.0 %copy-start.6 = (f32[768]{0:T(1024)S(1)}, f32[768]{0:T(1024)}, u32[]{:S(2)}) copy-start(f32[768]{0:T(1024)} %param.13) | copy-start | bytes 9220
  8.3 16.7 %collective-permute-start = (bf16[1,3,32,768]{3,2,1,0:T(8,128)(2,1)S(1)}, bf16[1,3,32,768]{3,2,1,0:T(8,128)(2,1)S(1)}, u32[]{:S(2)}, u32[]{:S(2)}) collective-permute-start(bf16[1,3,32,768]{3,2,1,0:T(8,128)(2,1)S(1)} %get-tuple-element.59), channel_id=1, source_target_pairs={{0,1},{1,2},{2,3},{4,5},{5,6},{6,7},{8,9},{9,10},{10,11},{12,13},{... | collective-permute-start | bytes 442376 | tf_op jit(solution)/shard_map/ppermute | solution.py:17
  10.8 14.3 %collective-permute-start.1 = (bf16[1,3,32,768]{3,2,1,0:T(8,128)(2,1)S(1)}, bf16[1,3,32,768]{3,2,1,0:T(8,128)(2,1)S(1)}, u32[]{:S(2)}, u32[]{:S(2)}) collective-permute-start(bf16[1,3,32,768]{3,2,1,0:T(8,128)(2,1)S(1)} %get-tuple-element.60), channel_id=1, source_target_pairs={{1,0},{2,1},{3,2},{5,4},{6,5},{7,6},{9,8},{10,9},{11,10},{13,12},{... | collective-permute-start | bytes 442376 | tf_op jit(solution)/shard_map/ppermute | solution.py:19
  12.1 19.1 %all-to-all-start.1 = ((bf16[8,16,384]{2,1,0:T(8,128)(2,1)}), bf16[8,16,384]{2,1,0:T(8,128)(2,1)S(1)}, u32[]{:S(2)}, u32[]{:S(2)}) async-start(bf16[8,16,384]{2,1,0:T(8,128)(2,1)} %bitcast.116), calls=%async_computation.1 | async-start | bytes 196608 | tf_op jit(solution)/shard_map/all_to_all | solution.py:130
  18.7 42.4 %reduce-scatter.2.cloned.1.call-start = ((), (), s32[]{:S(2)}) async-start(), calls=%async_computation.3 | async-start | bytes 983040 | tf_op jit(solution)/shard_map/reduce_scatter | solution.py:132
  26.2 4.9 %copy-start.5 = (f32[768]{0:T(1024)S(1)}, f32[768]{0:T(1024)}, u32[]{:S(2)}) copy-start(f32[768]{0:T(1024)} %param.14) | copy-start | bytes 9220
  33.8 2.3 %copy-start.2 = (bf16[1,4,32,768]{3,2,1,0:T(8,128)(2,1)S(1)}, bf16[1,4,32,768]{3,2,1,0:T(8,128)(2,1)}, u32[]{:S(2)}) copy-start(bf16[1,4,32,768]{3,2,1,0:T(8,128)(2,1)} %param.11) | copy-start | bytes 589828
  33.8 2.4 %copy-start.8 = (f32[768]{0:T(1024)S(1)}, f32[768]{0:T(1024)}, u32[]{:S(2)}) copy-start(f32[768]{0:T(1024)} %param.17) | copy-start | bytes 9220
  33.9 2.5 %copy-start.7 = (bf16[1536,768]{1,0:T(8,128)(2,1)S(1)}, bf16[1536,768]{1,0:T(8,128)(2,1)}, u32[]{:S(2)}) copy-start(bf16[1536,768]{1,0:T(8,128)(2,1)} %param.16) | copy-start | bytes 7077892
  36.2 3.0 %copy-start.3 = (f32[128,1536]{1,0:T(8,128)}, f32[128,1536]{1,0:T(8,128)S(1)}, u32[]{:S(2)}) copy-start(f32[128,1536]{1,0:T(8,128)S(1)} %fusion.215) | copy-start | bytes 2359300
  39.2 26.1 %copy-start.4 = (f32[768]{0:T(1024)S(1)}, f32[768]{0:T(1024)}, u32[]{:S(2)}) copy-start(f32[768]{0:T(1024)} %param.18) | copy-start | bytes 9220
  67.3 15.9 %copy-start.1 = (f32[128,768]{1,0:T(8,128)S(1)}, f32[128,768]{1,0:T(8,128)}, u32[]{:S(2)}) copy-start(f32[128,768]{1,0:T(8,128)} %reshape_reshape.7) | copy-start | bytes 1179652
  77.7 12.7 %all-to-all-start = ((bf16[8,16,384]{2,1,0:T(8,128)(2,1)}), bf16[8,16,384]{2,1,0:T(8,128)(2,1)S(1)}, u32[]{:S(2)}, u32[]{:S(2)}) async-start(bf16[8,16,384]{2,1,0:T(8,128)(2,1)} %bitcast.15), calls=%async_computation | async-start | bytes 196608 | tf_op jit(solution)/shard_map/all_to_all | solution.py:129
Sparse Core Ops, SparseCore 0:
  34.0 27.0 reduce-scatter.1
where the time goes:
time: 98.7 us; the launch traced here: 97.8 us
  waiting for transfers between devices  20.9 us (21%)
  starting transfers between devices  15.9 us (16%)
  between operations  14.3 us (14%)
  local copies, waits for them, and re-layouts  13.1 us (13%)
  other arithmetic  12.9 us (13%)
  matrix products  12.6 us (13%)
  blocking collectives  8.14 us (8%)
    reduce_scatter x1, waiting for transfers between devices, on_device(): lax.psum_scatter(lax.dot_general(grad_tokens, w_down, (((1,), (1,)), ((),...  20.8 us
    all_gather x1, blocking collectives, on_device(): lax.all_gather(patches, 'space', axis=0, tiled=True)  8.14 us
    all_to_all x1, starting transfers between devices, on_device(): lax.all_to_all(grad_packed[0], 'dp', split_axis=0, concat_axis=0, tiled=T...  6.66 us
    all_to_all x1, starting transfers between devices, on_device(): lax.all_to_all(send_buffer, 'dp', split_axis=0, concat_axis=0, tiled=True)  5.53 us
    dot_general x1, matrix products, on_device(): lax.dot_general(grad_pre, w_expand, (((1,), (1,)), ((), ())), preferred_e...  5.18 us
    reduce_sum x1, other arithmetic, layer_norm(): center = values - jnp.mean(values, axis=-1, keepdims=True)  4.48 us
    slice x3, local copies, waits for them, and re-layouts, depthwise(): kernel[offset_y, offset_x]  3.88 us
    dot_general x1, matrix products, on_device(): jnp.dot(hidden, w_reduce, preferred_element_type=jnp.float32)  2.81 us
  transfers between devices with their start and end apart: 5, of which 2 were waited for; matrix products, arithmetic and copies ran while one was open for 26% of the time, Pallas kernels for 0%

commit v1 on v0

v1 whole, which is shorter than its diff:
```python
import jax
import jax.numpy as jnp
from jax import lax
from jax.experimental import pallas as pl
from jax.experimental.pallas import tpu as pltpu
from jax.sharding import PartitionSpec as P

KS = 7
HALF = KS // 2
LANES = 128
LEFT = 8
F32 = jnp.float32
BF16 = jnp.bfloat16
VMEM = pl.BlockSpec(memory_space=pltpu.VMEM)
SMEM = pl.BlockSpec(memory_space=pltpu.SMEM)
ANY = pl.BlockSpec(memory_space=pl.ANY)


def call(body, ins, specs, outs, scratch, limit_mib, flops, moved, name):
    return pl.pallas_call(
        body,
        in_specs=specs,
        out_shape=tuple(jax.ShapeDtypeStruct(s, d) for s, d in outs),
        out_specs=tuple(VMEM for _ in outs),
        scratch_shapes=scratch,
        compiler_params=pltpu.CompilerParams(vmem_limit_bytes=limit_mib << 20),
        cost_estimate=pl.CostEstimate(
            flops=int(flops), bytes_accessed=int(moved), transcendentals=0
        ),
        name=name,
    )(*ins)


def nt(a, b):
    return lax.dot_general(a, b, (((1,), (1,)), ((), ())), preferred_element_type=F32)


def nn(a, b):
    return jnp.dot(a, b, preferred_element_type=F32)


def normalize(values):
    center = values - jnp.mean(values, axis=-1, keepdims=True)
    inv_std = lax.rsqrt(jnp.mean(center * center, axis=-1, keepdims=True) + 1e-06)
    return center * inv_std, inv_std


def norm_back(grad, normed, inv_std, gain):
    scaled = grad * gain
    return inv_std * (
        scaled
        - jnp.mean(scaled, axis=-1, keepdims=True)
        - normed * jnp.mean(scaled * normed, axis=-1, keepdims=True)
    )


def forward_body(
    rows, width, channels, hidden, block,
    place, x_ref, near_ref, far_ref, kernel_ref, bias_ref, gain_ref, w1_ref, w2_ref,
    scale_ref, down_gain_ref,
    patch_ref, slope_ref, n1_ref, inv1_ref, n2_ref, inv2_ref,
    padded, mixed, first, acc, grid,
):
    odd = place[0] % 2 == 1
    chunks = channels // LANES
    tall = rows + 2 * HALF
    padded[:, :, 0:LEFT, :] = jnp.zeros((chunks, tall, LEFT, LANES), F32)
    padded[:, :, LEFT + width :, :] = jnp.zeros((chunks, tall, LEFT, LANES), F32)

    def fill(c, _):
        at = pl.ds(pl.multiple_of(c * LANES, LANES), LANES)
        cols = pl.ds(LEFT, width)
        near, far = near_ref[0, :, :, at].astype(F32), far_ref[0, :, :, at].astype(F32)
        above, below = jnp.where(odd, near, far), jnp.where(odd, far, near)
        padded[c, 0:HALF, cols, :] = above[rows - HALF :]
        padded[c, HALF : HALF + rows, cols, :] = x_ref[0, :, :, at].astype(F32)
        padded[c, HALF + rows :, cols, :] = below[:HALF]
        total = [jnp.zeros((width, LANES), F32) for _ in range(rows)]
        for dx in range(KS):
            taps = [kernel_ref[dy, dx : dx + 1, at] for dy in range(KS)]
            for r in range(tall):
                line = padded[c, r, pl.ds(LEFT - HALF + dx, width), :]
                for out in range(rows):
                    if 0 <= r - out < KS:
                        total[out] = total[out] + line * taps[r - out]
        for out in range(rows):
            mixed[pl.ds(out * width, width), at] = total[out] + bias_ref[0:1, at]
        return 0

    lax.fori_loop(0, chunks, fill, 0)
    count = rows * width
    step = width
    for r in range(0, count, step):
        n1, inv1 = normalize(mixed[r : r + step, :])
        n1_ref[r : r + step, :] = n1
        inv1_ref[r : r + step, :] = jnp.broadcast_to(inv1, (step, LANES))
        first[r : r + step, :] = (n1 * gain_ref[...]).astype(BF16)
    for b in range(0, hidden, block):
        pre = nn(first[...], w1_ref[:, b : b + block])
        cumulative = 0.5 * (1.0 + lax.erf(pre * 0.7071067811865476))
        density = jnp.exp(-0.5 * pre * pre) * 0.3989422804014327
        slope_ref[:, b : b + block] = cumulative + pre * density
        term = nn((pre * cumulative).astype(BF16), w2_ref[b : b + block, :])
        if b == 0:
            acc[...] = term
        else:
            acc[...] += term
    for r in range(rows):
        at = pl.ds(r * width, width)
        v = x_ref[0, r].astype(F32) + scale_ref[...] * acc[at, :]
        n2, inv2 = normalize(v)
        n2_ref[at, :] = n2
        inv2_ref[at, :] = jnp.broadcast_to(inv2, (step, LANES))
        second = n2 * down_gain_ref[...]
        for c in range(chunks):
            grid[c, at, :] = second[:, c * LANES : (c + 1) * LANES]
    half = width // 2
    for r in range(rows // 2):
        for a in range(2):
            for b in range(2):
                piece = jnp.concatenate(
                    [
                        grid[c, pl.ds((2 * r + a) * width + b, half, stride=2), :]
                        for c in range(chunks)
                    ],
                    axis=1,
                )
                patch_ref[r * half : (r + 1) * half, (2 * a + b) * channels : (2 * a + b + 1) * channels] = (
                    piece.astype(BF16)
                )


def pull_body(
    spaces, owners, capacity,
    place, table_ref, returned_ref, w_ref, after_ref,
    keep_ref, send_ref, pick_ref,
    wanted, both,
):
    core = place[0] % 2
    targets = table_ref[0]
    count = targets.shape[0]
    wide = max(owners, LANES)
    hot = targets == lax.broadcasted_iota(jnp.int32, (count, wide), 1)
    hot_b = jnp.where(hot, 1.0, 0.0).astype(BF16)
    lower = lax.broadcasted_iota(jnp.int32, (count, count), 0) > lax.broadcasted_iota(
        jnp.int32, (count, count), 1
    )
    earlier = nn(jnp.where(lower, 1.0, 0.0).astype(BF16), hot_b)
    rank = jnp.sum(jnp.where(hot, earlier, 0.0), axis=1, keepdims=True).astype(jnp.int32)
    slots = returned_ref.shape[0]
    pick = jnp.where(
        targets * capacity + rank == lax.broadcasted_iota(jnp.int32, (count, slots), 1), 1.0, 0.0
    ).astype(BF16)
    pick_ref[...] = pick
    band = count // spaces
    wanted[...] = nn(pick, returned_ref[...]).astype(BF16).reshape(wanted.shape)
    chips = spaces // 2
    for i in range(chips):
        both[i * band : (i + 1) * band, :] = wanted[2 * i + core]
        both[(chips + i) * band : (chips + i + 1) * band, :] = wanted[2 * i + 1 - core]
    depth = w_ref.shape[0]
    step = 512
    for d in range(0, depth, step):
        part = nt(both[...], w_ref[d : d + step, :]).astype(BF16)
        for i in range(chips):
            keep_ref[i, :, d : d + step] = part[i * band : (i + 1) * band]
            send_ref[i, :, d : d + step] = part[(chips + i) * band : (chips + i + 1) * band]


def add_body(chips, place, keep_ref, near_ref, *outs):
    chip = place[0] // 2
    for j in range(1, chips):
        at = lax.rem(chip + j, chips)
        outs[j - 1][...] = (keep_ref[at].astype(F32) + near_ref[at].astype(F32)).astype(BF16)


def backward_body(
    rows, width, channels, hidden, block, chips,
    place, keep_ref, near_ref, *rest,
):
    far = rest[: chips - 1]
    (
        slope_ref, n1_ref, inv1_ref, n2_ref, inv2_ref, gain_ref, w1_ref, w2_ref, scale_ref,
        down_gain_ref, after_ref, out_ref, grid, scaled, acc,
    ) = rest[chips - 1 :]
    chip = place[0] // 2
    half = width // 2
    chunks = channels // LANES
    for r in range(rows // 2):
        for a in range(2):
            for b in range(2):
                at = (pl.ds(r * half, half), pl.ds((2 * a + b) * channels, channels))
                value = keep_ref[(chip,) + at].astype(F32) + near_ref[(chip,) + at].astype(F32)
                for piece in far:
                    value = value + piece[at].astype(F32)
                for c in range(chunks):
                    grid[c, pl.ds((2 * r + a) * width + b, half, stride=2), :] = (
                        value[:, c * LANES : (c + 1) * LANES]
                    )
    for r in range(rows):
        at = pl.ds(r * width, width)
        grad = jnp.concatenate([grid[c, at, :] for c in range(chunks)], axis=1)
        back = norm_back(grad, n2_ref[at, :], inv2_ref[at, 0:1], down_gain_ref[...])
        scaled[at, :] = (back * scale_ref[...]).astype(BF16)
    for b in range(0, hidden, block):
        grad_pre = (nt(scaled[...], w2_ref[b : b + block, :]) * slope_ref[:, b : b + block]).astype(BF16)
        term = nt(grad_pre, w1_ref[:, b : b + block])
        if b == 0:
            acc[...] = term
        else:
            acc[...] += term
    for r in range(rows):
        at = pl.ds(r * width, width)
        back = norm_back(acc[at, :], n1_ref[at, :], inv1_ref[at, 0:1], gain_ref[...])
        out_ref[0, r] = back.astype(BF16)


def push_body(chips, place, *rest):
    pieces = rest[: 2 * chips]
    pick_ref, w_ref, out_ref, patches, tokens = rest[2 * chips :]
    chip, core = place[0] // 2, place[0] % 2
    band = pieces[0].shape[0]
    for i, piece in enumerate(pieces):
        patches[i * band : (i + 1) * band, :] = piece[...]
    result = nn(patches[...], w_ref[...]).astype(BF16)
    for i in range(2 * chips):
        source = lax.rem(chip + chips - i // 2, chips)
        owner = 2 * source + (core if i % 2 == 0 else 1 - core)
        tokens[owner] = result[i * band : (i + 1) * band]
    flat = tokens[...].reshape(2 * chips * band, tokens.shape[2])
    out_ref[...] = lax.dot_general(
        pick_ref[...], flat, (((0,), (0,)), ((), ())), preferred_element_type=F32
    ).astype(BF16)


def on_device(
    section_three, dw_kernel, dw_bias, mix_gain, w_expand, w_reduce, layer_scale, down_gain,
    w_down, owner_table, grad_packed,
):
    owners = lax.axis_size("dp")
    spaces = lax.axis_size("space")
    chips = spaces // 2
    slots = grad_packed.shape[1]
    capacity = slots // owners
    _, rows, width, channels = section_three.shape
    hidden = w_expand.shape[1]
    count = rows * width
    band = count // 4
    tokens = owner_table.shape[1]
    deep, narrow = w_down.shape
    place = lax.axis_index("space").astype(jnp.int32).reshape(1)
    row = lambda v: v.reshape(1, -1)

    swap = [(i, i ^ 1) for i in range(spaces)]
    joints = [(i, i + 1) for i in range(1, spaces - 1, 2)]
    joints = joints + [(b, a) for a, b in joints]

    def onward(j):
        return [(i, (i + 2 * j) % spaces) for i in range(spaces)]

    near = lax.ppermute(section_three, "space", swap)
    far = lax.ppermute(section_three, "space", joints)
    returned = lax.all_to_all(grad_packed[0], "dp", split_axis=0, concat_axis=0, tiled=True)

    block = 256
    patches, slope, n1, inv1, n2, inv2 = call(
        lambda *refs: forward_body(rows, width, channels, hidden, block, *refs),
        (place, section_three, near, far, dw_kernel, row(dw_bias), row(mix_gain), w_expand, w_reduce,
         row(layer_scale), row(down_gain)),
        [SMEM] + [VMEM] * 10,
        [((band, 4 * channels), BF16), ((count, hidden), F32), ((count, channels), F32),
         ((count, LANES), F32), ((count, channels), F32), ((count, LANES), F32)],
        [pltpu.VMEM((channels // LANES, rows + 2 * HALF, width + 2 * LEFT, LANES), F32),
         pltpu.VMEM((count, channels), F32), pltpu.VMEM((count, channels), BF16),
         pltpu.VMEM((count, channels), F32), pltpu.VMEM((channels // LANES, count, LANES), F32)],
        24, 4 * count * channels * hidden, 9e6, "forward",
    )
    held = [patches] + [lax.ppermute(patches, "space", onward(j)) for j in range(1, chips)]
    keep, send, pick = call(
        lambda *refs: pull_body(spaces, owners, capacity, *refs),
        (place, owner_table, returned, w_down, inv2),
        [SMEM, VMEM, VMEM, VMEM, ANY],
        [((chips, band, deep), BF16), ((chips, band, deep), BF16), ((tokens, slots), BF16)],
        [pltpu.VMEM((spaces, band, narrow), BF16), pltpu.VMEM((tokens, narrow), BF16)],
        16, 2 * tokens * deep * narrow, 4e6, "pull",
    )
    sent = lax.ppermute(send, "space", swap)
    sums = call(
        lambda *refs: add_body(chips, *refs),
        (place, keep, sent), [SMEM, VMEM, VMEM],
        [((band, deep), BF16)] * (chips - 1), [], 8, 2e6, 1e6, "add",
    )
    across = [lax.ppermute(sums[j - 1], "space", onward(j)) for j in range(1, chips)]
    pieces = []
    for piece in held:
        pieces += [piece, lax.ppermute(piece, "space", swap)]
    (buffer,) = call(
        lambda *refs: push_body(chips, *refs),
        (place, *pieces, pick, w_down),
        [SMEM] + [VMEM] * (len(pieces) + 2),
        [((slots, narrow), BF16)],
        [pltpu.VMEM((tokens, deep), BF16), pltpu.VMEM((spaces, band, narrow), BF16)],
        16, 2 * tokens * deep * narrow, 4e6, "push",
    )
    arrived = lax.all_to_all(buffer, "dp", split_axis=0, concat_axis=0, tiled=True)
    (grad_mixed,) = call(
        lambda *refs: backward_body(rows, width, channels, hidden, block, chips, *refs),
        (place, keep, sent, *across, slope, n1, inv1, n2, inv2, row(mix_gain), w_expand, w_reduce,
         row(layer_scale), row(down_gain), buffer),
        [SMEM] + [VMEM] * (11 + chips) + [ANY],
        [(section_three.shape, BF16)],
        [pltpu.VMEM((channels // LANES, count, LANES), F32), pltpu.VMEM((count, channels), BF16),
         pltpu.VMEM((count, channels), F32)],
        24, 4 * count * channels * hidden, 9e6, "backward",
    )
    return arrived[None], grad_mixed


def solution(mesh):
    in_specs = (
        P("dp", "space", None, None), P(), P(), P(), P(), P(), P(), P(), P(None, "space"),
        P("dp", None, None), P("dp", None, "space"),
    )
    out_specs = (P("dp", None, "space"), P("dp", "space", None, None))
    return jax.shard_map(
        on_device, mesh=mesh, in_specs=in_specs, out_specs=out_specs, check_vma=False
    )
```

time: 98.7 us -> 59.4 us (0.60)
  waiting for transfers between devices: 20.9 us -> 6.06 us
  between operations: 14.3 us -> 0.76 us
  other arithmetic: 12.9 us -> 0 us
  matrix products: 12.6 us -> 0 us
  Pallas kernels: 0 us -> 8.6 us
  blocking collectives: 8.14 us -> 12.8 us
  local copies, waits for them, and re-layouts: 13.1 us -> 17.5 us
  starting transfers between devices: 15.9 us -> 13 us
    reduce_scatter x1 -> x0, waiting for transfers between devices: 20.8 us -> none  [on_device(): lax.psum_scatter(lax.dot_general(grad_tokens, w_down, (((1,), (1,)), ((),...]
    unnamed x19 -> x44, local copies, waits for them, and re-layouts: 0.83 us -> 14.8 us
    all_to_all x0 -> x1, blocking collectives: none -> 12.8 us  [on_device(): lax.all_to_all(buffer, 'dp', split_axis=0, concat_axis=0, tiled=True)]
    dot_general x5 -> x0, matrix products: 12.6 us -> none  [the longest x1 5.18 us: on_device(): lax.dot_general(grad_pre, w_expand, (((1,), (1,)), ((), ())), preferred_e...]
    pallas_call x0 -> x5, Pallas kernels: none -> 8.6 us  [call(): pl.pallas_call(body, in_specs=specs, out_shape=tuple((jax.ShapeDtypeStruc...]
    reduce_sum x6 -> x0, other arithmetic: 8.23 us -> none  [the longest x1 4.48 us: layer_norm(): center = values - jnp.mean(values, axis=-1, keepdims=True)]
    all_gather x1 -> x0, blocking collectives: 8.14 us -> none  [on_device(): lax.all_gather(patches, 'space', axis=0, tiled=True)]
    ppermute x2 -> x7, waiting for transfers between devices: 0.01 us -> 6.06 us  [the longest x1 5.91 us: on_device(): lax.ppermute(patches, 'space', onward(j))]
  transfers between devices with their start and end apart: 5 -> 8, of which waited for: 2 -> 2; matrix products, arithmetic and copies ran while one was open for 26% -> 7% of each run, Pallas kernels for 0% -> 6%
where the time goes in v1:
time: 59.4 us; the launch traced here: 58.7 us
  local copies, waits for them, and re-layouts  17.5 us (29%)
  starting transfers between devices  13 us (22%)
  blocking collectives  12.8 us (22%)
  Pallas kernels  8.6 us (14%)
  waiting for transfers between devices  6.06 us (10%)
  between operations  0.76 us (1%)
    unnamed x44, local copies, waits for them, and re-layouts  14.8 us
    all_to_all x1, blocking collectives, on_device(): lax.all_to_all(buffer, 'dp', split_axis=0, concat_axis=0, tiled=True)  12.8 us
    pallas_call x5, Pallas kernels, call(): pl.pallas_call(body, in_specs=specs, out_shape=tuple((jax.ShapeDtypeStruc...  8.6 us
    all_to_all x1, starting transfers between devices, on_device(): lax.all_to_all(grad_packed[0], 'dp', split_axis=0, concat_axis=0, tiled=T...  6.86 us
    ppermute x1, waiting for transfers between devices, on_device(): lax.ppermute(patches, 'space', onward(j))  5.91 us
    reshape x4, local copies, waits for them, and re-layouts, on_device(): row = lambda v: v.reshape(1, -1)  2.76 us
    ppermute x1, starting transfers between devices, on_device(): sent = lax.ppermute(send, 'space', swap)  2.65 us
    ppermute x1, starting transfers between devices, on_device(): lax.ppermute(sums[j - 1], 'space', onward(j))  1.24 us
  transfers between devices with their start and end apart: 8, of which 2 were waited for; matrix products, arithmetic and copies ran while one was open for 7% of the time, Pallas kernels for 6%

profile of v1, /device:TPU:0, one launch (start us, length us, event | category | flops | bytes accessed | tf_op | source)
XLA Modules:
  0.0 58.7 jit_solution(3717329285219742082)
XLA Ops:
  0.6 0.6 collective-permute-start
  1.2 0.7 %collective-permute-start.1 = (bf16[1,4,32,768]{3,2,1,0:T(8,128)(2,1)}, bf16[1,4,32,768]{3,2,1,0:T(8,128)(2,1)S(1)}, u32[]{:S(2)}, u32[]{:S(2)}) collective-permute-start(bf16[1,4,32,768]{3,2,1,0:T(8,128)(2,1)} %refs_1_.2), channel_id=1, source_target_pairs={{1,2},{2,1},{5,6},{6,5},{9,10},{10,9},{13,14},{14,13},{17,18},{18,... | collective-permute-start | bytes 589832 | tf_op jit(solution)/shard_map/ppermute | solution.py:262
  1.9 6.9 %all-to-all-start = ((bf16[8,16,384]{2,1,0:T(8,128)(2,1)}), bf16[8,16,384]{2,1,0:T(8,128)(2,1)}, u32[]{:S(2)}, u32[]{:S(2)}) async-start(bf16[8,16,384]{2,1,0:T(8,128)(2,1)} %bitcast.7), calls=%async_computation | async-start | bytes 196608 | tf_op jit(solution)/shard_map/all_to_all | solution.py:263
  8.7 0.7 %reshape.30.refs_6_.refs_9_ = f32[1,768]{1,0:T(1,128)S(1)} reshape(f32[768]{0:T(1024)} %param.14) | data formatting | bytes 6144 | tf_op jit(solution)/shard_map/reshape | solution.py:252
  9.4 0.7 %reshape.31.refs_9_.refs_12_ = f32[1,768]{1,0:T(1,128)S(1)} reshape(f32[768]{0:T(1024)} %param.17) | data formatting | bytes 6144 | tf_op jit(solution)/shard_map/reshape | solution.py:252
  10.1 0.7 %reshape.32.refs_10_.refs_13_ = f32[1,768]{1,0:T(1,128)S(1)} reshape(f32[768]{0:T(1024)} %param.18) | data formatting | bytes 6144 | tf_op jit(solution)/shard_map/reshape | solution.py:252
  10.8 0.7 %reshape.29.refs_5_ = f32[1,768]{1,0:T(1,128)S(1)} reshape(f32[768]{0:T(1024)} %param.13) | data formatting | bytes 6144 | tf_op jit(solution)/shard_map/reshape | solution.py:252
  11.5 1.4 %copy.13.refs_1_ = s32[1,128,1]{2,1,0:T(8,128)} copy(s32[1,128,1]{1,2,0:T(1,128)} %param.20) | data formatting | bytes 1024 | tf_op args[9]
  12.9 0.0 collective-permute-done.refs_2_
  12.9 0.7 %copy-done.12 = bf16[1,4,32,768]{3,2,1,0:T(8,128)(2,1)} copy-done((bf16[1,4,32,768]{3,2,1,0:T(8,128)(2,1)}, bf16[1,4,32,768]{3,2,1,0:T(8,128)(2,1)S(1)}, u32[]{:S(2)}) %copy-start.12) | copy-done | bytes 196632
  13.5 0.0 collective-permute-done.1.refs_3_
  13.5 0.7 %copy-done.14 = bf16[1,4,32,768]{3,2,1,0:T(8,128)(2,1)} copy-done((bf16[1,4,32,768]{3,2,1,0:T(8,128)(2,1)}, bf16[1,4,32,768]{3,2,1,0:T(8,128)(2,1)S(1)}, u32[]{:S(2)}) %copy-start.14) | copy-done | bytes 196632
  14.2 1.7 %copy-done = bf16[768,1536]{1,0:T(8,128)(2,1)S(1)} copy-done((bf16[768,1536]{1,0:T(8,128)(2,1)S(1)}, bf16[768,1536]{1,0:T(8,128)(2,1)}, u32[]{:S(2)}) %copy-start) | copy-done | bytes 2359320
  15.9 1.7 %copy-done.2 = bf16[1536,768]{1,0:T(8,128)(2,1)S(1)} copy-done((bf16[1536,768]{1,0:T(8,128)(2,1)S(1)}, bf16[1536,768]{1,0:T(8,128)(2,1)}, u32[]{:S(2)}) %copy-start.2) | copy-done | bytes 2359320
  17.6 0.9 %copy-done.11 = bf16[1,4,32,768]{3,2,1,0:T(8,128)(2,1)S(1)} copy-done((bf16[1,4,32,768]{3,2,1,0:T(8,128)(2,1)S(1)}, bf16[1,4,32,768]{3,2,1,0:T(8,128)(2,1)}, u32[]{:S(2)}) %copy-start.11) | copy-done | bytes 196632
  18.5 0.9 %copy-done.13 = bf16[1,4,32,768]{3,2,1,0:T(8,128)(2,1)S(1)} copy-done((bf16[1,4,32,768]{3,2,1,0:T(8,128)(2,1)S(1)}, bf16[1,4,32,768]{3,2,1,0:T(8,128)(2,1)}, u32[]{:S(2)}) %copy-start.13) | copy-done | bytes 196632
  19.4 0.9 %copy-done.15 = bf16[1,4,32,768]{3,2,1,0:T(8,128)(2,1)S(1)} copy-done((bf16[1,4,32,768]{3,2,1,0:T(8,128)(2,1)S(1)}, bf16[1,4,32,768]{3,2,1,0:T(8,128)(2,1)}, u32[]{:S(2)}) %copy-start.15) | copy-done | bytes 196632
  20.3 0.9 %copy-done.18 = f32[7,7,768]{2,1,0:T(8,128)S(1)} copy-done((f32[7,7,768]{2,1,0:T(8,128)S(1)}, f32[7,7,768]{2,1,0:T(8,128)}, u32[]{:S(2)}) %copy-start.18) | copy-done | bytes 150552
  21.3 2.8 %forward.1 = (bf16[32,3072]{1,0:T(8,128)(2,1)S(1)}, f32[128,1536]{1,0:T(8,128)S(1)}, f32[128,768]{1,0:T(8,128)S(1)}, f32[128,128]{1,0:T(8,128)S(1)}, f32[128,768]{1,0:T(8,128)S(1)}, /*index=5*/f32[128,128]{1,0:T(8,128)S(1)}) custom-call(s32[1]{0:T(128)} %bitcast.refs_0_, bf16[1,4,32,768]{3,2,1,0:T(8,128)(2,1)S(1)} %copy-done.11, ...), custom_call_target="tpu_custom_call" | custom-call | flops 603979776 | bytes 9000000 | tf_op jit(solution)/shard_map/forward/pallas_call | solution.py:20
  24.1 0.0 copy-start.5
  24.1 0.7 %copy-done.5 = f32[128,768]{1,0:T(8,128)} copy-done((f32[128,768]{1,0:T(8,128)}, f32[128,768]{1,0:T(8,128)S(1)}, u32[]{:S(2)}) %copy-start.5) | copy-done | bytes 393240
  24.8 0.6 %copy-done.7 = f32[128,128]{1,0:T(8,128)} copy-done((f32[128,128]{1,0:T(8,128)}, f32[128,128]{1,0:T(8,128)S(1)}, u32[]{:S(2)}) %copy-start.7) | copy-done | bytes 65560
  25.4 0.7 %copy-done.16 = bf16[32,3072]{1,0:T(8,128)(2,1)} copy-done((bf16[32,3072]{1,0:T(8,128)(2,1)}, bf16[32,3072]{1,0:T(8,128)(2,1)S(1)}, u32[]{:S(2)}) %copy-start.16) | copy-done | bytes 196632
  26.1 0.6 %copy-done.19 = f32[128,128]{1,0:T(8,128)} copy-done((f32[128,128]{1,0:T(8,128)}, f32[128,128]{1,0:T(8,128)S(1)}, u32[]{:S(2)}) %copy-start.19) | copy-done | bytes 65560
  26.7 0.0 all-to-all-done
  26.7 0.0 copy-done.4
  26.8 0.8 %copy-done.8 = f32[128,128]{1,0:T(8,128)S(1)} copy-done((f32[128,128]{1,0:T(8,128)S(1)}, f32[128,128]{1,0:T(8,128)}, u32[]{:S(2)}) %copy-start.8) | copy-done | bytes 65560
  27.6 0.8 %copy-done.10 = s32[1,128,1]{2,1,0:T(8,128)S(1)} copy-done((s32[1,128,1]{2,1,0:T(8,128)S(1)}, s32[1,128,1]{2,1,0:T(8,128)}, u32[]{:S(2)}) %copy-start.10) | copy-done | bytes 536
  28.4 2.4 %pull.1 = (bf16[2,32,3072]{2,1,0:T(8,128)(2,1)S(1)}, bf16[2,32,3072]{2,1,0:T(8,128)(2,1)S(1)}, bf16[128,128]{1,0:T(8,128)(2,1)S(1)}) custom-call(s32[1]{0:T(128)} %bitcast.refs_0_, s32[1,128,1]{2,1,0:T(8,128)S(1)} %copy-done.10, bf16[128,384]{1,0:T(8,128)(2,1)} %bitcast.2.refs_2_, bf16[3072,384]{1,0:T(8,128)(2,1)S(1)} %copy-done.4, f32[128,128]{1,0:T(8,128)S(1)} %copy-done.8), custom_call_target="tpu_custom_call" | custom-call | flops 301989888 | bytes 4000000 | tf_op jit(solution)/shard_map/pull/pallas_call | solution.py:20
  30.8 0.0 copy-start.1
  30.8 0.0 copy-start.6
  30.8 2.7 %collective-permute-start.5 = (bf16[2,32,3072]{2,1,0:T(8,128)(2,1)S(1)}, bf16[2,32,3072]{2,1,0:T(8,128)(2,1)S(1)}, u32[]{:S(2)}, u32[]{:S(2)}) collective-permute-start(bf16[2,32,3072]{2,1,0:T(8,128)(2,1)S(1)} %get-tuple-element.15), channel_id=1, source_target_pairs={{0,1},{1,0},{2,3},{3,2},{4,5},{5,4},{6,7},{7,6},{8,9},{9,8},{10,11... | collective-permute-start | bytes 1179656 | tf_op jit(solution)/shard_map/ppermute | solution.py:287
  33.5 0.8 %collective-permute-start.3 = (bf16[32,3072]{1,0:T(8,128)(2,1)S(1)}, bf16[32,3072]{1,0:T(8,128)(2,1)S(1)}, u32[]{:S(2)}, u32[]{:S(2)}) collective-permute-start(bf16[32,3072]{1,0:T(8,128)(2,1)S(1)} %copy-done.17), channel_id=1, source_target_pairs={{0,2},{1,3},{2,0},{3,1},{4,6},{5,7},{6,4},{7,5},{8,10},{9,11},{10,... | collective-permute-start | bytes 589832 | tf_op jit(solution)/shard_map/ppermute | solution.py:278
  34.3 0.1 collective-permute-start.2
  34.5 5.9 %collective-permute-done.3.refs_3_ = bf16[32,3072]{1,0:T(8,128)(2,1)S(1)} collective-permute-done((bf16[32,3072]{1,0:T(8,128)(2,1)S(1)}, bf16[32,3072]{1,0:T(8,128)(2,1)S(1)}, u32[]{:S(2)}, u32[]{:S(2)}) %collective-permute-start.3) | collective-permute-done | bytes 196640 | tf_op jit(solution)/shard_map/ppermute | solution.py:278
  40.4 0.0 collective-permute-start.4
  40.4 0.0 collective-permute-done.5.refs_2_
  40.4 1.2 %collective-permute-start.6 = (bf16[32,3072]{1,0:T(8,128)(2,1)S(1)}, bf16[32,3072]{1,0:T(8,128)(2,1)S(1)}, u32[]{:S(2)}, u32[]{:S(2)}) collective-permute-start(bf16[32,3072]{1,0:T(8,128)(2,1)S(1)} %add.1), channel_id=1, source_target_pairs={{0,2},{1,3},{2,0},{3,1},{4,6},{5,7},{6,4},{7,5},{8,10},{9,11},{10,... | collective-permute-start | bytes 589832 | tf_op jit(solution)/shard_map/ppermute | solution.py:293
  41.7 0.0 collective-permute-done.2.refs_2_
  41.7 0.1 collective-permute-done.4.refs_4_
  41.8 0.7 %push.1.refs_14_ = bf16[128,384]{1,0:T(8,128)(2,1)S(1)} custom-call(s32[1]{0:T(128)} %bitcast.refs_0_, bf16[32,3072]{1,0:T(8,128)(2,1)S(1)} %copy-done.17, bf16[32,3072]{1,0:T(8,128)(2,1)S(1)} %collective-permute-done.2.refs_2_, bf16[32,3072]{1,0:T(8,128)(2,1)S(1)} %collective-permute-done.3.refs_3_, bf16[32,3072]{1,0:T(8,128)(2,1)S(1)} %collective-permute-done.4.refs_4_, ...), custom_call_target="tpu_custom_call" | custom-call | flops 301989888 | bytes 4000000 | tf_op jit(solution)/shard_map/push/pallas_call | solution.py:20
  42.6 12.8 %all_to_all.20 = bf16[8,16,384]{2,1,0:T(8,128)(2,1)S(1)} all-to-all(bf16[8,16,384]{2,1,0:T(8,128)(2,1)S(1)} %bitcast.5), channel_id=1, replica_groups=mesh['dp'=8,'space'=4] {'dp'}, dimensions={0} | all-to-all | bytes 196608 | tf_op jit(solution)/shard_map/all_to_all | solution.py:305
  55.4 0.0 collective-permute-done.6.refs_3_
  55.4 0.0 copy-done.6
  55.4 0.0 copy-done.9
  55.4 0.0 copy-done.20
  55.4 2.6 %backward.1 = bf16[1,4,32,768]{3,2,1,0:T(8,128)(2,1)} custom-call(s32[1]{0:T(128)} %bitcast.refs_0_, bf16[2,32,3072]{2,1,0:T(8,128)(2,1)S(1)} %get-tuple-element.14.refs_1_, bf16[2,32,3072]{2,1,0:T(8,128)(2,1)S(1)} %collective-permute-done.5.refs_2_, bf16[32,3072]{1,0:T(8,128)(2,1)S(1)} %collective-permute-done.6.refs_3_, ...), custom_call_target="tpu_custom_call" | custom-call | flops 603979776 | bytes 9000000 | tf_op jit(solution)/shard_map/backward/pallas_call | solution.py:20
  58.1 0.6 %copy.15 = bf16[1,128,384]{2,1,0:T(8,128)(2,1)} copy(bf16[1,128,384]{2,1,0:T(8,128)(2,1)S(1)} %bitcast.6) | data formatting | bytes 196608
  (22 shorter events, 0.1 us)
Async XLA Ops:
  0.6 12.2 %collective-permute-start = (bf16[1,4,32,768]{3,2,1,0:T(8,128)(2,1)}, bf16[1,4,32,768]{3,2,1,0:T(8,128)(2,1)S(1)}, u32[]{:S(2)}, u32[]{:S(2)}) collective-permute-start(bf16[1,4,32,768]{3,2,1,0:T(8,128)(2,1)} %refs_1_.2), channel_id=1, source_target_pairs={{0,1},{1,0},{2,3},{3,2},{4,5},{5,4},{6,7},{7,6},{8,9},{9,8},{10,11... | collective-permute-start | bytes 589832 | tf_op jit(solution)/shard_map/ppermute | solution.py:261
  1.2 12.4 %collective-permute-start.1 = (bf16[1,4,32,768]{3,2,1,0:T(8,128)(2,1)}, bf16[1,4,32,768]{3,2,1,0:T(8,128)(2,1)S(1)}, u32[]{:S(2)}, u32[]{:S(2)}) collective-permute-start(bf16[1,4,32,768]{3,2,1,0:T(8,128)(2,1)} %refs_1_.2), channel_id=1, source_target_pairs={{1,2},{2,1},{5,6},{6,5},{9,10},{10,9},{13,14},{14,13},{17,18},{18,... | collective-permute-start | bytes 589832 | tf_op jit(solution)/shard_map/ppermute | solution.py:262
  1.9 24.9 %all-to-all-start = ((bf16[8,16,384]{2,1,0:T(8,128)(2,1)}), bf16[8,16,384]{2,1,0:T(8,128)(2,1)}, u32[]{:S(2)}, u32[]{:S(2)}) async-start(bf16[8,16,384]{2,1,0:T(8,128)(2,1)} %bitcast.7), calls=%async_computation | async-start | bytes 196608 | tf_op jit(solution)/shard_map/all_to_all | solution.py:263
  12.9 0.7 %copy-start.12 = (bf16[1,4,32,768]{3,2,1,0:T(8,128)(2,1)}, bf16[1,4,32,768]{3,2,1,0:T(8,128)(2,1)S(1)}, u32[]{:S(2)}) copy-start(bf16[1,4,32,768]{3,2,1,0:T(8,128)(2,1)S(1)} %collective-permute-done.refs_2_) | copy-start | bytes 589828
  13.5 0.7 %copy-start.14 = (bf16[1,4,32,768]{3,2,1,0:T(8,128)(2,1)}, bf16[1,4,32,768]{3,2,1,0:T(8,128)(2,1)S(1)}, u32[]{:S(2)}) copy-start(bf16[1,4,32,768]{3,2,1,0:T(8,128)(2,1)S(1)} %collective-permute-done.1.refs_3_) | copy-start | bytes 589828
  14.2 1.7 %copy-start = (bf16[768,1536]{1,0:T(8,128)(2,1)S(1)}, bf16[768,1536]{1,0:T(8,128)(2,1)}, u32[]{:S(2)}) copy-start(bf16[768,1536]{1,0:T(8,128)(2,1)} %refs_10_.1) | copy-start | bytes 7077892
  15.9 1.7 %copy-start.2 = (bf16[1536,768]{1,0:T(8,128)(2,1)S(1)}, bf16[1536,768]{1,0:T(8,128)(2,1)}, u32[]{:S(2)}) copy-start(bf16[1536,768]{1,0:T(8,128)(2,1)} %refs_11_.1) | copy-start | bytes 7077892
  17.6 0.9 %copy-start.11 = (bf16[1,4,32,768]{3,2,1,0:T(8,128)(2,1)S(1)}, bf16[1,4,32,768]{3,2,1,0:T(8,128)(2,1)}, u32[]{:S(2)}) copy-start(bf16[1,4,32,768]{3,2,1,0:T(8,128)(2,1)} %refs_1_.2) | copy-start | bytes 589828
  18.5 0.9 %copy-start.13 = (bf16[1,4,32,768]{3,2,1,0:T(8,128)(2,1)S(1)}, bf16[1,4,32,768]{3,2,1,0:T(8,128)(2,1)}, u32[]{:S(2)}) copy-start(bf16[1,4,32,768]{3,2,1,0:T(8,128)(2,1)} %copy-done.12) | copy-start | bytes 589828
  19.4 0.9 %copy-start.15 = (bf16[1,4,32,768]{3,2,1,0:T(8,128)(2,1)S(1)}, bf16[1,4,32,768]{3,2,1,0:T(8,128)(2,1)}, u32[]{:S(2)}) copy-start(bf16[1,4,32,768]{3,2,1,0:T(8,128)(2,1)} %copy-done.14) | copy-start | bytes 589828
  20.3 0.9 %copy-start.18 = (f32[7,7,768]{2,1,0:T(8,128)S(1)}, f32[7,7,768]{2,1,0:T(8,128)}, u32[]{:S(2)}) copy-start(f32[7,7,768]{2,1,0:T(8,128)} %refs_4_.1) | copy-start | bytes 451588
  21.3 5.5 %copy-start.4 = (bf16[3072,384]{1,0:T(8,128)(2,1)S(1)}, bf16[3072,384]{1,0:T(8,128)(2,1)}, u32[]{:S(2)}) copy-start(bf16[3072,384]{1,0:T(8,128)(2,1)} %refs_6_.1) | copy-start | bytes 7077892
  24.1 0.8 %copy-start.5 = (f32[128,768]{1,0:T(8,128)}, f32[128,768]{1,0:T(8,128)S(1)}, u32[]{:S(2)}) copy-start(f32[128,768]{1,0:T(8,128)S(1)} %get-tuple-element.19.refs_7_) | copy-start | bytes 1179652
  24.8 0.6 %copy-start.7 = (f32[128,128]{1,0:T(8,128)}, f32[128,128]{1,0:T(8,128)S(1)}, u32[]{:S(2)}) copy-start(f32[128,128]{1,0:T(8,128)S(1)} %get-tuple-element.12.refs_4_.refs_8_) | copy-start | bytes 196612
  25.4 0.7 %copy-start.16 = (bf16[32,3072]{1,0:T(8,128)(2,1)}, bf16[32,3072]{1,0:T(8,128)(2,1)S(1)}, u32[]{:S(2)}) copy-start(bf16[32,3072]{1,0:T(8,128)(2,1)S(1)} %get-tuple-element.11.refs_1_) | copy-start | bytes 589828
  26.1 0.6 %copy-start.19 = (f32[128,128]{1,0:T(8,128)}, f32[128,128]{1,0:T(8,128)S(1)}, u32[]{:S(2)}) copy-start(f32[128,128]{1,0:T(8,128)S(1)} %get-tuple-element.18.refs_6_) | copy-start | bytes 196612
  26.7 0.8 %copy-start.8 = (f32[128,128]{1,0:T(8,128)S(1)}, f32[128,128]{1,0:T(8,128)}, u32[]{:S(2)}) copy-start(f32[128,128]{1,0:T(8,128)} %copy-done.7) | copy-start | bytes 196612
  27.6 0.8 %copy-start.10 = (s32[1,128,1]{2,1,0:T(8,128)S(1)}, s32[1,128,1]{2,1,0:T(8,128)}, u32[]{:S(2)}) copy-start(s32[1,128,1]{2,1,0:T(8,128)} %copy.13.refs_1_) | copy-start | bytes 1540
  28.4 5.1 %copy-start.17 = (bf16[32,3072]{1,0:T(8,128)(2,1)S(1)}, bf16[32,3072]{1,0:T(8,128)(2,1)}, u32[]{:S(2)}) copy-start(bf16[32,3072]{1,0:T(8,128)(2,1)} %copy-done.16) | copy-start | bytes 589828
  28.4 26.9 %copy-start.3 = (bf16[1536,768]{1,0:T(8,128)(2,1)S(1)}, bf16[1536,768]{1,0:T(8,128)(2,1)}, u32[]{:S(2)}) copy-start(bf16[1536,768]{1,0:T(8,128)(2,1)} %refs_11_.1) | copy-start | bytes 7077892
  30.8 24.6 %copy-start.1 = (bf16[768,1536]{1,0:T(8,128)(2,1)S(1)}, bf16[768,1536]{1,0:T(8,128)(2,1)}, u32[]{:S(2)}) copy-start(bf16[768,1536]{1,0:T(8,128)(2,1)} %refs_10_.1) | copy-start | bytes 7077892
  30.8 24.6 %copy-start.6 = (f32[128,768]{1,0:T(8,128)S(1)}, f32[128,768]{1,0:T(8,128)}, u32[]{:S(2)}) copy-start(f32[128,768]{1,0:T(8,128)} %copy-done.5) | copy-start | bytes 1179652
  30.8 24.6 %copy-start.9 = (f32[128,128]{1,0:T(8,128)S(1)}, f32[128,128]{1,0:T(8,128)}, u32[]{:S(2)}) copy-start(f32[128,128]{1,0:T(8,128)} %copy-done.7) | copy-start | bytes 196612
  30.8 24.6 %copy-start.20 = (f32[128,128]{1,0:T(8,128)S(1)}, f32[128,128]{1,0:T(8,128)}, u32[]{:S(2)}) copy-start(f32[128,128]{1,0:T(8,128)} %copy-done.19) | copy-start | bytes 196612
  30.8 9.6 %collective-permute-start.5 = (bf16[2,32,3072]{2,1,0:T(8,128)(2,1)S(1)}, bf16[2,32,3072]{2,1,0:T(8,128)(2,1)S(1)}, u32[]{:S(2)}, u32[]{:S(2)}) collective-permute-start(bf16[2,32,3072]{2,1,0:T(8,128)(2,1)S(1)} %get-tuple-element.15), channel_id=1, source_target_pairs={{0,1},{1,0},{2,3},{3,2},{4,5},{5,4},{6,7},{7,6},{8,9},{9,8},{10,11... | collective-permute-start | bytes 1179656 | tf_op jit(solution)/shard_map/ppermute | solution.py:287
  33.5 6.9 %collective-permute-start.3 = (bf16[32,3072]{1,0:T(8,128)(2,1)S(1)}, bf16[32,3072]{1,0:T(8,128)(2,1)S(1)}, u32[]{:S(2)}, u32[]{:S(2)}) collective-permute-start(bf16[32,3072]{1,0:T(8,128)(2,1)S(1)} %copy-done.17), channel_id=1, source_target_pairs={{0,2},{1,3},{2,0},{3,1},{4,6},{5,7},{6,4},{7,5},{8,10},{9,11},{10,... | collective-permute-start | bytes 589832 | tf_op jit(solution)/shard_map/ppermute | solution.py:278
  34.3 7.4 %collective-permute-start.2 = (bf16[32,3072]{1,0:T(8,128)(2,1)S(1)}, bf16[32,3072]{1,0:T(8,128)(2,1)S(1)}, u32[]{:S(2)}, u32[]{:S(2)}) collective-permute-start(bf16[32,3072]{1,0:T(8,128)(2,1)S(1)} %copy-done.17), channel_id=1, source_target_pairs={{0,1},{1,0},{2,3},{3,2},{4,5},{5,4},{6,7},{7,6},{8,9},{9,8},{10,11... | collective-permute-start | bytes 589832 | tf_op jit(solution)/shard_map/ppermute | solution.py:296
  40.4 1.4 %collective-permute-start.4 = (bf16[32,3072]{1,0:T(8,128)(2,1)S(1)}, bf16[32,3072]{1,0:T(8,128)(2,1)S(1)}, u32[]{:S(2)}, u32[]{:S(2)}) collective-permute-start(bf16[32,3072]{1,0:T(8,128)(2,1)S(1)} %collective-permute-done.3.refs_3_), channel_id=1, source_target_pairs={{0,1},{1,0},{2,3},{3,2},{4,5},{5,4},{6,7},{7,6},{8,9},{9,8},{10,11... | collective-permute-start | bytes 589832 | tf_op jit(solution)/shard_map/ppermute | solution.py:296
  40.4 14.9 %collective-permute-start.6 = (bf16[32,3072]{1,0:T(8,128)(2,1)S(1)}, bf16[32,3072]{1,0:T(8,128)(2,1)S(1)}, u32[]{:S(2)}, u32[]{:S(2)}) collective-permute-start(bf16[32,3072]{1,0:T(8,128)(2,1)S(1)} %add.1), channel_id=1, source_target_pairs={{0,2},{1,3},{2,0},{3,1},{4,6},{5,7},{6,4},{7,5},{8,10},{9,11},{10,... | collective-permute-start | bytes 589832 | tf_op jit(solution)/shard_map/ppermute | solution.py:293

commit v2 on v1

v2 whole, which is shorter than its diff:
```python
import jax
import jax.numpy as jnp
from jax import lax
from jax.experimental import pallas as pl
from jax.experimental.pallas import tpu as pltpu
from jax.sharding import PartitionSpec as P


KS = 7
HALF = KS // 2
LANES = 128
LEFT = 8
F32 = jnp.float32
BF16 = jnp.bfloat16
VMEM = pl.BlockSpec(memory_space=pltpu.VMEM)
SMEM = pl.BlockSpec(memory_space=pltpu.SMEM)
HBM = pl.BlockSpec(memory_space=pltpu.HBM)


def call(body, ins, specs, outs, scratch, limit_mib, flops, moved):
    return pl.pallas_call(
        body,
        in_specs=specs,
        out_shape=tuple(jax.ShapeDtypeStruct(s, d) for s, d in outs),
        out_specs=tuple(VMEM for _ in outs),
        scratch_shapes=scratch,
        compiler_params=pltpu.CompilerParams(vmem_limit_bytes=limit_mib << 20),
        cost_estimate=pl.CostEstimate(
            flops=int(flops), bytes_accessed=int(moved), transcendentals=0
        ),
    )(*ins)


def nt(a, b):
    return lax.dot_general(a, b, (((1,), (1,)), ((), ())), preferred_element_type=F32)


def nn(a, b):
    return jnp.dot(a, b, preferred_element_type=F32)


def normalize(values):
    center = values - jnp.mean(values, axis=-1, keepdims=True)
    inv_std = lax.rsqrt(jnp.mean(center * center, axis=-1, keepdims=True) + 1e-06)
    return center * inv_std, inv_std


def norm_back(grad, normed, inv_std, gain):
    scaled = grad * gain
    return inv_std * (
        scaled
        - jnp.mean(scaled, axis=-1, keepdims=True)
        - normed * jnp.mean(scaled * normed, axis=-1, keepdims=True)
    )


def fetch(hidden, block, w1_hbm, w1_ref, w2_hbm, w2_ref, sems):
    loads = []
    for i, b in enumerate(range(0, hidden, block)):
        cols, lines = (slice(None), pl.ds(b, block)), pl.ds(b, block)
        loads.append(
            (
                pltpu.make_async_copy(w1_hbm.at[cols], w1_ref.at[cols], sems.at[0, i]),
                pltpu.make_async_copy(w2_hbm.at[lines], w2_ref.at[lines], sems.at[1, i]),
            )
        )
        loads[-1][0].start()
        loads[-1][1].start()
    return loads


def forward_body(
    rows, width, channels, hidden, block,
    place, x_ref, near_ref, far_ref, kernel_ref, bias_ref, gain_ref, w1_hbm, w2_hbm,
    scale_ref, down_gain_ref,
    patch_ref, slope_ref, n1_ref, inv1_ref, n2_ref, inv2_ref,
    padded, mixed, first, acc, grid, w1_ref, w2_ref, sems,
):
    loads = fetch(hidden, block, w1_hbm, w1_ref, w2_hbm, w2_ref, sems)
    odd = place[0] % 2 == 1
    chunks = channels // LANES
    tall = rows + 2 * HALF
    padded[:, :, 0:LEFT, :] = jnp.zeros((chunks, tall, LEFT, LANES), F32)
    padded[:, :, LEFT + width :, :] = jnp.zeros((chunks, tall, LEFT, LANES), F32)

    def fill(c, _):
        at = pl.ds(pl.multiple_of(c * LANES, LANES), LANES)
        cols = pl.ds(LEFT, width)
        near, far = near_ref[0, :, :, at].astype(F32), far_ref[0, :, :, at].astype(F32)
        above, below = jnp.where(odd, near, far), jnp.where(odd, far, near)
        padded[c, 0:HALF, cols, :] = above[rows - HALF :]
        padded[c, HALF : HALF + rows, cols, :] = x_ref[0, :, :, at].astype(F32)
        padded[c, HALF + rows :, cols, :] = below[:HALF]
        total = [jnp.zeros((width, LANES), F32) for _ in range(rows)]
        for dx in range(KS):
            taps = [kernel_ref[dy, dx : dx + 1, at] for dy in range(KS)]
            for r in range(tall):
                line = padded[c, r, pl.ds(LEFT - HALF + dx, width), :]
                for out in range(rows):
                    if 0 <= r - out < KS:
                        total[out] = total[out] + line * taps[r - out]
        for out in range(rows):
            mixed[pl.ds(out * width, width), at] = total[out] + bias_ref[at].reshape(1, LANES)
        return 0

    lax.fori_loop(0, chunks, fill, 0)
    count = rows * width
    step = width
    for r in range(0, count, step):
        n1, inv1 = normalize(mixed[r : r + step, :])
        n1_ref[r : r + step, :] = n1
        inv1_ref[r : r + step, :] = jnp.broadcast_to(inv1, (step, LANES))
        first[r : r + step, :] = (n1 * gain_ref[...].reshape(1, channels)).astype(BF16)
    for i, b in enumerate(range(0, hidden, block)):
        loads[i][0].wait()
        loads[i][1].wait()
        pre = nn(first[...], w1_ref[:, b : b + block])
        cumulative = 0.5 * (1.0 + lax.erf(pre * 0.7071067811865476))
        density = jnp.exp(-0.5 * pre * pre) * 0.3989422804014327
        slope_ref[:, b : b + block] = cumulative + pre * density
        term = nn((pre * cumulative).astype(BF16), w2_ref[b : b + block, :])
        if b == 0:
            acc[...] = term
        else:
            acc[...] += term
    for r in range(rows):
        at = pl.ds(r * width, width)
        v = x_ref[0, r].astype(F32) + scale_ref[...].reshape(1, channels) * acc[at, :]
        n2, inv2 = normalize(v)
        n2_ref[at, :] = n2
        inv2_ref[at, :] = jnp.broadcast_to(inv2, (step, LANES))
        second = n2 * down_gain_ref[...].reshape(1, channels)
        for c in range(chunks):
            grid[c, at, :] = second[:, c * LANES : (c + 1) * LANES]
    half = width // 2
    for r in range(rows // 2):
        for a in range(2):
            for b in range(2):
                piece = jnp.concatenate(
                    [
                        grid[c, pl.ds((2 * r + a) * width + b, half, stride=2), :]
                        for c in range(chunks)
                    ],
                    axis=1,
                )
                patch_ref[r * half : (r + 1) * half, (2 * a + b) * channels : (2 * a + b + 1) * channels] = (
                    piece.astype(BF16)
                )


def pull_body(
    spaces, owners, capacity, step,
    place, table_ref, returned_ref, w_hbm,
    keep_ref, send_ref, pick_ref,
    wanted, both, w_ref, sems,
):
    depth = w_ref.shape[0]
    loads = []
    for i, d in enumerate(range(0, depth, step)):
        lines = pl.ds(d, step)
        loads.append(pltpu.make_async_copy(w_hbm.at[lines], w_ref.at[lines], sems.at[i]))
        loads[-1].start()
    core = place[0] % 2
    targets = table_ref[...]
    count = targets.shape[1]
    tall = max(owners, 16)
    hot = targets == lax.broadcasted_iota(jnp.int32, (tall, count), 0)
    sooner = lax.broadcasted_iota(jnp.int32, (count, count), 0) < lax.broadcasted_iota(
        jnp.int32, (count, count), 1
    )
    earlier = nn(jnp.where(hot, 1.0, 0.0).astype(BF16), jnp.where(sooner, 1.0, 0.0).astype(BF16))
    rank = jnp.sum(jnp.where(hot, earlier, 0.0), axis=0, keepdims=True).astype(jnp.int32)
    slots = returned_ref.shape[0]
    pick = jnp.where(
        targets * capacity + rank == lax.broadcasted_iota(jnp.int32, (slots, count), 0), 1.0, 0.0
    ).astype(BF16)
    pick_ref[...] = pick
    band = count // spaces
    wanted[...] = (
        lax.dot_general(pick, returned_ref[...], (((0,), (0,)), ((), ())), preferred_element_type=F32)
        .astype(BF16)
        .reshape(wanted.shape)
    )
    chips = spaces // 2
    for i in range(chips):
        both[i * band : (i + 1) * band, :] = wanted[2 * i + core]
        both[(chips + i) * band : (chips + i + 1) * band, :] = wanted[2 * i + 1 - core]
    for n, d in enumerate(range(0, depth, step)):
        loads[n].wait()
        part = nt(both[...], w_ref[d : d + step, :]).astype(BF16)
        for i in range(chips):
            keep_ref[i, :, d : d + step] = part[i * band : (i + 1) * band]
            send_ref[i, :, d : d + step] = part[(chips + i) * band : (chips + i + 1) * band]


def add_body(chips, place, keep_ref, near_ref, *outs):
    chip = place[0] // 2
    for j in range(1, chips):
        at = lax.rem(chip + j, chips)
        outs[j - 1][...] = (keep_ref[at].astype(F32) + near_ref[at].astype(F32)).astype(BF16)


def backward_body(
    rows, width, channels, hidden, block, chips,
    place, keep_ref, near_ref, *rest,
):
    far = rest[: chips - 1]
    (
        slope_ref, n1_ref, inv1_ref, n2_ref, inv2_ref, gain_ref, w1_hbm, w2_hbm, scale_ref,
        down_gain_ref, out_ref, grid, scaled, acc, w1_ref, w2_ref, sems,
    ) = rest[chips - 1 :]
    loads = fetch(hidden, block, w1_hbm, w1_ref, w2_hbm, w2_ref, sems)
    chip = place[0] // 2
    half = width // 2
    chunks = channels // LANES
    for r in range(rows // 2):
        for a in range(2):
            for b in range(2):
                at = (pl.ds(r * half, half), pl.ds((2 * a + b) * channels, channels))
                value = keep_ref[(chip,) + at].astype(F32) + near_ref[(chip,) + at].astype(F32)
                for piece in far:
                    value = value + piece[at].astype(F32)
                for c in range(chunks):
                    grid[c, pl.ds((2 * r + a) * width + b, half, stride=2), :] = (
                        value[:, c * LANES : (c + 1) * LANES]
                    )
    for r in range(rows):
        at = pl.ds(r * width, width)
        grad = jnp.concatenate([grid[c, at, :] for c in range(chunks)], axis=1)
        back = norm_back(grad, n2_ref[at, :], inv2_ref[at, 0:1], down_gain_ref[...].reshape(1, channels))
        scaled[at, :] = (back * scale_ref[...].reshape(1, channels)).astype(BF16)
    for i, b in enumerate(range(0, hidden, block)):
        loads[i][0].wait()
        loads[i][1].wait()
        grad_pre = (nt(scaled[...], w2_ref[b : b + block, :]) * slope_ref[:, b : b + block]).astype(BF16)
        term = nt(grad_pre, w1_ref[:, b : b + block])
        if b == 0:
            acc[...] = term
        else:
            acc[...] += term
    for r in range(rows):
        at = pl.ds(r * width, width)
        back = norm_back(acc[at, :], n1_ref[at, :], inv1_ref[at, 0:1], gain_ref[...].reshape(1, channels))
        out_ref[0, r] = back.astype(BF16)


def push_body(chips, step, place, *rest):
    pieces = rest[: 2 * chips]
    pick_ref, w_hbm, out_ref, patches, tokens, w_ref, sems = rest[2 * chips :]
    loads = []
    depth = w_ref.shape[0]
    for i, d in enumerate(range(0, depth, step)):
        lines = pl.ds(d, step)
        loads.append(pltpu.make_async_copy(w_hbm.at[lines], w_ref.at[lines], sems.at[i]))
        loads[-1].start()
    chip, core = place[0] // 2, place[0] % 2
    band = pieces[0].shape[0]
    for i, piece in enumerate(pieces):
        patches[i * band : (i + 1) * band, :] = piece[...]
    result = 0.0
    for i, d in enumerate(range(0, depth, step)):
        loads[i].wait()
        result = result + nn(patches[:, d : d + step], w_ref[d : d + step, :])
    result = result.astype(BF16)
    for i in range(2 * chips):
        source = lax.rem(chip + chips - i // 2, chips)
        owner = 2 * source + (core if i % 2 == 0 else 1 - core)
        tokens[owner] = result[i * band : (i + 1) * band]
    flat = tokens[...].reshape(2 * chips * band, tokens.shape[2])
    out_ref[...] = nn(pick_ref[...], flat).astype(BF16)


def on_device(
    section_three, dw_kernel, dw_bias, mix_gain, w_expand, w_reduce, layer_scale, down_gain,
    w_down, owner_table, grad_packed,
):
    owners = lax.axis_size("dp")
    spaces = lax.axis_size("space")
    chips = spaces // 2
    slots = grad_packed.shape[1]
    capacity = slots // owners
    _, rows, width, channels = section_three.shape
    hidden = w_expand.shape[1]
    count = rows * width
    band = count // 4
    tokens = owner_table.shape[1]
    deep, narrow = w_down.shape
    place = lax.axis_index("space").astype(jnp.int32).reshape(1)
    block, step = 256, 768
    weights = [
        pltpu.VMEM(w_expand.shape, BF16), pltpu.VMEM(w_reduce.shape, BF16),
        pltpu.SemaphoreType.DMA((2, hidden // block)),
    ]
    down = [pltpu.VMEM(w_down.shape, BF16), pltpu.SemaphoreType.DMA((deep // step,))]

    swap = [(i, i ^ 1) for i in range(spaces)]
    joints = [(i, i + 1) for i in range(1, spaces - 1, 2)]
    joints = joints + [(b, a) for a, b in joints]

    def send(value, pairs):
        return lax.ppermute(value, "space", pairs)

    def trade(value):
        return lax.all_to_all(value, "dp", split_axis=0, concat_axis=0, tiled=True)

    def onward(j):
        return [(i, (i + 2 * j) % spaces) for i in range(spaces)]

    near = send(section_three, swap)
    far = send(section_three, joints)
    returned = trade(grad_packed[0])

    patches, slope, n1, inv1, n2, inv2 = call(
        lambda *refs: forward_body(rows, width, channels, hidden, block, *refs),
        (place, section_three, near, far, dw_kernel, dw_bias, mix_gain, w_expand, w_reduce,
         layer_scale, down_gain),
        [SMEM] + [VMEM] * 6 + [HBM] * 2 + [VMEM] * 2,
        [((band, 4 * channels), BF16), ((count, hidden), F32), ((count, channels), F32),
         ((count, LANES), F32), ((count, channels), F32), ((count, LANES), F32)],
        [pltpu.VMEM((channels // LANES, rows + 2 * HALF, width + 2 * LEFT, LANES), F32),
         pltpu.VMEM((count, channels), F32), pltpu.VMEM((count, channels), BF16),
         pltpu.VMEM((count, channels), F32), pltpu.VMEM((channels // LANES, count, LANES), F32)] + weights,
        20, 4 * count * channels * hidden, 9e6,
    )
    held = [patches] + [send(patches, onward(j)) for j in range(1, chips)]
    keep, give, pick = call(
        lambda *refs: pull_body(spaces, owners, capacity, step, *refs),
        (place, owner_table.reshape(1, tokens), returned, w_down),
        [SMEM, VMEM, VMEM, HBM],
        [((chips, band, deep), BF16), ((chips, band, deep), BF16), ((slots, tokens), BF16)],
        [pltpu.VMEM((spaces, band, narrow), BF16), pltpu.VMEM((tokens, narrow), BF16)] + down,
        12, 2 * tokens * deep * narrow, 4e6,
    )
    sent = send(give, swap)
    sums = call(
        lambda *refs: add_body(chips, *refs),
        (place, keep, sent), [SMEM, VMEM, VMEM],
        [((band, deep), BF16)] * (chips - 1), [], 4, 2e6, 1e6,
    )
    across = [send(sums[j - 1], onward(j)) for j in range(1, chips)]
    pieces = []
    for piece in held:
        pieces += [piece, send(piece, swap)]
    (buffer,) = call(
        lambda *refs: push_body(chips, step, *refs),
        (place, *pieces, pick, w_down),
        [SMEM] + [VMEM] * (len(pieces) + 1) + [HBM],
        [((slots, narrow), BF16)],
        [pltpu.VMEM((tokens, deep), BF16), pltpu.VMEM((spaces, band, narrow), BF16)] + down,
        12, 2 * tokens * deep * narrow, 4e6,
    )
    arrived = trade(buffer)
    (grad_mixed,) = call(
        lambda *refs: backward_body(rows, width, channels, hidden, block, chips, *refs),
        (place, keep, sent, *across, slope, n1, inv1, n2, inv2, mix_gain, w_expand, w_reduce,
         layer_scale, down_gain),
        [SMEM] + [VMEM] * (7 + chips) + [HBM] * 2 + [VMEM] * 2,
        [(section_three.shape, BF16)],
        [pltpu.VMEM((channels // LANES, count, LANES), F32), pltpu.VMEM((count, channels), BF16),
         pltpu.VMEM((count, channels), F32)] + weights,
        16, 4 * count * channels * hidden, 9e6,
    )
    return arrived[None], grad_mixed


def solution(mesh):
    in_specs = (
        P("dp", "space", None, None), P(), P(), P(), P(), P(), P(), P(), P(None, "space"),
        P("dp", None, None), P("dp", None, "space"),
    )
    out_specs = (P("dp", None, "space"), P("dp", "space", None, None))
    return jax.shard_map(
        on_device, mesh=mesh, in_specs=in_specs, out_specs=out_specs, check_vma=False
    )
```

time: 59.4 us -> 62.6 us (1.054)
  blocking collectives: 12.8 us -> 0 us
  Pallas kernels: 8.6 us -> 16.8 us
  waiting for transfers between devices: 6.06 us -> 12 us
  starting transfers between devices: 13 us -> 15.4 us
  local copies, waits for them, and re-layouts: 17.5 us -> 16.7 us
    all_to_all x1 -> x0, blocking collectives: 12.8 us -> none  [on_device(): lax.all_to_all(buffer, 'dp', split_axis=0, concat_axis=0, tiled=True)]
    pallas_call x5, Pallas kernels: 8.6 us -> 16.8 us  [call(): pl.pallas_call(body, in_specs=specs, out_shape=tuple((jax.ShapeDtypeStruc...]
    all_to_all x1 -> x2, waiting for transfers between devices: 0.01 us -> 6.43 us  [trade(): return lax.all_to_all(value, 'dp', split_axis=0, concat_axis=0, tiled=True)]
    all_to_all x1 -> x2, starting transfers between devices: 6.86 us -> 11.4 us  [trade(): return lax.all_to_all(value, 'dp', split_axis=0, concat_axis=0, tiled=True)]
    reshape x4 -> x0, local copies, waits for them, and re-layouts: 2.76 us -> none  [on_device(): row = lambda v: v.reshape(1, -1)]
    ppermute x7, starting transfers between devices: 6.1 us -> 4 us  [send(): return lax.ppermute(value, 'space', pairs)]
    unnamed x44 -> x51, local copies, waits for them, and re-layouts: 14.8 us -> 16.7 us
  transfers between devices with their start and end apart: 8 -> 9, of which waited for: 2 -> 2; matrix products, arithmetic and copies ran while one was open for 7% -> 0% of each run, Pallas kernels for 6% -> 27%
where the time goes in v2:
time: 62.6 us; the launch traced here: 61.8 us
  Pallas kernels  16.8 us (27%)
  local copies, waits for them, and re-layouts  16.7 us (27%)
  starting transfers between devices  15.4 us (25%)
  waiting for transfers between devices  12 us (19%)
  between operations  0.89 us (1%)
    pallas_call x5, Pallas kernels, call(): pl.pallas_call(body, in_specs=specs, out_shape=tuple((jax.ShapeDtypeStruc...  16.8 us
    unnamed x51, local copies, waits for them, and re-layouts  16.7 us
    all_to_all x2, starting transfers between devices, trade(): return lax.all_to_all(value, 'dp', split_axis=0, concat_axis=0, tiled=True)  11.4 us
    all_to_all x2, waiting for transfers between devices, trade(): return lax.all_to_all(value, 'dp', split_axis=0, concat_axis=0, tiled=True)  6.43 us
    ppermute x7, waiting for transfers between devices, send(): return lax.ppermute(value, 'space', pairs)  5.61 us
    ppermute x7, starting transfers between devices, send(): return lax.ppermute(value, 'space', pairs)  4 us
  transfers between devices with their start and end apart: 9, of which 2 were waited for; matrix products, arithmetic and copies ran while one was open for 0% of the time, Pallas kernels for 27%

profile of v2, /device:TPU:0, one launch (start us, length us, event | category | flops | bytes accessed | tf_op | source)
XLA Modules:
  0.0 61.8 jit_solution(11169794259517285932)
XLA Ops:
  0.6 0.0 copy-start.22
  0.6 0.0 copy-start.21
  0.7 7.5 %all-to-all-start = ((bf16[8,16,384]{2,1,0:T(8,128)(2,1)}), bf16[8,16,384]{2,1,0:T(8,128)(2,1)S(1)}, u32[]{:S(2)}, u32[]{:S(2)}) async-start(bf16[8,16,384]{2,1,0:T(8,128)(2,1)} %bitcast.9), calls=%async_computation | async-start | bytes 196608 | tf_op jit(solution)/shard_map/all_to_all | solution.py:304
  8.1 0.0 collective-permute-start
  8.1 0.7 %collective-permute-start.1 = (bf16[1,4,32,768]{3,2,1,0:T(8,128)(2,1)}, bf16[1,4,32,768]{3,2,1,0:T(8,128)(2,1)S(1)}, u32[]{:S(2)}, u32[]{:S(2)}) collective-permute-start(bf16[1,4,32,768]{3,2,1,0:T(8,128)(2,1)} %refs_1_.1), channel_id=1, source_target_pairs={{1,2},{2,1},{5,6},{6,5},{9,10},{10,9},{13,14},{14,13},{17,18},{18,... | collective-permute-start | bytes 589832 | tf_op jit(solution)/shard_map/ppermute | solution.py:301
  8.8 6.4 %all-to-all-done = bf16[8,16,384]{2,1,0:T(8,128)(2,1)S(1)} async-done(((bf16[8,16,384]{2,1,0:T(8,128)(2,1)}), bf16[8,16,384]{2,1,0:T(8,128)(2,1)S(1)}, u32[]{:S(2)}, u32[]{:S(2)}) %all-to-all-start) | async-done | bytes 98336 | tf_op jit(solution)/shard_map/all_to_all | solution.py:304
  15.3 1.7 %copy-done = bf16[3072,384]{1,0:T(8,128)(2,1)S(1)} copy-done((bf16[3072,384]{1,0:T(8,128)(2,1)S(1)}, bf16[3072,384]{1,0:T(8,128)(2,1)}, u32[]{:S(2)}) %copy-start) | copy-done | bytes 2359320
  16.9 0.7 %copy-done.24 = s32[1,128,1]{1,2,0:T(1,128)S(1)} copy-done((s32[1,128,1]{1,2,0:T(1,128)S(1)}, s32[1,128,1]{1,2,0:T(1,128)}, u32[]{:S(2)}) %copy-start.24) | copy-done | bytes 536
  17.6 2.4 %shard_map.123 = (bf16[2,32,3072]{2,1,0:T(8,128)(2,1)S(1)}, bf16[2,32,3072]{2,1,0:T(8,128)(2,1)S(1)}, bf16[128,128]{1,0:T(8,128)(2,1)S(1)}) custom-call(s32[1]{0:T(128)} %bitcast.refs_0_, s32[1,128]{1,0:T(1,128)S(1)} %bitcast.8, bf16[128,384]{1,0:T(8,128)(2,1)S(1)} %bitcast.6, bf16[3072,384]{1,0:T(8,128)(2,1)S(1)} %copy-done), custom_call_target="tpu_custom_call" | custom-call | flops 301989888 | bytes 4000000 | tf_op jit(solution)/shard_map/pallas_call | solution.py:21
  19.9 0.0 copy-start.1
  20.0 0.1 collective-permute-start.5
  20.0 0.0 collective-permute-done.refs_2_
  20.1 0.0 copy-start.11
  20.1 0.7 %copy-done.11 = bf16[1,4,32,768]{3,2,1,0:T(8,128)(2,1)} copy-done((bf16[1,4,32,768]{3,2,1,0:T(8,128)(2,1)}, bf16[1,4,32,768]{3,2,1,0:T(8,128)(2,1)S(1)}, u32[]{:S(2)}) %copy-start.11) | copy-done | bytes 196632
  20.7 0.0 collective-permute-done.1.refs_3_
  20.7 0.7 %copy-done.13 = bf16[1,4,32,768]{3,2,1,0:T(8,128)(2,1)} copy-done((bf16[1,4,32,768]{3,2,1,0:T(8,128)(2,1)}, bf16[1,4,32,768]{3,2,1,0:T(8,128)(2,1)S(1)}, u32[]{:S(2)}) %copy-start.13) | copy-done | bytes 196632
  21.4 0.0 copy-done.21
  21.4 0.0 copy-start.3
  21.4 1.7 %copy-done.3 = bf16[1536,768]{1,0:T(8,128)(2,1)S(1)} copy-done((bf16[1536,768]{1,0:T(8,128)(2,1)S(1)}, bf16[1536,768]{1,0:T(8,128)(2,1)}, u32[]{:S(2)}) %copy-start.3) | copy-done | bytes 2359320
  23.1 0.9 %copy-done.10 = bf16[1,4,32,768]{3,2,1,0:T(8,128)(2,1)S(1)} copy-done((bf16[1,4,32,768]{3,2,1,0:T(8,128)(2,1)S(1)}, bf16[1,4,32,768]{3,2,1,0:T(8,128)(2,1)}, u32[]{:S(2)}) %copy-start.10) | copy-done | bytes 196632
  24.0 0.9 %copy-done.12 = bf16[1,4,32,768]{3,2,1,0:T(8,128)(2,1)S(1)} copy-done((bf16[1,4,32,768]{3,2,1,0:T(8,128)(2,1)S(1)}, bf16[1,4,32,768]{3,2,1,0:T(8,128)(2,1)}, u32[]{:S(2)}) %copy-start.12) | copy-done | bytes 196632
  24.9 0.9 %copy-done.14 = bf16[1,4,32,768]{3,2,1,0:T(8,128)(2,1)S(1)} copy-done((bf16[1,4,32,768]{3,2,1,0:T(8,128)(2,1)S(1)}, bf16[1,4,32,768]{3,2,1,0:T(8,128)(2,1)}, u32[]{:S(2)}) %copy-start.14) | copy-done | bytes 196632
  25.9 0.9 %copy-done.15 = f32[7,7,768]{2,1,0:T(8,128)S(1)} copy-done((f32[7,7,768]{2,1,0:T(8,128)S(1)}, f32[7,7,768]{2,1,0:T(8,128)}, u32[]{:S(2)}) %copy-start.15) | copy-done | bytes 150552
  26.8 5.5 %shard_map.122 = (bf16[32,3072]{1,0:T(8,128)(2,1)S(1)}, f32[128,1536]{1,0:T(8,128)S(1)}, f32[128,768]{1,0:T(8,128)S(1)}, f32[128,128]{1,0:T(8,128)S(1)}, f32[128,768]{1,0:T(8,128)S(1)}, /*index=5*/f32[128,128]{1,0:T(8,128)S(1)}) custom-call(s32[1]{0:T(128)} %bitcast.refs_0_, bf16[1,4,32,768]{3,2,1,0:T(8,128)(2,1)S(1)} %copy-done.10, ...), custom_call_target="tpu_custom_call" | custom-call | flops 603979776 | bytes 9000000 | tf_op jit(solution)/shard_map/pallas_call | solution.py:21
  32.3 1.6 %collective-permute-start.3 = (bf16[32,3072]{1,0:T(8,128)(2,1)S(1)}, bf16[32,3072]{1,0:T(8,128)(2,1)S(1)}, u32[]{:S(2)}, u32[]{:S(2)}) collective-permute-start(bf16[32,3072]{1,0:T(8,128)(2,1)S(1)} %get-tuple-element.11.refs_1_), channel_id=1, source_target_pairs={{0,2},{1,3},{2,0},{3,1},{4,6},{5,7},{6,4},{7,5},{8,10},{9,11},{10,... | collective-permute-start | bytes 589832 | tf_op jit(solution)/shard_map/ppermute | solution.py:301
  33.9 0.2 collective-permute-start.2
  34.1 5.6 %collective-permute-done.3.refs_3_ = bf16[32,3072]{1,0:T(8,128)(2,1)S(1)} collective-permute-done((bf16[32,3072]{1,0:T(8,128)(2,1)S(1)}, bf16[32,3072]{1,0:T(8,128)(2,1)S(1)}, u32[]{:S(2)}, u32[]{:S(2)}) %collective-permute-start.3) | collective-permute-done | bytes 196640 | tf_op jit(solution)/shard_map/ppermute | solution.py:301
  39.7 0.0 collective-permute-start.4
  39.7 0.0 collective-permute-done.5.refs_2_
  39.7 0.7 %shard_map.125 = bf16[32,3072]{1,0:T(8,128)(2,1)} custom-call(s32[1]{0:T(128)} %bitcast.refs_0_, bf16[2,32,3072]{2,1,0:T(8,128)(2,1)S(1)} %get-tuple-element.13.refs_1_, bf16[2,32,3072]{2,1,0:T(8,128)(2,1)S(1)} %collective-permute-done.5.refs_2_), custom_call_target="tpu_custom_call" | custom-call | flops 2000000 | bytes 1000000 | tf_op jit(solution)/shard_map/pallas_call | solution.py:21
  40.4 1.5 %collective-permute-start.6 = (bf16[32,3072]{1,0:T(8,128)(2,1)}, bf16[32,3072]{1,0:T(8,128)(2,1)}, u32[]{:S(2)}, u32[]{:S(2)}) collective-permute-start(bf16[32,3072]{1,0:T(8,128)(2,1)} %shard_map.125), channel_id=1, source_target_pairs={{0,2},{1,3},{2,0},{3,1},{4,6},{5,7},{6,4},{7,5},{8,10},{9,11},{10,... | collective-permute-start | bytes 589832 | tf_op jit(solution)/shard_map/ppermute | solution.py:301
  41.9 0.0 collective-permute-done.2.refs_2_
  41.9 0.0 collective-permute-done.4.refs_4_
  41.9 0.0 copy-done.1
  41.9 1.6 %shard_map.124 = bf16[128,384]{1,0:T(8,128)(2,1)S(1)} custom-call(s32[1]{0:T(128)} %bitcast.refs_0_, bf16[32,3072]{1,0:T(8,128)(2,1)S(1)} %get-tuple-element.11.refs_1_, bf16[32,3072]{1,0:T(8,128)(2,1)S(1)} %collective-permute-done.2.refs_2_, bf16[32,3072]{1,0:T(8,128)(2,1)S(1)} %collective-permute-done.3.refs_3_, ...), custom_call_target="tpu_custom_call" | custom-call | flops 301989888 | bytes 4000000 | tf_op jit(solution)/shard_map/pallas_call | solution.py:21
  43.6 0.0 copy-start.9
  43.6 0.6 %copy-done.9 = bf16[128,384]{1,0:T(8,128)(2,1)} copy-done((bf16[128,384]{1,0:T(8,128)(2,1)}, bf16[128,384]{1,0:T(8,128)(2,1)S(1)}, u32[]{:S(2)}) %copy-start.9) | copy-done | bytes 98328
  44.2 4.0 %all-to-all-start.1 = ((bf16[8,16,384]{2,1,0:T(8,128)(2,1)}), bf16[8,16,384]{2,1,0:T(8,128)(2,1)}, u32[]{:S(2)}, u32[]{:S(2)}) async-start(bf16[8,16,384]{2,1,0:T(8,128)(2,1)} %bitcast.7), calls=%async_computation.1 | async-start | bytes 196608 | tf_op jit(solution)/shard_map/all_to_all | solution.py:304
  48.2 0.0 collective-permute-done.6.refs_3_
  48.2 0.0 copy-start.4
  48.2 1.7 %copy-done.4 = bf16[1536,768]{1,0:T(8,128)(2,1)S(1)} copy-done((bf16[1536,768]{1,0:T(8,128)(2,1)S(1)}, bf16[1536,768]{1,0:T(8,128)(2,1)}, u32[]{:S(2)}) %copy-start.4) | copy-done | bytes 2359320
  49.9 1.1 %copy-done.6 = f32[128,1536]{1,0:T(8,128)S(1)} copy-done((f32[128,1536]{1,0:T(8,128)S(1)}, f32[128,1536]{1,0:T(8,128)}, u32[]{:S(2)}) %copy-start.6) | copy-done | bytes 786456
  51.0 1.0 %copy-done.8 = f32[128,768]{1,0:T(8,128)S(1)} copy-done((f32[128,768]{1,0:T(8,128)S(1)}, f32[128,768]{1,0:T(8,128)}, u32[]{:S(2)}) %copy-start.8) | copy-done | bytes 393240
  52.0 0.8 %copy-done.17 = f32[128,128]{1,0:T(8,128)S(1)} copy-done((f32[128,128]{1,0:T(8,128)S(1)}, f32[128,128]{1,0:T(8,128)}, u32[]{:S(2)}) %copy-start.17) | copy-done | bytes 65560
  52.9 0.8 %copy-done.19 = f32[128,128]{1,0:T(8,128)S(1)} copy-done((f32[128,128]{1,0:T(8,128)S(1)}, f32[128,128]{1,0:T(8,128)}, u32[]{:S(2)}) %copy-start.19) | copy-done | bytes 65560
  53.7 6.6 %shard_map.126 = bf16[1,4,32,768]{3,2,1,0:T(8,128)(2,1)} custom-call(s32[1]{0:T(128)} %bitcast.refs_0_, bf16[2,32,3072]{2,1,0:T(8,128)(2,1)S(1)} %get-tuple-element.13.refs_1_, bf16[2,32,3072]{2,1,0:T(8,128)(2,1)S(1)} %collective-permute-done.5.refs_2_, bf16[32,3072]{1,0:T(8,128)(2,1)} %collective-permute-done.6.refs_3_, f32[128,1536]{1,0:T(8,128)S(1)} %copy-done.6, ...), custom_call_target="tpu_custom_call" | custom-call | flops 603979776 | bytes 9000000 | tf_op jit(solution)/shard_map/pallas_call | solution.py:21
  60.3 0.0 all-to-all-done.1
  60.3 1.5 %copy.14 = bf16[1,128,384]{2,1,0:T(8,128)(2,1)} copy(bf16[1,128,384]{2,1,0:T(8,128)(2,1)} %bitcast.5) | data formatting | bytes 196608
  (26 shorter events, 0.0 us)
Async XLA Ops:
  0.6 20.8 %copy-start.22 = (f32[768]{0:T(1024)S(1)}, f32[768]{0:T(1024)}, u32[]{:S(2)}) copy-start(f32[768]{0:T(1024)} %refs_13_.1) | copy-start | bytes 9220
  0.6 20.8 %copy-start.21 = (f32[768]{0:T(1024)S(1)}, f32[768]{0:T(1024)}, u32[]{:S(2)}) copy-start(f32[768]{0:T(1024)} %refs_12_.1) | copy-start | bytes 9220
  0.7 20.8 %copy-start.20 = (f32[768]{0:T(1024)S(1)}, f32[768]{0:T(1024)}, u32[]{:S(2)}) copy-start(f32[768]{0:T(1024)} %refs_9_.3) | copy-start | bytes 9220
  0.7 20.7 %copy-start.23 = (f32[768]{0:T(1024)S(1)}, f32[768]{0:T(1024)}, u32[]{:S(2)}) copy-start(f32[768]{0:T(1024)} %refs_5_.1) | copy-start | bytes 9220
  0.7 14.6 %all-to-all-start = ((bf16[8,16,384]{2,1,0:T(8,128)(2,1)}), bf16[8,16,384]{2,1,0:T(8,128)(2,1)S(1)}, u32[]{:S(2)}, u32[]{:S(2)}) async-start(bf16[8,16,384]{2,1,0:T(8,128)(2,1)} %bitcast.9), calls=%async_computation | async-start | bytes 196608 | tf_op jit(solution)/shard_map/all_to_all | solution.py:304
  8.1 11.9 %collective-permute-start = (bf16[1,4,32,768]{3,2,1,0:T(8,128)(2,1)}, bf16[1,4,32,768]{3,2,1,0:T(8,128)(2,1)S(1)}, u32[]{:S(2)}, u32[]{:S(2)}) collective-permute-start(bf16[1,4,32,768]{3,2,1,0:T(8,128)(2,1)} %refs_1_.1), channel_id=1, source_target_pairs={{0,1},{1,0},{2,3},{3,2},{4,5},{5,4},{6,7},{7,6},{8,9},{9,8},{10,11... | collective-permute-start | bytes 589832 | tf_op jit(solution)/shard_map/ppermute | solution.py:301
  8.1 12.6 %collective-permute-start.1 = (bf16[1,4,32,768]{3,2,1,0:T(8,128)(2,1)}, bf16[1,4,32,768]{3,2,1,0:T(8,128)(2,1)S(1)}, u32[]{:S(2)}, u32[]{:S(2)}) collective-permute-start(bf16[1,4,32,768]{3,2,1,0:T(8,128)(2,1)} %refs_1_.1), channel_id=1, source_target_pairs={{1,2},{2,1},{5,6},{6,5},{9,10},{10,9},{13,14},{14,13},{17,18},{18,... | collective-permute-start | bytes 589832 | tf_op jit(solution)/shard_map/ppermute | solution.py:301
  15.2 1.7 %copy-start = (bf16[3072,384]{1,0:T(8,128)(2,1)S(1)}, bf16[3072,384]{1,0:T(8,128)(2,1)}, u32[]{:S(2)}) copy-start(bf16[3072,384]{1,0:T(8,128)(2,1)} %refs_6_.3) | copy-start | bytes 7077892
  16.9 0.7 %copy-start.24 = (s32[1,128,1]{1,2,0:T(1,128)S(1)}, s32[1,128,1]{1,2,0:T(1,128)}, u32[]{:S(2)}) copy-start(s32[1,128,1]{1,2,0:T(1,128)} %param.20) | copy-start | bytes 1540
  17.6 3.8 %copy-start.2 = (bf16[768,1536]{1,0:T(8,128)(2,1)S(1)}, bf16[768,1536]{1,0:T(8,128)(2,1)}, u32[]{:S(2)}) copy-start(bf16[768,1536]{1,0:T(8,128)(2,1)} %refs_10_.3) | copy-start | bytes 7077892
  19.9 21.9 %copy-start.1 = (bf16[3072,384]{1,0:T(8,128)(2,1)S(1)}, bf16[3072,384]{1,0:T(8,128)(2,1)}, u32[]{:S(2)}) copy-start(bf16[3072,384]{1,0:T(8,128)(2,1)} %refs_6_.3) | copy-start | bytes 7077892
  20.0 19.7 %collective-permute-start.5 = (bf16[2,32,3072]{2,1,0:T(8,128)(2,1)S(1)}, bf16[2,32,3072]{2,1,0:T(8,128)(2,1)S(1)}, u32[]{:S(2)}, u32[]{:S(2)}) collective-permute-start(bf16[2,32,3072]{2,1,0:T(8,128)(2,1)S(1)} %get-tuple-element.14), channel_id=1, source_target_pairs={{0,1},{1,0},{2,3},{3,2},{4,5},{5,4},{6,7},{7,6},{8,9},{9,8},{10,11... | collective-permute-start | bytes 1179656 | tf_op jit(solution)/shard_map/ppermute | solution.py:301
  20.1 0.7 %copy-start.11 = (bf16[1,4,32,768]{3,2,1,0:T(8,128)(2,1)}, bf16[1,4,32,768]{3,2,1,0:T(8,128)(2,1)S(1)}, u32[]{:S(2)}) copy-start(bf16[1,4,32,768]{3,2,1,0:T(8,128)(2,1)S(1)} %collective-permute-done.refs_2_) | copy-start | bytes 589828
  20.7 0.7 %copy-start.13 = (bf16[1,4,32,768]{3,2,1,0:T(8,128)(2,1)}, bf16[1,4,32,768]{3,2,1,0:T(8,128)(2,1)S(1)}, u32[]{:S(2)}) copy-start(bf16[1,4,32,768]{3,2,1,0:T(8,128)(2,1)S(1)} %collective-permute-done.1.refs_3_) | copy-start | bytes 589828
  21.4 1.7 %copy-start.3 = (bf16[1536,768]{1,0:T(8,128)(2,1)S(1)}, bf16[1536,768]{1,0:T(8,128)(2,1)}, u32[]{:S(2)}) copy-start(bf16[1536,768]{1,0:T(8,128)(2,1)} %refs_11_.1) | copy-start | bytes 7077892
  23.1 0.9 %copy-start.10 = (bf16[1,4,32,768]{3,2,1,0:T(8,128)(2,1)S(1)}, bf16[1,4,32,768]{3,2,1,0:T(8,128)(2,1)}, u32[]{:S(2)}) copy-start(bf16[1,4,32,768]{3,2,1,0:T(8,128)(2,1)} %refs_1_.1) | copy-start | bytes 589828
  24.0 0.9 %copy-start.12 = (bf16[1,4,32,768]{3,2,1,0:T(8,128)(2,1)S(1)}, bf16[1,4,32,768]{3,2,1,0:T(8,128)(2,1)}, u32[]{:S(2)}) copy-start(bf16[1,4,32,768]{3,2,1,0:T(8,128)(2,1)} %copy-done.11) | copy-start | bytes 589828
  24.9 0.9 %copy-start.14 = (bf16[1,4,32,768]{3,2,1,0:T(8,128)(2,1)S(1)}, bf16[1,4,32,768]{3,2,1,0:T(8,128)(2,1)}, u32[]{:S(2)}) copy-start(bf16[1,4,32,768]{3,2,1,0:T(8,128)(2,1)} %copy-done.13) | copy-start | bytes 589828
  25.9 0.9 %copy-start.15 = (f32[7,7,768]{2,1,0:T(8,128)S(1)}, f32[7,7,768]{2,1,0:T(8,128)}, u32[]{:S(2)}) copy-start(f32[7,7,768]{2,1,0:T(8,128)} %refs_4_.1) | copy-start | bytes 451588
  32.3 11.3 %copy-start.5 = (f32[128,1536]{1,0:T(8,128)}, f32[128,1536]{1,0:T(8,128)S(1)}, u32[]{:S(2)}) copy-start(f32[128,1536]{1,0:T(8,128)S(1)} %get-tuple-element.15.refs_4_) | copy-start | bytes 2359300
  32.3 11.3 %copy-start.7 = (f32[128,768]{1,0:T(8,128)}, f32[128,768]{1,0:T(8,128)S(1)}, u32[]{:S(2)}) copy-start(f32[128,768]{1,0:T(8,128)S(1)} %get-tuple-element.18.refs_7_) | copy-start | bytes 1179652
  32.3 11.3 %copy-start.16 = (f32[128,128]{1,0:T(8,128)}, f32[128,128]{1,0:T(8,128)S(1)}, u32[]{:S(2)}) copy-start(f32[128,128]{1,0:T(8,128)S(1)} %get-tuple-element.17.refs_6_) | copy-start | bytes 196612
  32.3 11.3 %copy-start.18 = (f32[128,128]{1,0:T(8,128)}, f32[128,128]{1,0:T(8,128)S(1)}, u32[]{:S(2)}) copy-start(f32[128,128]{1,0:T(8,128)S(1)} %get-tuple-element.19.refs_8_) | copy-start | bytes 196612
  32.3 7.4 %collective-permute-start.3 = (bf16[32,3072]{1,0:T(8,128)(2,1)S(1)}, bf16[32,3072]{1,0:T(8,128)(2,1)S(1)}, u32[]{:S(2)}, u32[]{:S(2)}) collective-permute-start(bf16[32,3072]{1,0:T(8,128)(2,1)S(1)} %get-tuple-element.11.refs_1_), channel_id=1, source_target_pairs={{0,2},{1,3},{2,0},{3,1},{4,6},{5,7},{6,4},{7,5},{8,10},{9,11},{10,... | collective-permute-start | bytes 589832 | tf_op jit(solution)/shard_map/ppermute | solution.py:301
  33.9 8.0 %collective-permute-start.2 = (bf16[32,3072]{1,0:T(8,128)(2,1)S(1)}, bf16[32,3072]{1,0:T(8,128)(2,1)S(1)}, u32[]{:S(2)}, u32[]{:S(2)}) collective-permute-start(bf16[32,3072]{1,0:T(8,128)(2,1)S(1)} %get-tuple-element.11.refs_1_), channel_id=1, source_target_pairs={{0,1},{1,0},{2,3},{3,2},{4,5},{5,4},{6,7},{7,6},{8,9},{9,8},{10,11... | collective-permute-start | bytes 589832 | tf_op jit(solution)/shard_map/ppermute | solution.py:301
  39.7 2.2 %collective-permute-start.4 = (bf16[32,3072]{1,0:T(8,128)(2,1)S(1)}, bf16[32,3072]{1,0:T(8,128)(2,1)S(1)}, u32[]{:S(2)}, u32[]{:S(2)}) collective-permute-start(bf16[32,3072]{1,0:T(8,128)(2,1)S(1)} %collective-permute-done.3.refs_3_), channel_id=1, source_target_pairs={{0,1},{1,0},{2,3},{3,2},{4,5},{5,4},{6,7},{7,6},{8,9},{9,8},{10,11... | collective-permute-start | bytes 589832 | tf_op jit(solution)/shard_map/ppermute | solution.py:301
  40.4 7.8 %collective-permute-start.6 = (bf16[32,3072]{1,0:T(8,128)(2,1)}, bf16[32,3072]{1,0:T(8,128)(2,1)}, u32[]{:S(2)}, u32[]{:S(2)}) collective-permute-start(bf16[32,3072]{1,0:T(8,128)(2,1)} %shard_map.125), channel_id=1, source_target_pairs={{0,2},{1,3},{2,0},{3,1},{4,6},{5,7},{6,4},{7,5},{8,10},{9,11},{10,... | collective-permute-start | bytes 589832 | tf_op jit(solution)/shard_map/ppermute | solution.py:301
  43.6 0.6 %copy-start.9 = (bf16[128,384]{1,0:T(8,128)(2,1)}, bf16[128,384]{1,0:T(8,128)(2,1)S(1)}, u32[]{:S(2)}) copy-start(bf16[128,384]{1,0:T(8,128)(2,1)S(1)} %shard_map.124) | copy-start | bytes 294916
  44.2 16.1 %all-to-all-start.1 = ((bf16[8,16,384]{2,1,0:T(8,128)(2,1)}), bf16[8,16,384]{2,1,0:T(8,128)(2,1)}, u32[]{:S(2)}, u32[]{:S(2)}) async-start(bf16[8,16,384]{2,1,0:T(8,128)(2,1)} %bitcast.7), calls=%async_computation.1 | async-start | bytes 196608 | tf_op jit(solution)/shard_map/all_to_all | solution.py:304
  48.2 1.7 %copy-start.4 = (bf16[1536,768]{1,0:T(8,128)(2,1)S(1)}, bf16[1536,768]{1,0:T(8,128)(2,1)}, u32[]{:S(2)}) copy-start(bf16[1536,768]{1,0:T(8,128)(2,1)} %refs_11_.1) | copy-start | bytes 7077892
  49.9 1.1 %copy-start.6 = (f32[128,1536]{1,0:T(8,128)S(1)}, f32[128,1536]{1,0:T(8,128)}, u32[]{:S(2)}) copy-start(f32[128,1536]{1,0:T(8,128)} %copy-done.5) | copy-start | bytes 2359300
  51.0 1.0 %copy-start.8 = (f32[128,768]{1,0:T(8,128)S(1)}, f32[128,768]{1,0:T(8,128)}, u32[]{:S(2)}) copy-start(f32[128,768]{1,0:T(8,128)} %copy-done.7) | copy-start | bytes 1179652
  52.0 0.8 %copy-start.17 = (f32[128,128]{1,0:T(8,128)S(1)}, f32[128,128]{1,0:T(8,128)}, u32[]{:S(2)}) copy-start(f32[128,128]{1,0:T(8,128)} %copy-done.16) | copy-start | bytes 196612
  52.9 0.8 %copy-start.19 = (f32[128,128]{1,0:T(8,128)S(1)}, f32[128,128]{1,0:T(8,128)}, u32[]{:S(2)}) copy-start(f32[128,128]{1,0:T(8,128)} %copy-done.18) | copy-start | bytes 196612

commit v3 on v2

--- a/solution.py
+++ b/solution.py
@@ -17,12 +17,30 @@
 HBM = pl.BlockSpec(memory_space=pltpu.HBM)
 
 
+def far_off(*values):
+    return tuple(pltpu.with_memory_space_constraint(v, pltpu.HBM) for v in values)
+
+
+def close(*values):
+    return tuple(pltpu.with_memory_space_constraint(v, pltpu.VMEM) for v in values)
+
+
+def start(copies):
+    for copy in copies:
+        copy.start()
+
+
+def wait(copies):
+    for copy in copies:
+        copy.wait()
+
+
 def call(body, ins, specs, outs, scratch, limit_mib, flops, moved):
     return pl.pallas_call(
         body,
         in_specs=specs,
-        out_shape=tuple(jax.ShapeDtypeStruct(s, d) for s, d in outs),
-        out_specs=tuple(VMEM for _ in outs),
+        out_shape=tuple(o if isinstance(o, jax.ShapeDtypeStruct) else pltpu.VMEM(*o) for o in outs),
+        out_specs=tuple(HBM if isinstance(o, jax.ShapeDtypeStruct) else VMEM for o in outs),
         scratch_shapes=scratch,
         compiler_params=pltpu.CompilerParams(vmem_limit_bytes=limit_mib << 20),
         cost_estimate=pl.CostEstimate(
@@ -71,25 +89,40 @@
 
 def forward_body(
     rows, width, channels, hidden, block,
-    place, x_ref, near_ref, far_ref, kernel_ref, bias_ref, gain_ref, w1_hbm, w2_hbm,
-    scale_ref, down_gain_ref,
+    place, near_ref, far_ref, x_hbm, kernel_hbm, bias_hbm, gain_hbm, w1_hbm, w2_hbm,
+    scale_hbm, down_gain_hbm,
     patch_ref, slope_ref, n1_ref, inv1_ref, n2_ref, inv2_ref,
-    padded, mixed, first, acc, grid, w1_ref, w2_ref, sems,
+    x_ref, kernel_ref, bias_ref, gain_ref, scale_ref, down_gain_ref,
+    padded, mixed, first, acc, grid, small_sems, band_sems, w1_ref, w2_ref, sems,
 ):
-    loads = fetch(hidden, block, w1_hbm, w1_ref, w2_hbm, w2_ref, sems)
     odd = place[0] % 2 == 1
     chunks = channels // LANES
     tall = rows + 2 * HALF
+    sources = (kernel_hbm, bias_hbm, gain_hbm, scale_hbm, down_gain_hbm)
+    targets = (kernel_ref, bias_ref, gain_ref, scale_ref, down_gain_ref)
+    small = [pltpu.make_async_copy(s, t, small_sems.at[i]) for i, (s, t) in enumerate(zip(sources, targets))]
+
+    def bands(c):
+        at = (0, slice(None), slice(None), pl.ds(pl.multiple_of(c * LANES, LANES), LANES))
+        return [pltpu.make_async_copy(x_hbm.at[at], x_ref.at[c], band_sems.at[c])]
+
+    start(small[:2])
+    for c in range(chunks):
+        start(bands(c))
+    start(small[2:])
+    loads = fetch(hidden, block, w1_hbm, w1_ref, w2_hbm, w2_ref, sems)
     padded[:, :, 0:LEFT, :] = jnp.zeros((chunks, tall, LEFT, LANES), F32)
     padded[:, :, LEFT + width :, :] = jnp.zeros((chunks, tall, LEFT, LANES), F32)
+    wait(small[:2])
 
     def fill(c, _):
         at = pl.ds(pl.multiple_of(c * LANES, LANES), LANES)
         cols = pl.ds(LEFT, width)
+        wait(bands(c))
         near, far = near_ref[0, :, :, at].astype(F32), far_ref[0, :, :, at].astype(F32)
         above, below = jnp.where(odd, near, far), jnp.where(odd, far, near)
         padded[c, 0:HALF, cols, :] = above[rows - HALF :]
-        padded[c, HALF : HALF + rows, cols, :] = x_ref[0, :, :, at].astype(F32)
+        padded[c, HALF : HALF + rows, cols, :] = x_ref[c].astype(F32)
         padded[c, HALF + rows :, cols, :] = below[:HALF]
         total = [jnp.zeros((width, LANES), F32) for _ in range(rows)]
         for dx in range(KS):
@@ -104,6 +137,7 @@
         return 0
 
     lax.fori_loop(0, chunks, fill, 0)
+    wait(small[2:])
     count = rows * width
     step = width
     for r in range(0, count, step):
@@ -125,7 +159,8 @@
             acc[...] += term
     for r in range(rows):
         at = pl.ds(r * width, width)
-        v = x_ref[0, r].astype(F32) + scale_ref[...].reshape(1, channels) * acc[at, :]
+        line = jnp.concatenate([x_ref[c, r] for c in range(chunks)], axis=1)
+        v = line.astype(F32) + scale_ref[...].reshape(1, channels) * acc[at, :]
         n2, inv2 = normalize(v)
         n2_ref[at, :] = n2
         inv2_ref[at, :] = jnp.broadcast_to(inv2, (step, LANES))
@@ -150,17 +185,20 @@
 
 def pull_body(
     spaces, owners, capacity, step,
-    place, table_ref, returned_ref, w_hbm,
-    keep_ref, send_ref, pick_ref,
-    wanted, both, w_ref, sems,
+    place, returned_ref, table_hbm, w_hbm,
+    keep_ref, send_ref, pick_ref, w_ref,
+    table_ref, wanted, both, small_sems, sems,
 ):
     depth = w_ref.shape[0]
+    small = [pltpu.make_async_copy(table_hbm, table_ref, small_sems.at[0])]
+    start(small)
     loads = []
     for i, d in enumerate(range(0, depth, step)):
         lines = pl.ds(d, step)
         loads.append(pltpu.make_async_copy(w_hbm.at[lines], w_ref.at[lines], sems.at[i]))
         loads[-1].start()
     core = place[0] % 2
+    small[0].wait()
     targets = table_ref[...]
     count = targets.shape[1]
     tall = max(owners, 16)
@@ -206,9 +244,13 @@
 ):
     far = rest[: chips - 1]
     (
-        slope_ref, n1_ref, inv1_ref, n2_ref, inv2_ref, gain_ref, w1_hbm, w2_hbm, scale_ref,
-        down_gain_ref, out_ref, grid, scaled, acc, w1_ref, w2_ref, sems,
+        slope_ref, n1_ref, inv1_ref, n2_ref, inv2_ref, gain_hbm, w1_hbm, w2_hbm, scale_hbm,
+        down_gain_hbm, out_hbm, gain_ref, scale_ref, down_gain_ref, out_ref, grid, scaled, acc,
+        small_sems, out_sems, w1_ref, w2_ref, sems,
     ) = rest[chips - 1 :]
+    sources, targets = (down_gain_hbm, scale_hbm, gain_hbm), (down_gain_ref, scale_ref, gain_ref)
+    small = [pltpu.make_async_copy(s, t, small_sems.at[i]) for i, (s, t) in enumerate(zip(sources, targets))]
+    start(small)
     loads = fetch(hidden, block, w1_hbm, w1_ref, w2_hbm, w2_ref, sems)
     chip = place[0] // 2
     half = width // 2
@@ -224,6 +266,7 @@
                     grid[c, pl.ds((2 * r + a) * width + b, half, stride=2), :] = (
                         value[:, c * LANES : (c + 1) * LANES]
                     )
+    wait(small)
     for r in range(rows):
         at = pl.ds(r * width, width)
         grad = jnp.concatenate([grid[c, at, :] for c in range(chunks)], axis=1)
@@ -238,30 +281,24 @@
             acc[...] = term
         else:
             acc[...] += term
+    stores = []
     for r in range(rows):
         at = pl.ds(r * width, width)
         back = norm_back(acc[at, :], n1_ref[at, :], inv1_ref[at, 0:1], gain_ref[...].reshape(1, channels))
         out_ref[0, r] = back.astype(BF16)
-
-
-def push_body(chips, step, place, *rest):
+        stores.append(pltpu.make_async_copy(out_ref.at[0, r], out_hbm.at[0, r], out_sems.at[r]))
+        stores[-1].start()
+    wait(stores)
+
+
+def push_body(chips, place, *rest):
     pieces = rest[: 2 * chips]
-    pick_ref, w_hbm, out_ref, patches, tokens, w_ref, sems = rest[2 * chips :]
-    loads = []
-    depth = w_ref.shape[0]
-    for i, d in enumerate(range(0, depth, step)):
-        lines = pl.ds(d, step)
-        loads.append(pltpu.make_async_copy(w_hbm.at[lines], w_ref.at[lines], sems.at[i]))
-        loads[-1].start()
+    pick_ref, w_ref, out_ref, patches, tokens = rest[2 * chips :]
     chip, core = place[0] // 2, place[0] % 2
     band = pieces[0].shape[0]
     for i, piece in enumerate(pieces):
         patches[i * band : (i + 1) * band, :] = piece[...]
-    result = 0.0
-    for i, d in enumerate(range(0, depth, step)):
-        loads[i].wait()
-        result = result + nn(patches[:, d : d + step], w_ref[d : d + step, :])
-    result = result.astype(BF16)
+    result = nn(patches[...], w_ref[...]).astype(BF16)
     for i in range(2 * chips):
         source = lax.rem(chip + chips - i // 2, chips)
         owner = 2 * source + (core if i % 2 == 0 else 1 - core)
@@ -291,7 +328,6 @@
         pltpu.VMEM(w_expand.shape, BF16), pltpu.VMEM(w_reduce.shape, BF16),
         pltpu.SemaphoreType.DMA((2, hidden // block)),
     ]
-    down = [pltpu.VMEM(w_down.shape, BF16), pltpu.SemaphoreType.DMA((deep // step,))]
 
     swap = [(i, i ^ 1) for i in range(spaces)]
     joints = [(i, i + 1) for i in range(1, spaces - 1, 2)]
@@ -310,31 +346,39 @@
     far = send(section_three, joints)
     returned = trade(grad_packed[0])
 
+    vector = pltpu.VMEM((channels,), F32)
+    lanes = channels // LANES
     patches, slope, n1, inv1, n2, inv2 = call(
         lambda *refs: forward_body(rows, width, channels, hidden, block, *refs),
-        (place, section_three, near, far, dw_kernel, dw_bias, mix_gain, w_expand, w_reduce,
-         layer_scale, down_gain),
-        [SMEM] + [VMEM] * 6 + [HBM] * 2 + [VMEM] * 2,
+        (place, *close(near, far), *far_off(section_three, dw_kernel, dw_bias, mix_gain, w_expand, w_reduce,
+                         layer_scale, down_gain)),
+        [SMEM] + [VMEM] * 2 + [HBM] * 8,
         [((band, 4 * channels), BF16), ((count, hidden), F32), ((count, channels), F32),
          ((count, LANES), F32), ((count, channels), F32), ((count, LANES), F32)],
-        [pltpu.VMEM((channels // LANES, rows + 2 * HALF, width + 2 * LEFT, LANES), F32),
-         pltpu.VMEM((count, channels), F32), pltpu.VMEM((count, channels), BF16),
-         pltpu.VMEM((count, channels), F32), pltpu.VMEM((channels // LANES, count, LANES), F32)] + weights,
+        [pltpu.VMEM((lanes, rows, width, LANES), BF16)] + [pltpu.VMEM(dw_kernel.shape, F32)]
+        + [vector] * 4
+        + [pltpu.VMEM((lanes, rows + 2 * HALF, width + 2 * LEFT, LANES), F32),
+           pltpu.VMEM((count, channels), F32), pltpu.VMEM((count, channels), BF16),
+           pltpu.VMEM((count, channels), F32), pltpu.VMEM((lanes, count, LANES), F32),
+           pltpu.SemaphoreType.DMA((5,)), pltpu.SemaphoreType.DMA((lanes,))] + weights,
         20, 4 * count * channels * hidden, 9e6,
     )
     held = [patches] + [send(patches, onward(j)) for j in range(1, chips)]
-    keep, give, pick = call(
+    keep, give, pick, w_near = call(
         lambda *refs: pull_body(spaces, owners, capacity, step, *refs),
-        (place, owner_table.reshape(1, tokens), returned, w_down),
-        [SMEM, VMEM, VMEM, HBM],
-        [((chips, band, deep), BF16), ((chips, band, deep), BF16), ((slots, tokens), BF16)],
-        [pltpu.VMEM((spaces, band, narrow), BF16), pltpu.VMEM((tokens, narrow), BF16)] + down,
+        (place, *close(returned), *far_off(owner_table.reshape(1, tokens), w_down)),
+        [SMEM, VMEM, HBM, HBM],
+        [((chips, band, deep), BF16), ((chips, band, deep), BF16), ((slots, tokens), BF16),
+         (w_down.shape, BF16)],
+        [pltpu.VMEM((1, tokens), jnp.int32),
+         pltpu.VMEM((spaces, band, narrow), BF16), pltpu.VMEM((tokens, narrow), BF16),
+         pltpu.SemaphoreType.DMA((1,)), pltpu.SemaphoreType.DMA((deep // step,))],
         12, 2 * tokens * deep * narrow, 4e6,
     )
     sent = send(give, swap)
     sums = call(
         lambda *refs: add_body(chips, *refs),
-        (place, keep, sent), [SMEM, VMEM, VMEM],
+        (place, *close(keep, sent)), [SMEM, VMEM, VMEM],
         [((band, deep), BF16)] * (chips - 1), [], 4, 2e6, 1e6,
     )
     across = [send(sums[j - 1], onward(j)) for j in range(1, chips)]
@@ -342,22 +386,24 @@
     for piece in held:
         pieces += [piece, send(piece, swap)]
     (buffer,) = call(
-        lambda *refs: push_body(chips, step, *refs),
-        (place, *pieces, pick, w_down),
-        [SMEM] + [VMEM] * (len(pieces) + 1) + [HBM],
+        lambda *refs: push_body(chips, *refs),
+        (place, *close(*pieces, pick, w_near)),
+        [SMEM] + [VMEM] * (len(pieces) + 2),
         [((slots, narrow), BF16)],
-        [pltpu.VMEM((tokens, deep), BF16), pltpu.VMEM((spaces, band, narrow), BF16)] + down,
+        [pltpu.VMEM((tokens, deep), BF16), pltpu.VMEM((spaces, band, narrow), BF16)],
         12, 2 * tokens * deep * narrow, 4e6,
     )
     arrived = trade(buffer)
     (grad_mixed,) = call(
         lambda *refs: backward_body(rows, width, channels, hidden, block, chips, *refs),
-        (place, keep, sent, *across, slope, n1, inv1, n2, inv2, mix_gain, w_expand, w_reduce,
-         layer_scale, down_gain),
-        [SMEM] + [VMEM] * (7 + chips) + [HBM] * 2 + [VMEM] * 2,
-        [(section_three.shape, BF16)],
-        [pltpu.VMEM((channels // LANES, count, LANES), F32), pltpu.VMEM((count, channels), BF16),
-         pltpu.VMEM((count, channels), F32)] + weights,
+        (place, *close(keep, sent, *across, slope, n1, inv1, n2, inv2),
+         *far_off(mix_gain, w_expand, w_reduce, layer_scale, down_gain)),
+        [SMEM] + [VMEM] * (6 + chips) + [HBM] * 5,
+        [jax.ShapeDtypeStruct(section_three.shape, BF16)],
+        [vector] * 3
+        + [pltpu.VMEM(section_three.shape, BF16), pltpu.VMEM((lanes, count, LANES), F32),
+           pltpu.VMEM((count, channels), BF16), pltpu.VMEM((count, channels), F32),
+           pltpu.SemaphoreType.DMA((3,)), pltpu.SemaphoreType.DMA((rows,))] + weights,
         16, 4 * count * channels * hidden, 9e6,
     )
     return arrived[None], grad_mixed

time: 62.6 us -> 46.4 us (0.74)
  local copies, waits for them, and re-layouts: 16.7 us -> 0.64 us
  waiting for transfers between devices: 12 us -> 13.1 us
    unnamed x51 -> x1, local copies, waits for them, and re-layouts: 16.7 us -> 0.64 us
    ppermute x7, waiting for transfers between devices: 5.61 us -> 6.65 us  [send(): return lax.ppermute(value, 'space', pairs)]
    all_to_all x2, starting transfers between devices: 11.4 us -> 10.7 us  [trade(): return lax.all_to_all(value, 'dp', split_axis=0, concat_axis=0, tiled=True)]
  transfers between devices with their start and end apart: 9 -> 9, of which waited for: 2 -> 3; matrix products, arithmetic and copies ran while one was open for 0% -> 0% of each run, Pallas kernels for 27% -> 37%
where the time goes in v3:
time: 46.4 us; the launch traced here: 46 us
  Pallas kernels  16.8 us (36%)
  starting transfers between devices  14.8 us (32%)
  waiting for transfers between devices  13.1 us (28%)
  between operations  0.72 us (2%)
  local copies, waits for them, and re-layouts  0.64 us (1%)
    pallas_call x5, Pallas kernels, call(): pl.pallas_call(body, in_specs=specs, out_shape=tuple((o if isinstance(o,...  16.8 us
    all_to_all x2, starting transfers between devices, trade(): return lax.all_to_all(value, 'dp', split_axis=0, concat_axis=0, tiled=True)  10.7 us
    ppermute x7, waiting for transfers between devices, send(): return lax.ppermute(value, 'space', pairs)  6.65 us
    all_to_all x2, waiting for transfers between devices, trade(): return lax.all_to_all(value, 'dp', split_axis=0, concat_axis=0, tiled=True)  6.43 us
    ppermute x7, starting transfers between devices, send(): return lax.ppermute(value, 'space', pairs)  4.07 us
  transfers between devices with their start and end apart: 9, of which 3 were waited for; matrix products, arithmetic and copies ran while one was open for 0% of the time, Pallas kernels for 37%

profile of v3, /device:TPU:0, one launch (start us, length us, event | category | flops | bytes accessed | tf_op | source)
XLA Modules:
  0.0 46.0 jit_solution(17775642189763103335)
XLA Ops:
  0.6 7.3 %all-to-all-start = ((bf16[8,16,384]{2,1,0:T(8,128)(2,1)}), bf16[8,16,384]{2,1,0:T(8,128)(2,1)S(1)}, u32[]{:S(2)}, u32[]{:S(2)}) async-start(bf16[8,16,384]{2,1,0:T(8,128)(2,1)} %bitcast.8), calls=%async_computation | async-start | bytes 196608 | tf_op jit(solution)/shard_map/all_to_all | solution.py:340
  8.0 0.0 collective-permute-start
  8.0 0.7 %collective-permute-start.1 = (bf16[1,4,32,768]{3,2,1,0:T(8,128)(2,1)}, bf16[1,4,32,768]{3,2,1,0:T(8,128)(2,1)S(1)}, u32[]{:S(2)}, u32[]{:S(2)}) collective-permute-start(bf16[1,4,32,768]{3,2,1,0:T(8,128)(2,1)} %refs_3_.2), channel_id=1, source_target_pairs={{1,2},{2,1},{5,6},{6,5},{9,10},{10,9},{13,14},{14,13},{17,18},{18,... | collective-permute-start | bytes 589832 | tf_op jit(solution)/shard_map/ppermute | solution.py:337
  8.6 6.4 %all-to-all-done = bf16[8,16,384]{2,1,0:T(8,128)(2,1)S(1)} async-done(((bf16[8,16,384]{2,1,0:T(8,128)(2,1)}), bf16[8,16,384]{2,1,0:T(8,128)(2,1)S(1)}, u32[]{:S(2)}, u32[]{:S(2)}) %all-to-all-start) | async-done | bytes 98336 | tf_op jit(solution)/shard_map/all_to_all | solution.py:340
  15.1 3.1 %shard_map.123 = (bf16[2,32,3072]{2,1,0:T(8,128)(2,1)S(1)}, bf16[2,32,3072]{2,1,0:T(8,128)(2,1)S(1)}, bf16[128,128]{1,0:T(8,128)(2,1)S(1)}, bf16[3072,384]{1,0:T(8,128)(2,1)S(1)}) custom-call(s32[1]{0:T(128)} %bitcast.refs_0_, bf16[128,384]{1,0:T(8,128)(2,1)S(1)} %bitcast.6, s32[1,128]{1,0:T(1,128)} %bitcast.9, bf16[3072,384]{1,0:T(8,128)(2,1)} %refs_3_.3), custom_call_target="tpu_custom_call" | custom-call | flops 301989888 | bytes 4000000 | tf_op jit(solution)/shard_map/pallas_call | solution.py:39
  18.2 0.1 collective-permute-start.5
  18.2 0.0 collective-permute-done.refs_1_
  18.3 0.0 collective-permute-done.1.refs_2_
  18.3 6.0 %shard_map.122 = (bf16[32,3072]{1,0:T(8,128)(2,1)S(1)}, f32[128,1536]{1,0:T(8,128)S(1)}, f32[128,768]{1,0:T(8,128)S(1)}, f32[128,128]{1,0:T(8,128)S(1)}, f32[128,768]{1,0:T(8,128)S(1)}, /*index=5*/f32[128,128]{1,0:T(8,128)S(1)}) custom-call(s32[1]{0:T(128)} %bitcast.refs_0_, bf16[1,4,32,768]{3,2,1,0:T(8,128)(2,1)S(1)} %collective-permute-done.refs_1_, ...), custom_call_target="tpu_custom_call" | custom-call | flops 603979776 | bytes 9000000 | tf_op jit(solution)/shard_map/pallas_call | solution.py:39
  24.3 1.6 %collective-permute-start.3 = (bf16[32,3072]{1,0:T(8,128)(2,1)S(1)}, bf16[32,3072]{1,0:T(8,128)(2,1)S(1)}, u32[]{:S(2)}, u32[]{:S(2)}) collective-permute-start(bf16[32,3072]{1,0:T(8,128)(2,1)S(1)} %get-tuple-element.12.refs_1_), channel_id=1, source_target_pairs={{0,2},{1,3},{2,0},{3,1},{4,6},{5,7},{6,4},{7,5},{8,10},{9,11},{10,... | collective-permute-start | bytes 589832 | tf_op jit(solution)/shard_map/ppermute | solution.py:337
  25.9 0.2 collective-permute-start.2
  26.1 5.6 %collective-permute-done.3.refs_3_ = bf16[32,3072]{1,0:T(8,128)(2,1)S(1)} collective-permute-done((bf16[32,3072]{1,0:T(8,128)(2,1)S(1)}, bf16[32,3072]{1,0:T(8,128)(2,1)S(1)}, u32[]{:S(2)}, u32[]{:S(2)}) %collective-permute-start.3) | collective-permute-done | bytes 196640 | tf_op jit(solution)/shard_map/ppermute | solution.py:337
  31.7 0.0 collective-permute-start.4
  31.7 0.0 collective-permute-done.5.refs_2_
  31.7 1.6 %collective-permute-start.6 = (bf16[32,3072]{1,0:T(8,128)(2,1)S(1)}, bf16[32,3072]{1,0:T(8,128)(2,1)S(1)}, u32[]{:S(2)}, u32[]{:S(2)}) collective-permute-start(bf16[32,3072]{1,0:T(8,128)(2,1)S(1)} %shard_map.125), channel_id=1, source_target_pairs={{0,2},{1,3},{2,0},{3,1},{4,6},{5,7},{6,4},{7,5},{8,10},{9,11},{10,... | collective-permute-start | bytes 589832 | tf_op jit(solution)/shard_map/ppermute | solution.py:337
  33.3 0.0 collective-permute-done.2.refs_2_
  33.3 0.0 collective-permute-done.4.refs_4_
  33.3 1.4 %shard_map.124 = bf16[128,384]{1,0:T(8,128)(2,1)} custom-call(s32[1]{0:T(128)} %bitcast.refs_0_, bf16[32,3072]{1,0:T(8,128)(2,1)S(1)} %get-tuple-element.12.refs_1_, bf16[32,3072]{1,0:T(8,128)(2,1)S(1)} %collective-permute-done.2.refs_2_, bf16[32,3072]{1,0:T(8,128)(2,1)S(1)} %collective-permute-done.3.refs_3_, ...), custom_call_target="tpu_custom_call" | custom-call | flops 301989888 | bytes 4000000 | tf_op jit(solution)/shard_map/pallas_call | solution.py:39
  34.7 3.4 %all-to-all-start.1 = ((bf16[8,16,384]{2,1,0:T(8,128)(2,1)}), bf16[8,16,384]{2,1,0:T(8,128)(2,1)S(1)}, u32[]{:S(2)}, u32[]{:S(2)}) async-start(bf16[8,16,384]{2,1,0:T(8,128)(2,1)} %bitcast.4), calls=%async_computation.1 | async-start | bytes 196608 | tf_op jit(solution)/shard_map/all_to_all | solution.py:340
  38.0 1.1 %collective-permute-done.6.refs_3_ = bf16[32,3072]{1,0:T(8,128)(2,1)S(1)} collective-permute-done((bf16[32,3072]{1,0:T(8,128)(2,1)S(1)}, bf16[32,3072]{1,0:T(8,128)(2,1)S(1)}, u32[]{:S(2)}, u32[]{:S(2)}) %collective-permute-start.6) | collective-permute-done | bytes 196640 | tf_op jit(solution)/shard_map/ppermute | solution.py:337
  39.1 6.3 %shard_map.126 = bf16[1,4,32,768]{3,2,1,0:T(8,128)(2,1)} custom-call(s32[1]{0:T(128)} %bitcast.refs_0_, bf16[2,32,3072]{2,1,0:T(8,128)(2,1)S(1)} %get-tuple-element.15.refs_1_, bf16[2,32,3072]{2,1,0:T(8,128)(2,1)S(1)} %collective-permute-done.5.refs_2_, bf16[32,3072]{1,0:T(8,128)(2,1)S(1)} %collective-permute-done.6.refs_3_, ...), custom_call_target="tpu_custom_call" | custom-call | flops 603979776 | bytes 9000000 | tf_op jit(solution)/shard_map/pallas_call | solution.py:39
  45.4 0.0 all-to-all-done.1
  45.4 0.6 %copy.14 = bf16[1,128,384]{2,1,0:T(8,128)(2,1)} copy(bf16[1,128,384]{2,1,0:T(8,128)(2,1)S(1)} %bitcast.7) | data formatting | bytes 196608
  (1 shorter events, 0.0 us)
Async XLA Ops:
  0.6 14.4 %all-to-all-start = ((bf16[8,16,384]{2,1,0:T(8,128)(2,1)}), bf16[8,16,384]{2,1,0:T(8,128)(2,1)S(1)}, u32[]{:S(2)}, u32[]{:S(2)}) async-start(bf16[8,16,384]{2,1,0:T(8,128)(2,1)} %bitcast.8), calls=%async_computation | async-start | bytes 196608 | tf_op jit(solution)/shard_map/all_to_all | solution.py:340
  8.0 10.3 %collective-permute-start = (bf16[1,4,32,768]{3,2,1,0:T(8,128)(2,1)}, bf16[1,4,32,768]{3,2,1,0:T(8,128)(2,1)S(1)}, u32[]{:S(2)}, u32[]{:S(2)}) collective-permute-start(bf16[1,4,32,768]{3,2,1,0:T(8,128)(2,1)} %refs_3_.2), channel_id=1, source_target_pairs={{0,1},{1,0},{2,3},{3,2},{4,5},{5,4},{6,7},{7,6},{8,9},{9,8},{10,11... | collective-permute-start | bytes 589832 | tf_op jit(solution)/shard_map/ppermute | solution.py:337
  8.0 10.3 %collective-permute-start.1 = (bf16[1,4,32,768]{3,2,1,0:T(8,128)(2,1)}, bf16[1,4,32,768]{3,2,1,0:T(8,128)(2,1)S(1)}, u32[]{:S(2)}, u32[]{:S(2)}) collective-permute-start(bf16[1,4,32,768]{3,2,1,0:T(8,128)(2,1)} %refs_3_.2), channel_id=1, source_target_pairs={{1,2},{2,1},{5,6},{6,5},{9,10},{10,9},{13,14},{14,13},{17,18},{18,... | collective-permute-start | bytes 589832 | tf_op jit(solution)/shard_map/ppermute | solution.py:337
  18.2 13.5 %collective-permute-start.5 = (bf16[2,32,3072]{2,1,0:T(8,128)(2,1)S(1)}, bf16[2,32,3072]{2,1,0:T(8,128)(2,1)S(1)}, u32[]{:S(2)}, u32[]{:S(2)}) collective-permute-start(bf16[2,32,3072]{2,1,0:T(8,128)(2,1)S(1)} %get-tuple-element.16), channel_id=1, source_target_pairs={{0,1},{1,0},{2,3},{3,2},{4,5},{5,4},{6,7},{7,6},{8,9},{9,8},{10,11... | collective-permute-start | bytes 1179656 | tf_op jit(solution)/shard_map/ppermute | solution.py:337
  24.3 7.3 %collective-permute-start.3 = (bf16[32,3072]{1,0:T(8,128)(2,1)S(1)}, bf16[32,3072]{1,0:T(8,128)(2,1)S(1)}, u32[]{:S(2)}, u32[]{:S(2)}) collective-permute-start(bf16[32,3072]{1,0:T(8,128)(2,1)S(1)} %get-tuple-element.12.refs_1_), channel_id=1, source_target_pairs={{0,2},{1,3},{2,0},{3,1},{4,6},{5,7},{6,4},{7,5},{8,10},{9,11},{10,... | collective-permute-start | bytes 589832 | tf_op jit(solution)/shard_map/ppermute | solution.py:337
  25.9 7.4 %collective-permute-start.2 = (bf16[32,3072]{1,0:T(8,128)(2,1)S(1)}, bf16[32,3072]{1,0:T(8,128)(2,1)S(1)}, u32[]{:S(2)}, u32[]{:S(2)}) collective-permute-start(bf16[32,3072]{1,0:T(8,128)(2,1)S(1)} %get-tuple-element.12.refs_1_), channel_id=1, source_target_pairs={{0,1},{1,0},{2,3},{3,2},{4,5},{5,4},{6,7},{7,6},{8,9},{9,8},{10,11... | collective-permute-start | bytes 589832 | tf_op jit(solution)/shard_map/ppermute | solution.py:337
  31.7 1.6 %collective-permute-start.4 = (bf16[32,3072]{1,0:T(8,128)(2,1)S(1)}, bf16[32,3072]{1,0:T(8,128)(2,1)S(1)}, u32[]{:S(2)}, u32[]{:S(2)}) collective-permute-start(bf16[32,3072]{1,0:T(8,128)(2,1)S(1)} %collective-permute-done.3.refs_3_), channel_id=1, source_target_pairs={{0,1},{1,0},{2,3},{3,2},{4,5},{5,4},{6,7},{7,6},{8,9},{9,8},{10,11... | collective-permute-start | bytes 589832 | tf_op jit(solution)/shard_map/ppermute | solution.py:337
  31.7 7.4 %collective-permute-start.6 = (bf16[32,3072]{1,0:T(8,128)(2,1)S(1)}, bf16[32,3072]{1,0:T(8,128)(2,1)S(1)}, u32[]{:S(2)}, u32[]{:S(2)}) collective-permute-start(bf16[32,3072]{1,0:T(8,128)(2,1)S(1)} %shard_map.125), channel_id=1, source_target_pairs={{0,2},{1,3},{2,0},{3,1},{4,6},{5,7},{6,4},{7,5},{8,10},{9,11},{10,... | collective-permute-start | bytes 589832 | tf_op jit(solution)/shard_map/ppermute | solution.py:337
  34.7 10.7 %all-to-all-start.1 = ((bf16[8,16,384]{2,1,0:T(8,128)(2,1)}), bf16[8,16,384]{2,1,0:T(8,128)(2,1)S(1)}, u32[]{:S(2)}, u32[]{:S(2)}) async-start(bf16[8,16,384]{2,1,0:T(8,128)(2,1)} %bitcast.4), calls=%async_computation.1 | async-start | bytes 196608 | tf_op jit(solution)/shard_map/all_to_all | solution.py:340

commit v4 on v3

--- a/solution.py
+++ b/solution.py
@@ -72,19 +72,10 @@
     )
 
 
-def fetch(hidden, block, w1_hbm, w1_ref, w2_hbm, w2_ref, sems):
-    loads = []
-    for i, b in enumerate(range(0, hidden, block)):
-        cols, lines = (slice(None), pl.ds(b, block)), pl.ds(b, block)
-        loads.append(
-            (
-                pltpu.make_async_copy(w1_hbm.at[cols], w1_ref.at[cols], sems.at[0, i]),
-                pltpu.make_async_copy(w2_hbm.at[lines], w2_ref.at[lines], sems.at[1, i]),
-            )
-        )
-        loads[-1][0].start()
-        loads[-1][1].start()
-    return loads
+def fetch(pairs, sems):
+    copies = [pltpu.make_async_copy(src, dst, sems.at[i]) for i, (src, dst) in enumerate(pairs)]
+    start(copies)
+    return copies
 
 
 def forward_body(
@@ -93,7 +84,7 @@
     scale_hbm, down_gain_hbm,
     patch_ref, slope_ref, n1_ref, inv1_ref, n2_ref, inv2_ref,
     x_ref, kernel_ref, bias_ref, gain_ref, scale_ref, down_gain_ref,
-    padded, mixed, first, acc, grid, small_sems, band_sems, w1_ref, w2_ref, sems,
+    padded, mixed, first, active, acc, grid, small_sems, band_sems, w1_ref, w2_ref, sems,
 ):
     odd = place[0] % 2 == 1
     chunks = channels // LANES
@@ -110,7 +101,7 @@
     for c in range(chunks):
         start(bands(c))
     start(small[2:])
-    loads = fetch(hidden, block, w1_hbm, w1_ref, w2_hbm, w2_ref, sems)
+    loads = fetch(((w1_hbm, w1_ref), (w2_hbm, w2_ref)), sems)
     padded[:, :, 0:LEFT, :] = jnp.zeros((chunks, tall, LEFT, LANES), F32)
     padded[:, :, LEFT + width :, :] = jnp.zeros((chunks, tall, LEFT, LANES), F32)
     wait(small[:2])
@@ -145,18 +136,16 @@
         n1_ref[r : r + step, :] = n1
         inv1_ref[r : r + step, :] = jnp.broadcast_to(inv1, (step, LANES))
         first[r : r + step, :] = (n1 * gain_ref[...].reshape(1, channels)).astype(BF16)
-    for i, b in enumerate(range(0, hidden, block)):
-        loads[i][0].wait()
-        loads[i][1].wait()
+    loads[0].wait()
+    for b in range(0, hidden, block):
         pre = nn(first[...], w1_ref[:, b : b + block])
         cumulative = 0.5 * (1.0 + lax.erf(pre * 0.7071067811865476))
         density = jnp.exp(-0.5 * pre * pre) * 0.3989422804014327
         slope_ref[:, b : b + block] = cumulative + pre * density
-        term = nn((pre * cumulative).astype(BF16), w2_ref[b : b + block, :])
-        if b == 0:
-            acc[...] = term
-        else:
-            acc[...] += term
+        active[:, b : b + block] = (pre * cumulative).astype(BF16)
+    loads[1].wait()
+    for b in range(0, channels, block):
+        acc[:, b : b + block] = nn(active[...], w2_ref[:, b : b + block])
     for r in range(rows):
         at = pl.ds(r * width, width)
         line = jnp.concatenate([x_ref[c, r] for c in range(chunks)], axis=1)
@@ -245,13 +234,13 @@
     far = rest[: chips - 1]
     (
         slope_ref, n1_ref, inv1_ref, n2_ref, inv2_ref, gain_hbm, w1_hbm, w2_hbm, scale_hbm,
-        down_gain_hbm, out_hbm, gain_ref, scale_ref, down_gain_ref, out_ref, grid, scaled, acc,
+        down_gain_hbm, out_hbm, gain_ref, scale_ref, down_gain_ref, out_ref, grid, scaled, active, acc,
         small_sems, out_sems, w1_ref, w2_ref, sems,
     ) = rest[chips - 1 :]
     sources, targets = (down_gain_hbm, scale_hbm, gain_hbm), (down_gain_ref, scale_ref, gain_ref)
     small = [pltpu.make_async_copy(s, t, small_sems.at[i]) for i, (s, t) in enumerate(zip(sources, targets))]
     start(small)
-    loads = fetch(hidden, block, w1_hbm, w1_ref, w2_hbm, w2_ref, sems)
+    loads = fetch(((w2_hbm, w2_ref), (w1_hbm, w1_ref)), sems)
     chip = place[0] // 2
     half = width // 2
     chunks = channels // LANES
@@ -272,15 +261,12 @@
         grad = jnp.concatenate([grid[c, at, :] for c in range(chunks)], axis=1)
         back = norm_back(grad, n2_ref[at, :], inv2_ref[at, 0:1], down_gain_ref[...].reshape(1, channels))
         scaled[at, :] = (back * scale_ref[...].reshape(1, channels)).astype(BF16)
-    for i, b in enumerate(range(0, hidden, block)):
-        loads[i][0].wait()
-        loads[i][1].wait()
-        grad_pre = (nt(scaled[...], w2_ref[b : b + block, :]) * slope_ref[:, b : b + block]).astype(BF16)
-        term = nt(grad_pre, w1_ref[:, b : b + block])
-        if b == 0:
-            acc[...] = term
-        else:
-            acc[...] += term
+    loads[0].wait()
+    for b in range(0, hidden, block):
+        active[:, b : b + block] = (nt(scaled[...], w2_ref[b : b + block, :]) * slope_ref[:, b : b + block]).astype(BF16)
+    loads[1].wait()
+    for b in range(0, channels, block):
+        acc[:, b : b + block] = nt(active[...], w1_ref[b : b + block, :])
     stores = []
     for r in range(rows):
         at = pl.ds(r * width, width)
@@ -326,7 +312,7 @@
     block, step = 256, 768
     weights = [
         pltpu.VMEM(w_expand.shape, BF16), pltpu.VMEM(w_reduce.shape, BF16),
-        pltpu.SemaphoreType.DMA((2, hidden // block)),
+        pltpu.SemaphoreType.DMA((2,)),
     ]
 
     swap = [(i, i ^ 1) for i in range(spaces)]
@@ -359,7 +345,8 @@
         + [vector] * 4
         + [pltpu.VMEM((lanes, rows + 2 * HALF, width + 2 * LEFT, LANES), F32),
            pltpu.VMEM((count, channels), F32), pltpu.VMEM((count, channels), BF16),
-           pltpu.VMEM((count, channels), F32), pltpu.VMEM((lanes, count, LANES), F32),
+           pltpu.VMEM((count, hidden), BF16), pltpu.VMEM((count, channels), F32),
+           pltpu.VMEM((lanes, count, LANES), F32),
            pltpu.SemaphoreType.DMA((5,)), pltpu.SemaphoreType.DMA((lanes,))] + weights,
         20, 4 * count * channels * hidden, 9e6,
     )
@@ -402,8 +389,8 @@
         [jax.ShapeDtypeStruct(section_three.shape, BF16)],
         [vector] * 3
         + [pltpu.VMEM(section_three.shape, BF16), pltpu.VMEM((lanes, count, LANES), F32),
-           pltpu.VMEM((count, channels), BF16), pltpu.VMEM((count, channels), F32),
-           pltpu.SemaphoreType.DMA((3,)), pltpu.SemaphoreType.DMA((rows,))] + weights,
+           pltpu.VMEM((count, channels), BF16), pltpu.VMEM((count, hidden), BF16),
+           pltpu.VMEM((count, channels), F32), pltpu.SemaphoreType.DMA((3,)), pltpu.SemaphoreType.DMA((rows,))] + weights,
         16, 4 * count * channels * hidden, 9e6,
     )
     return arrived[None], grad_mixed
@@ -415,6 +402,4 @@
         P("dp", None, None), P("dp", None, "space"),
     )
     out_specs = (P("dp", None, "space"), P("dp", "space", None, None))
-    return jax.shard_map(
-        on_device, mesh=mesh, in_specs=in_specs, out_specs=out_specs, check_vma=False
-    )
+    return jax.shard_map(on_device, mesh=mesh, in_specs=in_specs, out_specs=out_specs, check_vma=False)

time: 46.4 us -> 44.2 us (0.953)
  Pallas kernels: 16.8 us -> 13.2 us
  waiting for transfers between devices: 13.1 us -> 14.5 us
    pallas_call x5, Pallas kernels: 16.8 us -> 13.2 us  [call(): pl.pallas_call(body, in_specs=specs, out_shape=tuple((o if isinstance(o,...]
    all_to_all x2, waiting for transfers between devices: 6.43 us -> 7.84 us  [trade(): return lax.all_to_all(value, 'dp', split_axis=0, concat_axis=0, tiled=True)]
  transfers between devices with their start and end apart: 9 -> 9, of which waited for: 3 -> 4; matrix products, arithmetic and copies ran while one was open for 0% -> 0% of each run, Pallas kernels for 37% -> 30%
where the time goes in v4:
time: 44.2 us; the launch traced here: 43.8 us
  starting transfers between devices  14.8 us (33%)
  waiting for transfers between devices  14.5 us (33%)
  Pallas kernels  13.2 us (30%)
  between operations  0.72 us (2%)
  local copies, waits for them, and re-layouts  0.64 us (1%)
    pallas_call x5, Pallas kernels, call(): pl.pallas_call(body, in_specs=specs, out_shape=tuple((o if isinstance(o,...  13.2 us
    all_to_all x2, starting transfers between devices, trade(): return lax.all_to_all(value, 'dp', split_axis=0, concat_axis=0, tiled=True)  10.7 us
    all_to_all x2, waiting for transfers between devices, trade(): return lax.all_to_all(value, 'dp', split_axis=0, concat_axis=0, tiled=True)  7.84 us
    ppermute x7, waiting for transfers between devices, send(): return lax.ppermute(value, 'space', pairs)  6.65 us
    ppermute x7, starting transfers between devices, send(): return lax.ppermute(value, 'space', pairs)  4.08 us
  transfers between devices with their start and end apart: 9, of which 4 were waited for; matrix products, arithmetic and copies ran while one was open for 0% of the time, Pallas kernels for 30%

profile of v4, /device:TPU:0, one launch (start us, length us, event | category | flops | bytes accessed | tf_op | source)
XLA Modules:
  0.0 43.8 jit_solution(5876872949254221985)
XLA Ops:
  0.6 7.3 %all-to-all-start = ((bf16[8,16,384]{2,1,0:T(8,128)(2,1)}), bf16[8,16,384]{2,1,0:T(8,128)(2,1)S(1)}, u32[]{:S(2)}, u32[]{:S(2)}) async-start(bf16[8,16,384]{2,1,0:T(8,128)(2,1)} %bitcast.8), calls=%async_computation | async-start | bytes 196608 | tf_op jit(solution)/shard_map/all_to_all | solution.py:326
  8.0 0.0 collective-permute-start
  8.0 0.7 %collective-permute-start.1 = (bf16[1,4,32,768]{3,2,1,0:T(8,128)(2,1)}, bf16[1,4,32,768]{3,2,1,0:T(8,128)(2,1)S(1)}, u32[]{:S(2)}, u32[]{:S(2)}) collective-permute-start(bf16[1,4,32,768]{3,2,1,0:T(8,128)(2,1)} %refs_3_.2), channel_id=1, source_target_pairs={{1,2},{2,1},{5,6},{6,5},{9,10},{10,9},{13,14},{14,13},{17,18},{18,... | collective-permute-start | bytes 589832 | tf_op jit(solution)/shard_map/ppermute | solution.py:323
  8.6 6.4 %all-to-all-done = bf16[8,16,384]{2,1,0:T(8,128)(2,1)S(1)} async-done(((bf16[8,16,384]{2,1,0:T(8,128)(2,1)}), bf16[8,16,384]{2,1,0:T(8,128)(2,1)S(1)}, u32[]{:S(2)}, u32[]{:S(2)}) %all-to-all-start) | async-done | bytes 98336 | tf_op jit(solution)/shard_map/all_to_all | solution.py:326
  15.1 3.1 %shard_map.123 = (bf16[2,32,3072]{2,1,0:T(8,128)(2,1)S(1)}, bf16[2,32,3072]{2,1,0:T(8,128)(2,1)S(1)}, bf16[128,128]{1,0:T(8,128)(2,1)S(1)}, bf16[3072,384]{1,0:T(8,128)(2,1)S(1)}) custom-call(s32[1]{0:T(128)} %bitcast.refs_0_, bf16[128,384]{1,0:T(8,128)(2,1)S(1)} %bitcast.6, s32[1,128]{1,0:T(1,128)} %bitcast.9, bf16[3072,384]{1,0:T(8,128)(2,1)} %refs_3_.3), custom_call_target="tpu_custom_call" | custom-call | flops 301989888 | bytes 4000000 | tf_op jit(solution)/shard_map/pallas_call | solution.py:39
  18.2 0.1 collective-permute-start.5
  18.2 0.0 collective-permute-done.refs_1_
  18.3 0.0 collective-permute-done.1.refs_2_
  18.3 4.1 %shard_map.122 = (bf16[32,3072]{1,0:T(8,128)(2,1)S(1)}, f32[128,1536]{1,0:T(8,128)S(1)}, f32[128,768]{1,0:T(8,128)S(1)}, f32[128,128]{1,0:T(8,128)S(1)}, f32[128,768]{1,0:T(8,128)S(1)}, /*index=5*/f32[128,128]{1,0:T(8,128)S(1)}) custom-call(s32[1]{0:T(128)} %bitcast.refs_0_, bf16[1,4,32,768]{3,2,1,0:T(8,128)(2,1)S(1)} %collective-permute-done.refs_1_, ...), custom_call_target="tpu_custom_call" | custom-call | flops 603979776 | bytes 9000000 | tf_op jit(solution)/shard_map/pallas_call | solution.py:39
  22.3 1.6 %collective-permute-start.3 = (bf16[32,3072]{1,0:T(8,128)(2,1)S(1)}, bf16[32,3072]{1,0:T(8,128)(2,1)S(1)}, u32[]{:S(2)}, u32[]{:S(2)}) collective-permute-start(bf16[32,3072]{1,0:T(8,128)(2,1)S(1)} %get-tuple-element.12.refs_1_), channel_id=1, source_target_pairs={{0,2},{1,3},{2,0},{3,1},{4,6},{5,7},{6,4},{7,5},{8,10},{9,11},{10,... | collective-permute-start | bytes 589832 | tf_op jit(solution)/shard_map/ppermute | solution.py:323
  23.9 0.2 collective-permute-start.2
  24.1 5.6 %collective-permute-done.3.refs_3_ = bf16[32,3072]{1,0:T(8,128)(2,1)S(1)} collective-permute-done((bf16[32,3072]{1,0:T(8,128)(2,1)S(1)}, bf16[32,3072]{1,0:T(8,128)(2,1)S(1)}, u32[]{:S(2)}, u32[]{:S(2)}) %collective-permute-start.3) | collective-permute-done | bytes 196640 | tf_op jit(solution)/shard_map/ppermute | solution.py:323
  29.7 0.0 collective-permute-start.4
  29.7 0.0 collective-permute-done.5.refs_2_
  29.7 1.6 %collective-permute-start.6 = (bf16[32,3072]{1,0:T(8,128)(2,1)S(1)}, bf16[32,3072]{1,0:T(8,128)(2,1)S(1)}, u32[]{:S(2)}, u32[]{:S(2)}) collective-permute-start(bf16[32,3072]{1,0:T(8,128)(2,1)S(1)} %shard_map.125), channel_id=1, source_target_pairs={{0,2},{1,3},{2,0},{3,1},{4,6},{5,7},{6,4},{7,5},{8,10},{9,11},{10,... | collective-permute-start | bytes 589832 | tf_op jit(solution)/shard_map/ppermute | solution.py:323
  31.3 0.0 collective-permute-done.2.refs_2_
  31.3 0.0 collective-permute-done.4.refs_4_
  31.3 1.4 %shard_map.124 = bf16[128,384]{1,0:T(8,128)(2,1)} custom-call(s32[1]{0:T(128)} %bitcast.refs_0_, bf16[32,3072]{1,0:T(8,128)(2,1)S(1)} %get-tuple-element.12.refs_1_, bf16[32,3072]{1,0:T(8,128)(2,1)S(1)} %collective-permute-done.2.refs_2_, bf16[32,3072]{1,0:T(8,128)(2,1)S(1)} %collective-permute-done.3.refs_3_, ...), custom_call_target="tpu_custom_call" | custom-call | flops 301989888 | bytes 4000000 | tf_op jit(solution)/shard_map/pallas_call | solution.py:39
  32.7 3.4 %all-to-all-start.1 = ((bf16[8,16,384]{2,1,0:T(8,128)(2,1)}), bf16[8,16,384]{2,1,0:T(8,128)(2,1)S(1)}, u32[]{:S(2)}, u32[]{:S(2)}) async-start(bf16[8,16,384]{2,1,0:T(8,128)(2,1)} %bitcast.4), calls=%async_computation.1 | async-start | bytes 196608 | tf_op jit(solution)/shard_map/all_to_all | solution.py:326
  36.1 1.0 %collective-permute-done.6.refs_3_ = bf16[32,3072]{1,0:T(8,128)(2,1)S(1)} collective-permute-done((bf16[32,3072]{1,0:T(8,128)(2,1)S(1)}, bf16[32,3072]{1,0:T(8,128)(2,1)S(1)}, u32[]{:S(2)}, u32[]{:S(2)}) %collective-permute-start.6) | collective-permute-done | bytes 196640 | tf_op jit(solution)/shard_map/ppermute | solution.py:323
  37.1 4.6 %shard_map.126 = bf16[1,4,32,768]{3,2,1,0:T(8,128)(2,1)} custom-call(s32[1]{0:T(128)} %bitcast.refs_0_, bf16[2,32,3072]{2,1,0:T(8,128)(2,1)S(1)} %get-tuple-element.15.refs_1_, bf16[2,32,3072]{2,1,0:T(8,128)(2,1)S(1)} %collective-permute-done.5.refs_2_, bf16[32,3072]{1,0:T(8,128)(2,1)S(1)} %collective-permute-done.6.refs_3_, ...), custom_call_target="tpu_custom_call" | custom-call | flops 603979776 | bytes 9000000 | tf_op jit(solution)/shard_map/pallas_call | solution.py:39
  41.8 1.4 %all-to-all-done.1 = bf16[8,16,384]{2,1,0:T(8,128)(2,1)S(1)} async-done(((bf16[8,16,384]{2,1,0:T(8,128)(2,1)}), bf16[8,16,384]{2,1,0:T(8,128)(2,1)S(1)}, u32[]{:S(2)}, u32[]{:S(2)}) %all-to-all-start.1) | async-done | bytes 98336 | tf_op jit(solution)/shard_map/all_to_all | solution.py:326
  43.2 0.6 %copy.14 = bf16[1,128,384]{2,1,0:T(8,128)(2,1)} copy(bf16[1,128,384]{2,1,0:T(8,128)(2,1)S(1)} %bitcast.7) | data formatting | bytes 196608
  (1 shorter events, 0.0 us)
Async XLA Ops:
  0.6 14.4 %all-to-all-start = ((bf16[8,16,384]{2,1,0:T(8,128)(2,1)}), bf16[8,16,384]{2,1,0:T(8,128)(2,1)S(1)}, u32[]{:S(2)}, u32[]{:S(2)}) async-start(bf16[8,16,384]{2,1,0:T(8,128)(2,1)} %bitcast.8), calls=%async_computation | async-start | bytes 196608 | tf_op jit(solution)/shard_map/all_to_all | solution.py:326
  8.0 10.3 %collective-permute-start = (bf16[1,4,32,768]{3,2,1,0:T(8,128)(2,1)}, bf16[1,4,32,768]{3,2,1,0:T(8,128)(2,1)S(1)}, u32[]{:S(2)}, u32[]{:S(2)}) collective-permute-start(bf16[1,4,32,768]{3,2,1,0:T(8,128)(2,1)} %refs_3_.2), channel_id=1, source_target_pairs={{0,1},{1,0},{2,3},{3,2},{4,5},{5,4},{6,7},{7,6},{8,9},{9,8},{10,11... | collective-permute-start | bytes 589832 | tf_op jit(solution)/shard_map/ppermute | solution.py:323
  8.0 10.3 %collective-permute-start.1 = (bf16[1,4,32,768]{3,2,1,0:T(8,128)(2,1)}, bf16[1,4,32,768]{3,2,1,0:T(8,128)(2,1)S(1)}, u32[]{:S(2)}, u32[]{:S(2)}) collective-permute-start(bf16[1,4,32,768]{3,2,1,0:T(8,128)(2,1)} %refs_3_.2), channel_id=1, source_target_pairs={{1,2},{2,1},{5,6},{6,5},{9,10},{10,9},{13,14},{14,13},{17,18},{18,... | collective-permute-start | bytes 589832 | tf_op jit(solution)/shard_map/ppermute | solution.py:323
  18.2 11.5 %collective-permute-start.5 = (bf16[2,32,3072]{2,1,0:T(8,128)(2,1)S(1)}, bf16[2,32,3072]{2,1,0:T(8,128)(2,1)S(1)}, u32[]{:S(2)}, u32[]{:S(2)}) collective-permute-start(bf16[2,32,3072]{2,1,0:T(8,128)(2,1)S(1)} %get-tuple-element.16), channel_id=1, source_target_pairs={{0,1},{1,0},{2,3},{3,2},{4,5},{5,4},{6,7},{7,6},{8,9},{9,8},{10,11... | collective-permute-start | bytes 1179656 | tf_op jit(solution)/shard_map/ppermute | solution.py:323
  22.3 7.4 %collective-permute-start.3 = (bf16[32,3072]{1,0:T(8,128)(2,1)S(1)}, bf16[32,3072]{1,0:T(8,128)(2,1)S(1)}, u32[]{:S(2)}, u32[]{:S(2)}) collective-permute-start(bf16[32,3072]{1,0:T(8,128)(2,1)S(1)} %get-tuple-element.12.refs_1_), channel_id=1, source_target_pairs={{0,2},{1,3},{2,0},{3,1},{4,6},{5,7},{6,4},{7,5},{8,10},{9,11},{10,... | collective-permute-start | bytes 589832 | tf_op jit(solution)/shard_map/ppermute | solution.py:323
  23.9 7.4 %collective-permute-start.2 = (bf16[32,3072]{1,0:T(8,128)(2,1)S(1)}, bf16[32,3072]{1,0:T(8,128)(2,1)S(1)}, u32[]{:S(2)}, u32[]{:S(2)}) collective-permute-start(bf16[32,3072]{1,0:T(8,128)(2,1)S(1)} %get-tuple-element.12.refs_1_), channel_id=1, source_target_pairs={{0,1},{1,0},{2,3},{3,2},{4,5},{5,4},{6,7},{7,6},{8,9},{9,8},{10,11... | collective-permute-start | bytes 589832 | tf_op jit(solution)/shard_map/ppermute | solution.py:323
  29.7 1.6 %collective-permute-start.4 = (bf16[32,3072]{1,0:T(8,128)(2,1)S(1)}, bf16[32,3072]{1,0:T(8,128)(2,1)S(1)}, u32[]{:S(2)}, u32[]{:S(2)}) collective-permute-start(bf16[32,3072]{1,0:T(8,128)(2,1)S(1)} %collective-permute-done.3.refs_3_), channel_id=1, source_target_pairs={{0,1},{1,0},{2,3},{3,2},{4,5},{5,4},{6,7},{7,6},{8,9},{9,8},{10,11... | collective-permute-start | bytes 589832 | tf_op jit(solution)/shard_map/ppermute | solution.py:323
  29.7 7.4 %collective-permute-start.6 = (bf16[32,3072]{1,0:T(8,128)(2,1)S(1)}, bf16[32,3072]{1,0:T(8,128)(2,1)S(1)}, u32[]{:S(2)}, u32[]{:S(2)}) collective-permute-start(bf16[32,3072]{1,0:T(8,128)(2,1)S(1)} %shard_map.125), channel_id=1, source_target_pairs={{0,2},{1,3},{2,0},{3,1},{4,6},{5,7},{6,4},{7,5},{8,10},{9,11},{10,... | collective-permute-start | bytes 589832 | tf_op jit(solution)/shard_map/ppermute | solution.py:323
  32.7 10.5 %all-to-all-start.1 = ((bf16[8,16,384]{2,1,0:T(8,128)(2,1)}), bf16[8,16,384]{2,1,0:T(8,128)(2,1)S(1)}, u32[]{:S(2)}, u32[]{:S(2)}) async-start(bf16[8,16,384]{2,1,0:T(8,128)(2,1)} %bitcast.4), calls=%async_computation.1 | async-start | bytes 196608 | tf_op jit(solution)/shard_map/all_to_all | solution.py:326

commit v5 on v4

v5 whole, which is shorter than its diff:
```python
import jax
import jax.numpy as jnp
from jax import lax
from jax.experimental import pallas as pl
from jax.experimental.pallas import tpu as pltpu
from jax.sharding import PartitionSpec as P


KS = 7
HALF = KS // 2
LANES = 128
LEFT = 8
F32 = jnp.float32
BF16 = jnp.bfloat16
VMEM = pl.BlockSpec(memory_space=pltpu.VMEM)
SMEM = pl.BlockSpec(memory_space=pltpu.SMEM)
HBM = pl.BlockSpec(memory_space=pltpu.HBM)


def far_off(*values):
    return tuple(pltpu.with_memory_space_constraint(v, pltpu.HBM) for v in values)


def close(*values):
    return tuple(pltpu.with_memory_space_constraint(v, pltpu.VMEM) for v in values)


def start(copies):
    for copy in copies:
        copy.start()


def wait(copies):
    for copy in copies:
        copy.wait()


def call(body, ins, specs, outs, scratch, limit_mib, flops, moved):
    return pl.pallas_call(
        body,
        in_specs=specs,
        out_shape=tuple(pltpu.VMEM(*o) if isinstance(o, tuple) else o for o in outs),
        out_specs=tuple(VMEM if isinstance(o, tuple) else HBM for o in outs),
        scratch_shapes=scratch,
        compiler_params=pltpu.CompilerParams(vmem_limit_bytes=limit_mib << 20),
        cost_estimate=pl.CostEstimate(
            flops=int(flops), bytes_accessed=int(moved), transcendentals=0
        ),
    )(*ins)


def nt(a, b):
    return lax.dot_general(a, b, (((1,), (1,)), ((), ())), preferred_element_type=F32)


def nn(a, b):
    return jnp.dot(a, b, preferred_element_type=F32)


def normalize(values):
    center = values - jnp.mean(values, axis=-1, keepdims=True)
    inv_std = lax.rsqrt(jnp.mean(center * center, axis=-1, keepdims=True) + 1e-06)
    return center * inv_std, inv_std


def norm_back(grad, normed, inv_std, gain):
    scaled = grad * gain
    return inv_std * (
        scaled
        - jnp.mean(scaled, axis=-1, keepdims=True)
        - normed * jnp.mean(scaled * normed, axis=-1, keepdims=True)
    )


def fetch(pairs, sems):
    copies = [pltpu.make_async_copy(src, dst, sems.at[i]) for i, (src, dst) in enumerate(pairs)]
    start(copies)
    return copies


def prime_body(out_ref):
    out_ref[...] = jnp.zeros(out_ref.shape, F32)


def forward_body(
    rows, width, channels, hidden, block,
    place, near_ref, far_ref, kernel_ref, bias_ref, gain_ref, scale_ref, down_gain_ref,
    x_hbm, w1_hbm, w2_hbm,
    patch_ref, slope_ref, n1_ref, n2_ref, inv_ref,
    x_ref, padded, mixed, first, active, acc, grid, w1_ref, w2_ref, in_sems,
):
    odd = place[0] % 2 == 1
    chunks = channels // LANES
    tall = rows + 2 * HALF
    loads = fetch(((x_hbm, x_ref), (w1_hbm, w1_ref), (w2_hbm, w2_ref)), in_sems)
    padded[:, :, 0:LEFT, :] = jnp.zeros((chunks, tall, LEFT, LANES), F32)
    padded[:, :, LEFT + width :, :] = jnp.zeros((chunks, tall, LEFT, LANES), F32)
    cols = pl.ds(LEFT, width)
    own = range(HALF, HALF + rows)

    def convolve(c, at, lines, total):
        for dx in range(KS):
            taps = [kernel_ref[dy, dx : dx + 1, at] for dy in range(KS)]
            for r in lines:
                line = padded[c, r, pl.ds(LEFT - HALF + dx, width), :]
                for out in range(rows):
                    if 0 <= r - out < KS:
                        total[out] = total[out] + line * taps[r - out]
        for out in range(rows):
            mixed[pl.ds(out * width, width), at] = total[out]

    def outer(c, _):
        at = pl.ds(pl.multiple_of(c * LANES, LANES), LANES)
        near, far = near_ref[0, :, :, at].astype(F32), far_ref[0, :, :, at].astype(F32)
        above, below = jnp.where(odd, near, far), jnp.where(odd, far, near)
        padded[c, 0:HALF, cols, :] = above[rows - HALF :]
        padded[c, HALF + rows :, cols, :] = below[:HALF]
        bias = jnp.broadcast_to(bias_ref[at].reshape(1, LANES), (width, LANES))
        convolve(c, at, [r for r in range(tall) if r not in own], [bias for _ in range(rows)])
        return 0

    def inner(c, _):
        at = pl.ds(pl.multiple_of(c * LANES, LANES), LANES)
        padded[c, HALF : HALF + rows, cols, :] = x_ref[0, :, :, at].astype(F32)
        convolve(c, at, own, [mixed[pl.ds(out * width, width), at] for out in range(rows)])
        return 0

    lax.fori_loop(0, chunks, outer, 0)
    loads[0].wait()
    lax.fori_loop(0, chunks, inner, 0)
    count = rows * width
    gain = gain_ref[...].reshape(1, channels)
    for r in range(0, count, width):
        n1, inv1 = normalize(mixed[r : r + width, :])
        n1_ref[r : r + width, :] = n1.astype(BF16)
        inv_ref[r : r + width, 0:LANES] = jnp.broadcast_to(inv1, (width, LANES))
        first[r : r + width, :] = (n1 * gain).astype(BF16)
    loads[1].wait()
    for b in range(0, hidden, block):
        pre = nn(first[...], w1_ref[:, b : b + block])
        cumulative = 0.5 * (1.0 + lax.erf(pre * 0.7071067811865476))
        density = jnp.exp(-0.5 * pre * pre) * 0.3989422804014327
        slope_ref[:, b : b + block] = (cumulative + pre * density).astype(BF16)
        active[:, b : b + block] = (pre * cumulative).astype(BF16)
    loads[2].wait()
    for b in range(0, channels, block):
        acc[:, b : b + block] = nn(active[...], w2_ref[:, b : b + block])
    scale, gain = scale_ref[...].reshape(1, channels), down_gain_ref[...].reshape(1, channels)
    for r in range(rows):
        at = pl.ds(r * width, width)
        n2, inv2 = normalize(x_ref[0, r].astype(F32) + scale * acc[at, :])
        n2_ref[at, :] = n2.astype(BF16)
        inv_ref[at, LANES:] = jnp.broadcast_to(inv2, (width, LANES))
        second = n2 * gain
        for c in range(chunks):
            grid[c, at, :] = second[:, c * LANES : (c + 1) * LANES]
    half = width // 2
    for r in range(rows // 2):
        for a in range(2):
            for b in range(2):
                piece = jnp.concatenate(
                    [grid[c, pl.ds((2 * r + a) * width + b, half, stride=2), :] for c in range(chunks)],
                    axis=1,
                )
                patch_ref[r * half : (r + 1) * half, (2 * a + b) * channels : (2 * a + b + 1) * channels] = (
                    piece.astype(BF16)
                )


def index_body(owners, capacity, table_ref, pick_ref):
    targets = table_ref[...]
    slots, count = pick_ref.shape
    tall = max(owners, 16)
    hot = targets == lax.broadcasted_iota(jnp.int32, (tall, count), 0)
    sooner = lax.broadcasted_iota(jnp.int32, (count, count), 0) < lax.broadcasted_iota(
        jnp.int32, (count, count), 1
    )
    earlier = nn(jnp.where(hot, 1.0, 0.0).astype(BF16), jnp.where(sooner, 1.0, 0.0).astype(BF16))
    rank = jnp.sum(jnp.where(hot, earlier, 0.0), axis=0, keepdims=True).astype(jnp.int32)
    pick_ref[...] = jnp.where(
        targets * capacity + rank == lax.broadcasted_iota(jnp.int32, (slots, count), 0), 1.0, 0.0
    ).astype(BF16)


def pull_body(
    spaces, step,
    place, returned_ref, pick_ref, w_hbm, w2_hbm,
    keep_ref, send_ref, w_ref, w2_ref,
    wanted, both, sems,
):
    depth = w_ref.shape[0]
    low, high = pl.ds(0, depth // 2), pl.ds(depth // 2, depth // 2)
    loads = fetch(((w_hbm.at[low], w_ref.at[low]), (w_hbm.at[high], w_ref.at[high])), sems)
    late = pltpu.make_async_copy(w2_hbm.at[pl.ds(0, w2_ref.shape[0])], w2_ref, sems.at[2])
    core = place[0] % 2
    band = both.shape[0] // spaces
    wanted[...] = (
        lax.dot_general(pick_ref[...], returned_ref[...], (((0,), (0,)), ((), ())), preferred_element_type=F32)
        .astype(BF16)
        .reshape(wanted.shape)
    )
    chips = spaces // 2
    for i in range(chips):
        both[i * band : (i + 1) * band, :] = wanted[2 * i + core]
        both[(chips + i) * band : (chips + i + 1) * band, :] = wanted[2 * i + 1 - core]
    for d in range(0, depth, step):
        if d == 0:
            loads[0].wait()
            late.start()
        if d == depth // 2:
            loads[1].wait()
        part = nt(both[...], w_ref[d : d + step, :]).astype(BF16)
        for i in range(chips):
            keep_ref[i, :, d : d + step] = part[i * band : (i + 1) * band]
            send_ref[i, :, d : d + step] = part[(chips + i) * band : (chips + i + 1) * band]
    late.wait()


def add_body(chips, place, keep_ref, near_ref, mine_ref, *outs):
    chip = place[0] // 2
    mine_ref[...] = keep_ref[chip].astype(F32) + near_ref[chip].astype(F32)
    for j in range(1, chips):
        at = lax.rem(chip + j, chips)
        outs[j - 1][...] = (keep_ref[at].astype(F32) + near_ref[at].astype(F32)).astype(BF16)


def backward_body(rows, width, channels, hidden, block, chips, mine_ref, *rest):
    far = rest[: chips - 1]
    (
        slope_ref, n1_ref, n2_ref, inv_ref, w2_near, down_gain_ref, scale_ref, gain_ref, w1_hbm, w2_hbm,
        out_hbm, out_ref, grid, scaled, active, acc, w1_ref, w2_far, in_sems, out_sems,
    ) = rest[chips - 1 :]
    split = w2_near.shape[0]
    loads = fetch(((w2_hbm.at[pl.ds(split, split)], w2_far), (w1_hbm, w1_ref)), in_sems)
    half = width // 2
    chunks = channels // LANES
    for r in range(rows // 2):
        for a in range(2):
            for b in range(2):
                at = (pl.ds(r * half, half), pl.ds((2 * a + b) * channels, channels))
                value = mine_ref[at]
                for piece in far:
                    value = value + piece[at].astype(F32)
                for c in range(chunks):
                    grid[c, pl.ds((2 * r + a) * width + b, half, stride=2), :] = (
                        value[:, c * LANES : (c + 1) * LANES]
                    )
    gain, scale = down_gain_ref[...].reshape(1, channels), scale_ref[...].reshape(1, channels)
    for r in range(rows):
        at = pl.ds(r * width, width)
        grad = jnp.concatenate([grid[c, at, :] for c in range(chunks)], axis=1)
        back = norm_back(grad, n2_ref[at, :].astype(F32), inv_ref[at, LANES : LANES + 1], gain)
        scaled[at, :] = (back * scale).astype(BF16)
    for b in range(0, hidden, block):
        if b == split:
            loads[0].wait()
        weight = w2_near[b : b + block, :] if b < split else w2_far[b - split : b - split + block, :]
        slope = slope_ref[:, b : b + block].astype(F32)
        active[:, b : b + block] = (nt(scaled[...], weight) * slope).astype(BF16)
    loads[1].wait()
    for b in range(0, channels, block):
        acc[:, b : b + block] = nt(active[...], w1_ref[b : b + block, :])
    gain = gain_ref[...].reshape(1, channels)
    stores = []
    for r in range(rows):
        at = pl.ds(r * width, width)
        back = norm_back(acc[at, :], n1_ref[at, :].astype(F32), inv_ref[at, 0:1], gain)
        out_ref[0, r] = back.astype(BF16)
        stores.append(pltpu.make_async_copy(out_ref.at[0, r], out_hbm.at[0, r], out_sems.at[r]))
        stores[-1].start()
    wait(stores)


def push_body(chips, place, *rest):
    pieces = rest[: 2 * chips]
    pick_ref, w_ref, out_ref, patches, tokens = rest[2 * chips :]
    chip, core = place[0] // 2, place[0] % 2
    band = pieces[0].shape[0]
    for i, piece in enumerate(pieces):
        patches[i * band : (i + 1) * band, :] = piece[...]
    result = nn(patches[...], w_ref[...]).astype(BF16)
    for i in range(2 * chips):
        source = lax.rem(chip + chips - i // 2, chips)
        owner = 2 * source + (core if i % 2 == 0 else 1 - core)
        tokens[owner] = result[i * band : (i + 1) * band]
    flat = tokens[...].reshape(2 * chips * band, tokens.shape[2])
    out_ref[...] = nn(pick_ref[...], flat).astype(BF16)


def on_device(
    section_three, dw_kernel, dw_bias, mix_gain, w_expand, w_reduce, layer_scale, down_gain,
    w_down, owner_table, grad_packed,
):
    owners = lax.axis_size("dp")
    spaces = lax.axis_size("space")
    chips = spaces // 2
    slots = grad_packed.shape[1]
    capacity = slots // owners
    _, rows, width, channels = section_three.shape
    hidden = w_expand.shape[1]
    count = rows * width
    band = count // 4
    tokens = owner_table.shape[1]
    deep, narrow = w_down.shape
    place = lax.axis_index("space").astype(jnp.int32).reshape(1)
    lanes = channels // LANES
    block, step = 256, 768

    swap = [(i, i ^ 1) for i in range(spaces)]
    joints = [(i, i + 1) for i in range(1, spaces - 1, 2)]
    joints = joints + [(b, a) for a, b in joints]

    def send(value, pairs):
        return lax.ppermute(value, "space", pairs)

    def trade(value):
        return lax.all_to_all(value, "dp", split_axis=0, concat_axis=0, tiled=True)

    def onward(j):
        return [(i, (i + 2 * j) % spaces) for i in range(spaces)]

    (ready,) = call(prime_body, (), [], [((8, LANES), F32)], [], 1, 5e10, 1e3)
    near = send(section_three, swap)
    far = send(section_three, joints)
    returned = trade(grad_packed[0])

    patches, slope, n1, n2, inv = call(
        lambda *refs: forward_body(rows, width, channels, hidden, block, *refs[:8], *refs[9:]),
        (place, *close(near, far, dw_kernel, dw_bias, mix_gain, layer_scale, down_gain, ready),
         *far_off(section_three, w_expand, w_reduce)),
        [SMEM] + [VMEM] * 8 + [HBM] * 3,
        [((band, 4 * channels), BF16), ((count, hidden), BF16), ((count, channels), BF16),
         ((count, channels), BF16), ((count, 2 * LANES), F32)],
        [pltpu.VMEM(section_three.shape, BF16),
         pltpu.VMEM((lanes, rows + 2 * HALF, width + 2 * LEFT, LANES), F32),
         pltpu.VMEM((count, channels), F32), pltpu.VMEM((count, channels), BF16),
         pltpu.VMEM((count, hidden), BF16), pltpu.VMEM((count, channels), F32),
         pltpu.VMEM((lanes, count, LANES), F32),
         pltpu.VMEM(w_expand.shape, BF16), pltpu.VMEM(w_reduce.shape, BF16),
         pltpu.SemaphoreType.DMA((3,))],
        20, 4 * count * channels * hidden, 9e6,
    )
    held = [patches] + [send(patches, onward(j)) for j in range(1, chips)]
    (pick,) = call(
        lambda *refs: index_body(owners, capacity, *refs),
        close(owner_table.reshape(1, tokens)), [VMEM],
        [((slots, tokens), BF16)], [], 2, 1e7, 1e5,
    )
    keep, give, w_near, w2_near = call(
        lambda *refs: pull_body(spaces, step, *refs),
        (place, *close(returned, pick), *far_off(w_down, w_reduce)),
        [SMEM] + [VMEM] * 2 + [HBM] * 2,
        [((chips, band, deep), BF16), ((chips, band, deep), BF16), (w_down.shape, BF16),
         ((hidden // 2, channels), BF16)],
        [pltpu.VMEM((spaces, band, narrow), BF16), pltpu.VMEM((tokens, narrow), BF16),
         pltpu.SemaphoreType.DMA((3,))],
        6, 2 * tokens * deep * narrow, 4e6,
    )
    sent = send(give, swap)
    mine, *sums = call(
        lambda *refs: add_body(chips, *refs),
        (place, *close(keep, sent)), [SMEM, VMEM, VMEM],
        [((band, deep), F32)] + [((band, deep), BF16)] * (chips - 1), [], 4, 2e6, 1e6,
    )
    across = [send(sums[j - 1], onward(j)) for j in range(1, chips)]
    pieces = []
    for piece in held:
        pieces += [piece, send(piece, swap)]
    (buffer,) = call(
        lambda *refs: push_body(chips, *refs),
        (place, *close(*pieces, pick, w_near)),
        [SMEM] + [VMEM] * (len(pieces) + 2),
        [((slots, narrow), BF16)],
        [pltpu.VMEM((tokens, deep), BF16), pltpu.VMEM((spaces, band, narrow), BF16)],
        6, 2 * tokens * deep * narrow, 4e6,
    )
    arrived = trade(buffer)
    (grad_mixed,) = call(
        lambda *refs: backward_body(rows, width, channels, hidden, block, chips, *refs),
        (*close(mine, *across, slope, n1, n2, inv, w2_near, down_gain, layer_scale, mix_gain),
         *far_off(w_expand, w_reduce)),
        [VMEM] * (8 + chips) + [HBM] * 2,
        [jax.ShapeDtypeStruct(section_three.shape, BF16)],
        [pltpu.VMEM(section_three.shape, BF16), pltpu.VMEM((lanes, count, LANES), F32),
         pltpu.VMEM((count, channels), BF16), pltpu.VMEM((count, hidden), BF16),
         pltpu.VMEM((count, channels), F32),
         pltpu.VMEM(w_expand.shape, BF16), pltpu.VMEM((hidden // 2, channels), BF16),
         pltpu.SemaphoreType.DMA((2,)), pltpu.SemaphoreType.DMA((rows,))],
        16, 4 * count * channels * hidden, 9e6,
    )
    return arrived[None], grad_mixed


def solution(mesh):
    in_specs = (
        P("dp", "space", None, None), P(), P(), P(), P(), P(), P(), P(), P(None, "space"),
        P("dp", None, None), P("dp", None, "space"),
    )
    out_specs = (P("dp", None, "space"), P("dp", "space", None, None))
    return jax.shard_map(
        on_device, mesh=mesh, in_specs=in_specs, out_specs=out_specs, check_vma=False
    )
```

time: 44.2 us -> 45.9 us (1.038)
  starting transfers between devices: 14.8 us -> 17 us
  Pallas kernels: 13.2 us -> 11.6 us
  local copies, waits for them, and re-layouts: 0.64 us -> 1.3 us
    ppermute x7, starting transfers between devices: 4.08 us -> 6.74 us  [send(): return lax.ppermute(value, 'space', pairs)]
    pallas_call x5 -> x7, Pallas kernels: 13.2 us -> 11.6 us  [call(): pl.pallas_call(body, in_specs=specs, out_shape=tuple((pltpu.VMEM(*o) if i...]
    all_to_all x2, waiting for transfers between devices: 7.84 us -> 8.71 us  [trade(): return lax.all_to_all(value, 'dp', split_axis=0, concat_axis=0, tiled=True)]
    unnamed x1 -> x13, local copies, waits for them, and re-layouts: 0.64 us -> 1.3 us
    ppermute x7, waiting for transfers between devices: 6.65 us -> 6.17 us  [send(): return lax.ppermute(value, 'space', pairs)]
    all_to_all x2, starting transfers between devices: 10.7 us -> 10.2 us  [trade(): return lax.all_to_all(value, 'dp', split_axis=0, concat_axis=0, tiled=True)]
  transfers between devices with their start and end apart: 9 -> 9, of which waited for: 4 -> 4; matrix products, arithmetic and copies ran while one was open for 0% -> 0% of each run, Pallas kernels for 30% -> 25%
where the time goes in v5:
time: 45.9 us; the launch traced here: 45.5 us
  starting transfers between devices  17 us (37%)
  waiting for transfers between devices  14.9 us (32%)
  Pallas kernels  11.6 us (25%)
  local copies, waits for them, and re-layouts  1.3 us (3%)
  between operations  0.75 us (2%)
    pallas_call x7, Pallas kernels, call(): pl.pallas_call(body, in_specs=specs, out_shape=tuple((pltpu.VMEM(*o) if i...  11.6 us
    all_to_all x2, starting transfers between devices, trade(): return lax.all_to_all(value, 'dp', split_axis=0, concat_axis=0, tiled=True)  10.2 us
    all_to_all x2, waiting for transfers between devices, trade(): return lax.all_to_all(value, 'dp', split_axis=0, concat_axis=0, tiled=True)  8.71 us
    ppermute x7, starting transfers between devices, send(): return lax.ppermute(value, 'space', pairs)  6.74 us
    ppermute x7, waiting for transfers between devices, send(): return lax.ppermute(value, 'space', pairs)  6.17 us
    unnamed x13, local copies, waits for them, and re-layouts  1.3 us
  transfers between devices with their start and end apart: 9, of which 4 were waited for; matrix products, arithmetic and copies ran while one was open for 0% of the time, Pallas kernels for 25%

profile of v5, /device:TPU:0, one launch (start us, length us, event | category | flops | bytes accessed | tf_op | source)
XLA Modules:
  0.0 45.5 jit_solution(2863998258134542989)
XLA Ops:
  0.6 0.6 %collective-permute-start = (bf16[1,4,32,768]{3,2,1,0:T(8,128)(2,1)}, bf16[1,4,32,768]{3,2,1,0:T(8,128)(2,1)S(1)}, u32[]{:S(2)}, u32[]{:S(2)}) collective-permute-start(bf16[1,4,32,768]{3,2,1,0:T(8,128)(2,1)} %refs_9_.2), channel_id=1, source_target_pairs={{0,1},{1,0},{2,3},{3,2},{4,5},{5,4},{6,7},{7,6},{8,9},{9,8},{10,11... | collective-permute-start | bytes 589832 | tf_op jit(solution)/shard_map/ppermute | solution.py:314
  1.2 0.7 %collective-permute-start.1 = (bf16[1,4,32,768]{3,2,1,0:T(8,128)(2,1)}, bf16[1,4,32,768]{3,2,1,0:T(8,128)(2,1)S(1)}, u32[]{:S(2)}, u32[]{:S(2)}) collective-permute-start(bf16[1,4,32,768]{3,2,1,0:T(8,128)(2,1)} %refs_9_.2), channel_id=1, source_target_pairs={{1,2},{2,1},{5,6},{6,5},{9,10},{10,9},{13,14},{14,13},{17,18},{18,... | collective-permute-start | bytes 589832 | tf_op jit(solution)/shard_map/ppermute | solution.py:314
  1.9 6.9 %all-to-all-start = ((bf16[8,16,384]{2,1,0:T(8,128)(2,1)}), bf16[8,16,384]{2,1,0:T(8,128)(2,1)S(1)}, u32[]{:S(2)}, u32[]{:S(2)}) async-start(bf16[8,16,384]{2,1,0:T(8,128)(2,1)} %bitcast.9), calls=%async_computation | async-start | bytes 196608 | tf_op jit(solution)/shard_map/all_to_all | solution.py:317
  8.7 0.0 copy-start.5
  8.7 0.6 %copy-done.5 = s32[1,128,1]{1,2,0:T(1,128)S(1)} copy-done((s32[1,128,1]{1,2,0:T(1,128)S(1)}, s32[1,128,1]{1,2,0:T(1,128)}, u32[]{:S(2)}) %copy-start.5) | copy-done | bytes 536
  9.4 0.1 shard_map.124.refs_2_.refs_5_
  9.5 6.3 %all-to-all-done = bf16[8,16,384]{2,1,0:T(8,128)(2,1)S(1)} async-done(((bf16[8,16,384]{2,1,0:T(8,128)(2,1)}), bf16[8,16,384]{2,1,0:T(8,128)(2,1)S(1)}, u32[]{:S(2)}, u32[]{:S(2)}) %all-to-all-start) | async-done | bytes 98336 | tf_op jit(solution)/shard_map/all_to_all | solution.py:317
  15.8 0.0 copy-start
  15.8 0.0 copy-start.1
  15.8 0.0 copy-start.2
  15.8 0.0 copy-start.3
  15.8 0.0 copy-start.4
  15.9 2.7 %shard_map.125 = (bf16[2,32,3072]{2,1,0:T(8,128)(2,1)S(1)}, bf16[2,32,3072]{2,1,0:T(8,128)(2,1)S(1)}, bf16[3072,384]{1,0:T(8,128)(2,1)S(1)}, bf16[768,768]{1,0:T(8,128)(2,1)S(1)}) custom-call(s32[1]{0:T(128)} %bitcast.refs_0_, bf16[128,384]{1,0:T(8,128)(2,1)S(1)} %bitcast.6, bf16[128,128]{1,0:T(8,128)(2,1)S(1)} %shard_map.124.refs_2_.refs_5_, ...), custom_call_target="tpu_custom_call" | custom-call | flops 301989888 | bytes 4000000 | tf_op jit(solution)/shard_map/pallas_call | solution.py:39
  18.6 1.5 %collective-permute-start.5 = (bf16[2,32,3072]{2,1,0:T(8,128)(2,1)S(1)}, bf16[2,32,3072]{2,1,0:T(8,128)(2,1)S(1)}, u32[]{:S(2)}, u32[]{:S(2)}) collective-permute-start(bf16[2,32,3072]{2,1,0:T(8,128)(2,1)S(1)} %get-tuple-element.16), channel_id=1, source_target_pairs={{0,1},{1,0},{2,3},{3,2},{4,5},{5,4},{6,7},{7,6},{8,9},{9,8},{10,11... | collective-permute-start | bytes 1179656 | tf_op jit(solution)/shard_map/ppermute | solution.py:314
  20.1 0.0 collective-permute-done.refs_1_
  20.1 0.0 collective-permute-done.1.refs_2_
  20.1 0.0 copy-done
  20.1 0.0 copy-done.1
  20.1 0.0 copy-done.2
  20.1 0.0 copy-done.3
  20.1 0.0 copy-done.4
  20.1 3.4 %shard_map.123 = (bf16[32,3072]{1,0:T(8,128)(2,1)S(1)}, bf16[128,1536]{1,0:T(8,128)(2,1)S(1)}, bf16[128,768]{1,0:T(8,128)(2,1)S(1)}, bf16[128,768]{1,0:T(8,128)(2,1)S(1)}, f32[128,256]{1,0:T(8,128)S(1)}) custom-call(s32[1]{0:T(128)} %bitcast.refs_0_, bf16[1,4,32,768]{3,2,1,0:T(8,128)(2,1)S(1)} %collective-permute-done.refs_1_, ...), custom_call_target="tpu_custom_call" | custom-call | flops 603979776 | bytes 9000000 | tf_op jit(solution)/shard_map/pallas_call | solution.py:39
  23.5 2.0 %collective-permute-start.3 = (bf16[32,3072]{1,0:T(8,128)(2,1)S(1)}, bf16[32,3072]{1,0:T(8,128)(2,1)S(1)}, u32[]{:S(2)}, u32[]{:S(2)}) collective-permute-start(bf16[32,3072]{1,0:T(8,128)(2,1)S(1)} %get-tuple-element.13.refs_1_), channel_id=1, source_target_pairs={{0,2},{1,3},{2,0},{3,1},{4,6},{5,7},{6,4},{7,5},{8,10},{9,11},{10,... | collective-permute-start | bytes 589832 | tf_op jit(solution)/shard_map/ppermute | solution.py:314
  25.5 0.2 collective-permute-start.2
  25.7 5.3 %collective-permute-done.3.refs_3_ = bf16[32,3072]{1,0:T(8,128)(2,1)S(1)} collective-permute-done((bf16[32,3072]{1,0:T(8,128)(2,1)S(1)}, bf16[32,3072]{1,0:T(8,128)(2,1)S(1)}, u32[]{:S(2)}, u32[]{:S(2)}) %collective-permute-start.3) | collective-permute-done | bytes 196640 | tf_op jit(solution)/shard_map/ppermute | solution.py:314
  31.1 0.0 collective-permute-start.4
  31.1 0.0 collective-permute-done.5.refs_2_
  31.1 0.1 shard_map.127
  31.2 1.8 %collective-permute-start.6 = (bf16[32,3072]{1,0:T(8,128)(2,1)S(1)}, bf16[32,3072]{1,0:T(8,128)(2,1)S(1)}, u32[]{:S(2)}, u32[]{:S(2)}) collective-permute-start(bf16[32,3072]{1,0:T(8,128)(2,1)S(1)} %get-tuple-element.18), channel_id=1, source_target_pairs={{0,2},{1,3},{2,0},{3,1},{4,6},{5,7},{6,4},{7,5},{8,10},{9,11},{10,... | collective-permute-start | bytes 589832 | tf_op jit(solution)/shard_map/ppermute | solution.py:314
  33.0 0.0 collective-permute-done.2.refs_2_
  33.0 0.0 collective-permute-done.4.refs_4_
  33.0 1.4 %shard_map.126 = bf16[128,384]{1,0:T(8,128)(2,1)} custom-call(s32[1]{0:T(128)} %bitcast.refs_0_, bf16[32,3072]{1,0:T(8,128)(2,1)S(1)} %get-tuple-element.13.refs_1_, bf16[32,3072]{1,0:T(8,128)(2,1)S(1)} %collective-permute-done.2.refs_2_, bf16[32,3072]{1,0:T(8,128)(2,1)S(1)} %collective-permute-done.3.refs_3_, ...), custom_call_target="tpu_custom_call" | custom-call | flops 301989888 | bytes 4000000 | tf_op jit(solution)/shard_map/pallas_call | solution.py:39
  34.4 3.4 %all-to-all-start.1 = ((bf16[8,16,384]{2,1,0:T(8,128)(2,1)}), bf16[8,16,384]{2,1,0:T(8,128)(2,1)S(1)}, u32[]{:S(2)}, u32[]{:S(2)}) async-start(bf16[8,16,384]{2,1,0:T(8,128)(2,1)} %bitcast.4), calls=%async_computation.1 | async-start | bytes 196608 | tf_op jit(solution)/shard_map/all_to_all | solution.py:317
  37.7 0.8 %collective-permute-done.6.refs_1_ = bf16[32,3072]{1,0:T(8,128)(2,1)S(1)} collective-permute-done((bf16[32,3072]{1,0:T(8,128)(2,1)S(1)}, bf16[32,3072]{1,0:T(8,128)(2,1)S(1)}, u32[]{:S(2)}, u32[]{:S(2)}) %collective-permute-start.6) | collective-permute-done | bytes 196640 | tf_op jit(solution)/shard_map/ppermute | solution.py:314
  38.5 3.9 %shard_map.128 = bf16[1,4,32,768]{3,2,1,0:T(8,128)(2,1)} custom-call(f32[32,3072]{1,0:T(8,128)S(1)} %get-tuple-element.17.refs_0_, bf16[32,3072]{1,0:T(8,128)(2,1)S(1)} %collective-permute-done.6.refs_1_, bf16[128,1536]{1,0:T(8,128)(2,1)S(1)} %get-tuple-element.19.refs_2_, bf16[128,768]{1,0:T(8,128)(2,1)S(1)} %get-tuple-element.20.refs_3_, ...), custom_call_target="tpu_custom_call" | custom-call | flops 603979776 | bytes 9000000 | tf_op jit(solution)/shard_map/pallas_call | solution.py:39
  42.5 2.4 %all-to-all-done.1 = bf16[8,16,384]{2,1,0:T(8,128)(2,1)S(1)} async-done(((bf16[8,16,384]{2,1,0:T(8,128)(2,1)}), bf16[8,16,384]{2,1,0:T(8,128)(2,1)S(1)}, u32[]{:S(2)}, u32[]{:S(2)}) %all-to-all-start.1) | async-done | bytes 98336 | tf_op jit(solution)/shard_map/all_to_all | solution.py:317
  44.8 0.6 %copy.14 = bf16[1,128,384]{2,1,0:T(8,128)(2,1)} copy(bf16[1,128,384]{2,1,0:T(8,128)(2,1)S(1)} %bitcast.8) | data formatting | bytes 196608
  (1 shorter events, 0.0 us)
Async XLA Ops:
  0.6 19.4 %collective-permute-start = (bf16[1,4,32,768]{3,2,1,0:T(8,128)(2,1)}, bf16[1,4,32,768]{3,2,1,0:T(8,128)(2,1)S(1)}, u32[]{:S(2)}, u32[]{:S(2)}) collective-permute-start(bf16[1,4,32,768]{3,2,1,0:T(8,128)(2,1)} %refs_9_.2), channel_id=1, source_target_pairs={{0,1},{1,0},{2,3},{3,2},{4,5},{5,4},{6,7},{7,6},{8,9},{9,8},{10,11... | collective-permute-start | bytes 589832 | tf_op jit(solution)/shard_map/ppermute | solution.py:314
  1.2 18.9 %collective-permute-start.1 = (bf16[1,4,32,768]{3,2,1,0:T(8,128)(2,1)}, bf16[1,4,32,768]{3,2,1,0:T(8,128)(2,1)S(1)}, u32[]{:S(2)}, u32[]{:S(2)}) collective-permute-start(bf16[1,4,32,768]{3,2,1,0:T(8,128)(2,1)} %refs_9_.2), channel_id=1, source_target_pairs={{1,2},{2,1},{5,6},{6,5},{9,10},{10,9},{13,14},{14,13},{17,18},{18,... | collective-permute-start | bytes 589832 | tf_op jit(solution)/shard_map/ppermute | solution.py:314
  1.9 14.0 %all-to-all-start = ((bf16[8,16,384]{2,1,0:T(8,128)(2,1)}), bf16[8,16,384]{2,1,0:T(8,128)(2,1)S(1)}, u32[]{:S(2)}, u32[]{:S(2)}) async-start(bf16[8,16,384]{2,1,0:T(8,128)(2,1)} %bitcast.9), calls=%async_computation | async-start | bytes 196608 | tf_op jit(solution)/shard_map/all_to_all | solution.py:317
  8.7 0.7 %copy-start.5 = (s32[1,128,1]{1,2,0:T(1,128)S(1)}, s32[1,128,1]{1,2,0:T(1,128)}, u32[]{:S(2)}) copy-start(s32[1,128,1]{1,2,0:T(1,128)} %param.20) | copy-start | bytes 1540
  15.8 4.2 %copy-start = (f32[7,7,768]{2,1,0:T(8,128)S(1)}, f32[7,7,768]{2,1,0:T(8,128)}, u32[]{:S(2)}) copy-start(f32[7,7,768]{2,1,0:T(8,128)} %refs_3_.2) | copy-start | bytes 451588
  15.8 4.2 %copy-start.1 = (f32[768]{0:T(1024)S(1)}, f32[768]{0:T(1024)}, u32[]{:S(2)}) copy-start(f32[768]{0:T(1024)} %refs_9_.3) | copy-start | bytes 9220
  15.8 4.2 %copy-start.2 = (f32[768]{0:T(1024)S(1)}, f32[768]{0:T(1024)}, u32[]{:S(2)}) copy-start(f32[768]{0:T(1024)} %refs_8_.1) | copy-start | bytes 9220
  15.8 4.2 %copy-start.3 = (f32[768]{0:T(1024)S(1)}, f32[768]{0:T(1024)}, u32[]{:S(2)}) copy-start(f32[768]{0:T(1024)} %refs_7_.3) | copy-start | bytes 9220
  15.8 4.3 %copy-start.4 = (f32[768]{0:T(1024)S(1)}, f32[768]{0:T(1024)}, u32[]{:S(2)}) copy-start(f32[768]{0:T(1024)} %refs_4_.2) | copy-start | bytes 9220
  18.6 12.5 %collective-permute-start.5 = (bf16[2,32,3072]{2,1,0:T(8,128)(2,1)S(1)}, bf16[2,32,3072]{2,1,0:T(8,128)(2,1)S(1)}, u32[]{:S(2)}, u32[]{:S(2)}) collective-permute-start(bf16[2,32,3072]{2,1,0:T(8,128)(2,1)S(1)} %get-tuple-element.16), channel_id=1, source_target_pairs={{0,1},{1,0},{2,3},{3,2},{4,5},{5,4},{6,7},{7,6},{8,9},{9,8},{10,11... | collective-permute-start | bytes 1179656 | tf_op jit(solution)/shard_map/ppermute | solution.py:314
  23.5 7.6 %collective-permute-start.3 = (bf16[32,3072]{1,0:T(8,128)(2,1)S(1)}, bf16[32,3072]{1,0:T(8,128)(2,1)S(1)}, u32[]{:S(2)}, u32[]{:S(2)}) collective-permute-start(bf16[32,3072]{1,0:T(8,128)(2,1)S(1)} %get-tuple-element.13.refs_1_), channel_id=1, source_target_pairs={{0,2},{1,3},{2,0},{3,1},{4,6},{5,7},{6,4},{7,5},{8,10},{9,11},{10,... | collective-permute-start | bytes 589832 | tf_op jit(solution)/shard_map/ppermute | solution.py:314
  25.5 7.5 %collective-permute-start.2 = (bf16[32,3072]{1,0:T(8,128)(2,1)S(1)}, bf16[32,3072]{1,0:T(8,128)(2,1)S(1)}, u32[]{:S(2)}, u32[]{:S(2)}) collective-permute-start(bf16[32,3072]{1,0:T(8,128)(2,1)S(1)} %get-tuple-element.13.refs_1_), channel_id=1, source_target_pairs={{0,1},{1,0},{2,3},{3,2},{4,5},{5,4},{6,7},{7,6},{8,9},{9,8},{10,11... | collective-permute-start | bytes 589832 | tf_op jit(solution)/shard_map/ppermute | solution.py:314
  31.1 1.9 %collective-permute-start.4 = (bf16[32,3072]{1,0:T(8,128)(2,1)S(1)}, bf16[32,3072]{1,0:T(8,128)(2,1)S(1)}, u32[]{:S(2)}, u32[]{:S(2)}) collective-permute-start(bf16[32,3072]{1,0:T(8,128)(2,1)S(1)} %collective-permute-done.3.refs_3_), channel_id=1, source_target_pairs={{0,1},{1,0},{2,3},{3,2},{4,5},{5,4},{6,7},{7,6},{8,9},{9,8},{10,11... | collective-permute-start | bytes 589832 | tf_op jit(solution)/shard_map/ppermute | solution.py:314
  31.2 7.4 %collective-permute-start.6 = (bf16[32,3072]{1,0:T(8,128)(2,1)S(1)}, bf16[32,3072]{1,0:T(8,128)(2,1)S(1)}, u32[]{:S(2)}, u32[]{:S(2)}) collective-permute-start(bf16[32,3072]{1,0:T(8,128)(2,1)S(1)} %get-tuple-element.18), channel_id=1, source_target_pairs={{0,2},{1,3},{2,0},{3,1},{4,6},{5,7},{6,4},{7,5},{8,10},{9,11},{10,... | collective-permute-start | bytes 589832 | tf_op jit(solution)/shard_map/ppermute | solution.py:314
  34.4 10.5 %all-to-all-start.1 = ((bf16[8,16,384]{2,1,0:T(8,128)(2,1)}), bf16[8,16,384]{2,1,0:T(8,128)(2,1)S(1)}, u32[]{:S(2)}, u32[]{:S(2)}) async-start(bf16[8,16,384]{2,1,0:T(8,128)(2,1)} %bitcast.4), calls=%async_computation.1 | async-start | bytes 196608 | tf_op jit(solution)/shard_map/all_to_all | solution.py:317

commit v6 on v5

--- a/solution.py
+++ b/solution.py
@@ -82,89 +82,111 @@
     out_ref[...] = jnp.zeros(out_ref.shape, F32)
 
 
-def forward_body(
-    rows, width, channels, hidden, block,
-    place, near_ref, far_ref, kernel_ref, bias_ref, gain_ref, scale_ref, down_gain_ref,
-    x_hbm, w1_hbm, w2_hbm,
-    patch_ref, slope_ref, n1_ref, n2_ref, inv_ref,
-    x_ref, padded, mixed, first, active, acc, grid, w1_ref, w2_ref, in_sems,
-):
-    odd = place[0] % 2 == 1
+def convolve(padded, c, first_line, lines, total, kernel_ref, at, rows, width):
+    for dx in range(KS):
+        taps = [kernel_ref[dy, dx : dx + 1, at] for dy in range(KS)]
+        for r in lines:
+            line = padded[c, first_line(r), pl.ds(LEFT - HALF + dx, width), :]
+            for out in range(rows):
+                if 0 <= r - out < KS:
+                    total[out] = total[out] + line * taps[r - out]
+    return total
+
+
+def conv_body(rows, width, channels, chips, kernel_ref, bias_ref, ready, *rest):
+    bands, (w1_hbm, w2_hbm, part_ref, w1_ref, w2_ref, padded, sems) = rest[:chips], rest[chips:]
+    loads = fetch(((w1_hbm, w1_ref), (w2_hbm, w2_ref)), sems)
     chunks = channels // LANES
-    tall = rows + 2 * HALF
-    loads = fetch(((x_hbm, x_ref), (w1_hbm, w1_ref), (w2_hbm, w2_ref)), in_sems)
-    padded[:, :, 0:LEFT, :] = jnp.zeros((chunks, tall, LEFT, LANES), F32)
-    padded[:, :, LEFT + width :, :] = jnp.zeros((chunks, tall, LEFT, LANES), F32)
     cols = pl.ds(LEFT, width)
-    own = range(HALF, HALF + rows)
-
-    def convolve(c, at, lines, total):
-        for dx in range(KS):
-            taps = [kernel_ref[dy, dx : dx + 1, at] for dy in range(KS)]
-            for r in lines:
-                line = padded[c, r, pl.ds(LEFT - HALF + dx, width), :]
-                for out in range(rows):
-                    if 0 <= r - out < KS:
-                        total[out] = total[out] + line * taps[r - out]
-        for out in range(rows):
-            mixed[pl.ds(out * width, width), at] = total[out]
-
-    def outer(c, _):
-        at = pl.ds(pl.multiple_of(c * LANES, LANES), LANES)
-        near, far = near_ref[0, :, :, at].astype(F32), far_ref[0, :, :, at].astype(F32)
-        above, below = jnp.where(odd, near, far), jnp.where(odd, far, near)
-        padded[c, 0:HALF, cols, :] = above[rows - HALF :]
-        padded[c, HALF + rows :, cols, :] = below[:HALF]
-        bias = jnp.broadcast_to(bias_ref[at].reshape(1, LANES), (width, LANES))
-        convolve(c, at, [r for r in range(tall) if r not in own], [bias for _ in range(rows)])
-        return 0
-
-    def inner(c, _):
-        at = pl.ds(pl.multiple_of(c * LANES, LANES), LANES)
-        padded[c, HALF : HALF + rows, cols, :] = x_ref[0, :, :, at].astype(F32)
-        convolve(c, at, own, [mixed[pl.ds(out * width, width), at] for out in range(rows)])
-        return 0
-
-    lax.fori_loop(0, chunks, outer, 0)
-    loads[0].wait()
-    lax.fori_loop(0, chunks, inner, 0)
+    padded[:, :, 0:LEFT, :] = jnp.zeros((chunks, rows, LEFT, LANES), F32)
+    padded[:, :, LEFT + width :, :] = jnp.zeros((chunks, rows, LEFT, LANES), F32)
+    for q, band_ref in enumerate(bands):
+
+        def own(c, _):
+            at = pl.ds(pl.multiple_of(c * LANES, LANES), LANES)
+            padded[c, :, cols, :] = band_ref[0, :, :, at].astype(F32)
+            bias = jnp.broadcast_to(bias_ref[at].reshape(1, LANES), (width, LANES))
+            lines = range(HALF, HALF + rows)
+            total = convolve(padded, c, lambda r: r - HALF, lines, [bias] * rows, kernel_ref, at, rows, width)
+            for out in range(rows):
+                part_ref[pl.ds((q * rows + out) * width, width), at] = total[out]
+            return 0
+
+        lax.fori_loop(0, chunks, own, 0)
+    wait(loads)
+
+
+def forward_body(rows, width, channels, hidden, block, chips, place, part_ref, kernel_ref, *rest):
+    mates, bands = rest[:chips], rest[chips : 2 * chips]
+    (
+        gain_ref, scale_ref, down_gain_ref, w1_ref, w2_ref,
+        patch_ref, slope_ref, n1_ref, n2_ref, inv_ref,
+        padded, mixed, first, active, acc, grid,
+    ) = rest[2 * chips :]
+    chip, odd = place[0] // 2, place[0] % 2 == 1
+    chunks = channels // LANES
     count = rows * width
+    cols = pl.ds(LEFT, width)
+    padded[:, :, 0:LEFT, :] = jnp.zeros((chunks, 2 * HALF, LEFT, LANES), F32)
+    padded[:, :, LEFT + width :, :] = jnp.zeros((chunks, 2 * HALF, LEFT, LANES), F32)
+    for q in range(chips):
+        level = lax.rem(chip + chips - q, chips)
+        same, over, under = mates[q], mates[(q + 1) % chips], mates[(q - 1) % chips]
+
+        def outer(c, _):
+            at = pl.ds(pl.multiple_of(c * LANES, LANES), LANES)
+            low, high = slice(0, HALF), slice(rows - HALF, rows)
+            above = jnp.where(level > 0, over[0, high, :, at].astype(F32), 0.0)
+            below = jnp.where(level < chips - 1, under[0, low, :, at].astype(F32), 0.0)
+            padded[c, 0:HALF, cols, :] = jnp.where(odd, same[0, high, :, at].astype(F32), above)
+            padded[c, HALF:, cols, :] = jnp.where(odd, below, same[0, low, :, at].astype(F32))
+            spots = [pl.ds((q * rows + out) * width, width) for out in range(rows)]
+            lines = [r for r in range(rows + 2 * HALF) if not HALF <= r < HALF + rows]
+            total = convolve(
+                padded, c, lambda r: r if r < HALF else r - rows, lines, [part_ref[p, at] for p in spots],
+                kernel_ref, at, rows, width,
+            )
+            for p, value in zip(spots, total):
+                mixed[p, at] = value
+            return 0
+
+        lax.fori_loop(0, chunks, outer, 0)
     gain = gain_ref[...].reshape(1, channels)
-    for r in range(0, count, width):
+    for r in range(0, chips * count, width):
         n1, inv1 = normalize(mixed[r : r + width, :])
-        n1_ref[r : r + width, :] = n1.astype(BF16)
-        inv_ref[r : r + width, 0:LANES] = jnp.broadcast_to(inv1, (width, LANES))
+        if r < count:
+            n1_ref[r : r + width, :] = n1.astype(BF16)
+            inv_ref[r : r + width, 0:LANES] = jnp.broadcast_to(inv1, (width, LANES))
         first[r : r + width, :] = (n1 * gain).astype(BF16)
-    loads[1].wait()
     for b in range(0, hidden, block):
         pre = nn(first[...], w1_ref[:, b : b + block])
         cumulative = 0.5 * (1.0 + lax.erf(pre * 0.7071067811865476))
-        density = jnp.exp(-0.5 * pre * pre) * 0.3989422804014327
-        slope_ref[:, b : b + block] = (cumulative + pre * density).astype(BF16)
+        mine = pre[:count]
+        density = jnp.exp(-0.5 * mine * mine) * 0.3989422804014327
+        slope_ref[:, b : b + block] = (cumulative[:count] + mine * density).astype(BF16)
         active[:, b : b + block] = (pre * cumulative).astype(BF16)
-    loads[2].wait()
     for b in range(0, channels, block):
         acc[:, b : b + block] = nn(active[...], w2_ref[:, b : b + block])
     scale, gain = scale_ref[...].reshape(1, channels), down_gain_ref[...].reshape(1, channels)
-    for r in range(rows):
-        at = pl.ds(r * width, width)
-        n2, inv2 = normalize(x_ref[0, r].astype(F32) + scale * acc[at, :])
-        n2_ref[at, :] = n2.astype(BF16)
-        inv_ref[at, LANES:] = jnp.broadcast_to(inv2, (width, LANES))
-        second = n2 * gain
-        for c in range(chunks):
-            grid[c, at, :] = second[:, c * LANES : (c + 1) * LANES]
     half = width // 2
-    for r in range(rows // 2):
-        for a in range(2):
-            for b in range(2):
-                piece = jnp.concatenate(
-                    [grid[c, pl.ds((2 * r + a) * width + b, half, stride=2), :] for c in range(chunks)],
-                    axis=1,
-                )
-                patch_ref[r * half : (r + 1) * half, (2 * a + b) * channels : (2 * a + b + 1) * channels] = (
-                    piece.astype(BF16)
-                )
+    for q in range(chips):
+        for r in range(rows):
+            at = pl.ds(r * width, width)
+            n2, inv2 = normalize(bands[q][0, r].astype(F32) + scale * acc[pl.ds(q * count + r * width, width), :])
+            if q == 0:
+                n2_ref[at, :] = n2.astype(BF16)
+                inv_ref[at, LANES:] = jnp.broadcast_to(inv2, (width, LANES))
+            second = n2 * gain
+            for c in range(chunks):
+                grid[c, pl.ds(q * count + r * width, width), :] = second[:, c * LANES : (c + 1) * LANES]
+        for r in range(rows // 2):
+            for a in range(2):
+                for b in range(2):
+                    spot = pl.ds(q * count + (2 * r + a) * width + b, half, stride=2)
+                    piece = jnp.concatenate([grid[c, spot, :] for c in range(chunks)], axis=1)
+                    patch_ref[q, r * half : (r + 1) * half, (2 * a + b) * channels : (2 * a + b + 1) * channels] = (
+                        piece.astype(BF16)
+                    )
 
 
 def index_body(owners, capacity, table_ref, pick_ref):
@@ -271,13 +293,12 @@
     wait(stores)
 
 
-def push_body(chips, place, *rest):
-    pieces = rest[: 2 * chips]
-    pick_ref, w_ref, out_ref, patches, tokens = rest[2 * chips :]
+def push_body(chips, place, own_ref, mate_ref, pick_ref, w_ref, out_ref, patches, tokens):
     chip, core = place[0] // 2, place[0] % 2
-    band = pieces[0].shape[0]
-    for i, piece in enumerate(pieces):
-        patches[i * band : (i + 1) * band, :] = piece[...]
+    band = own_ref.shape[1]
+    for i in range(2 * chips):
+        source_ref = own_ref if i % 2 == 0 else mate_ref
+        patches[i * band : (i + 1) * band, :] = source_ref[i // 2]
     result = nn(patches[...], w_ref[...]).astype(BF16)
     for i in range(2 * chips):
         source = lax.rem(chip + chips - i // 2, chips)
@@ -307,8 +328,6 @@
     block, step = 256, 768
 
     swap = [(i, i ^ 1) for i in range(spaces)]
-    joints = [(i, i + 1) for i in range(1, spaces - 1, 2)]
-    joints = joints + [(b, a) for a, b in joints]
 
     def send(value, pairs):
         return lax.ppermute(value, "space", pairs)
@@ -321,26 +340,32 @@
 
     (ready,) = call(prime_body, (), [], [((8, LANES), F32)], [], 1, 5e10, 1e3)
     near = send(section_three, swap)
-    far = send(section_three, joints)
+    bands = [section_three] + [send(section_three, onward(j)) for j in range(1, chips)]
     returned = trade(grad_packed[0])
 
+    mates = [near] + [send(bands[j], swap) for j in range(1, chips)]
+    wide = chips * count
+    part, w1_near, w2_whole = call(
+        lambda *refs: conv_body(rows, width, channels, chips, *refs),
+        (*close(dw_kernel, dw_bias, ready, *bands), *far_off(w_expand, w_reduce)),
+        [VMEM] * (3 + chips) + [HBM] * 2,
+        [((wide, channels), F32), (w_expand.shape, BF16), (w_reduce.shape, BF16)],
+        [pltpu.VMEM((lanes, rows, width + 2 * LEFT, LANES), F32), pltpu.SemaphoreType.DMA((2,))],
+        6, 4e9, 6e6,
+    )
     patches, slope, n1, n2, inv = call(
-        lambda *refs: forward_body(rows, width, channels, hidden, block, *refs[:8], *refs[9:]),
-        (place, *close(near, far, dw_kernel, dw_bias, mix_gain, layer_scale, down_gain, ready),
-         *far_off(section_three, w_expand, w_reduce)),
-        [SMEM] + [VMEM] * 8 + [HBM] * 3,
-        [((band, 4 * channels), BF16), ((count, hidden), BF16), ((count, channels), BF16),
+        lambda *refs: forward_body(rows, width, channels, hidden, block, chips, *refs),
+        (place, *close(part, dw_kernel, *mates, *bands, mix_gain, layer_scale, down_gain, w1_near, w2_whole)),
+        [SMEM] + [VMEM] * (7 + 2 * chips),
+        [((chips, band, 4 * channels), BF16), ((count, hidden), BF16), ((count, channels), BF16),
          ((count, channels), BF16), ((count, 2 * LANES), F32)],
-        [pltpu.VMEM(section_three.shape, BF16),
-         pltpu.VMEM((lanes, rows + 2 * HALF, width + 2 * LEFT, LANES), F32),
-         pltpu.VMEM((count, channels), F32), pltpu.VMEM((count, channels), BF16),
-         pltpu.VMEM((count, hidden), BF16), pltpu.VMEM((count, channels), F32),
-         pltpu.VMEM((lanes, count, LANES), F32),
-         pltpu.VMEM(w_expand.shape, BF16), pltpu.VMEM(w_reduce.shape, BF16),
-         pltpu.SemaphoreType.DMA((3,))],
-        20, 4 * count * channels * hidden, 9e6,
-    )
-    held = [patches] + [send(patches, onward(j)) for j in range(1, chips)]
+        [pltpu.VMEM((lanes, 2 * HALF, width + 2 * LEFT, LANES), F32),
+         pltpu.VMEM((wide, channels), F32), pltpu.VMEM((wide, channels), BF16),
+         pltpu.VMEM((wide, hidden), BF16), pltpu.VMEM((wide, channels), F32),
+         pltpu.VMEM((lanes, wide, LANES), F32)],
+        20, 4 * wide * channels * hidden, 9e6,
+    )
+    mate_patches = send(patches, swap)
     (pick,) = call(
         lambda *refs: index_body(owners, capacity, *refs),
         close(owner_table.reshape(1, tokens)), [VMEM],
@@ -363,13 +388,10 @@
         [((band, deep), F32)] + [((band, deep), BF16)] * (chips - 1), [], 4, 2e6, 1e6,
     )
     across = [send(sums[j - 1], onward(j)) for j in range(1, chips)]
-    pieces = []
-    for piece in held:
-        pieces += [piece, send(piece, swap)]
     (buffer,) = call(
         lambda *refs: push_body(chips, *refs),
-        (place, *close(*pieces, pick, w_near)),
-        [SMEM] + [VMEM] * (len(pieces) + 2),
+        (place, *close(patches, mate_patches, pick, w_near)),
+        [SMEM] + [VMEM] * 4,
         [((slots, narrow), BF16)],
         [pltpu.VMEM((tokens, deep), BF16), pltpu.VMEM((spaces, band, narrow), BF16)],
         6, 2 * tokens * deep * narrow, 4e6,
@@ -397,6 +419,4 @@
         P("dp", None, None), P("dp", None, "space"),
     )
     out_specs = (P("dp", None, "space"), P("dp", "space", None, None))
-    return jax.shard_map(
-        on_device, mesh=mesh, in_specs=in_specs, out_specs=out_specs, check_vma=False
-    )
+    return jax.shard_map(on_device, mesh=mesh, in_specs=in_specs, out_specs=out_specs, check_vma=False)

time: 45.9 us -> 40.6 us (0.88)
  waiting for transfers between devices: 14.9 us -> 10.5 us
  starting transfers between devices: 17 us -> 13.5 us
  Pallas kernels: 11.6 us -> 14.1 us
    ppermute x7 -> x6, waiting for transfers between devices: 6.17 us -> 1.97 us  [send(): return lax.ppermute(value, 'space', pairs)]
    pallas_call x7 -> x8, Pallas kernels: 11.6 us -> 14.1 us  [call(): pl.pallas_call(body, in_specs=specs, out_shape=tuple((pltpu.VMEM(*o) if i...]
    ppermute x7 -> x6, starting transfers between devices: 6.74 us -> 4.32 us  [send(): return lax.ppermute(value, 'space', pairs)]
    all_to_all x2, starting transfers between devices: 10.2 us -> 9.2 us  [trade(): return lax.all_to_all(value, 'dp', split_axis=0, concat_axis=0, tiled=True)]
    unnamed x13 -> x15, local copies, waits for them, and re-layouts: 1.3 us -> 1.31 us
  transfers between devices with their start and end apart: 9 -> 8, of which waited for: 4 -> 4; matrix products, arithmetic and copies ran while one was open for 0% -> 0% of each run, Pallas kernels for 25% -> 35%
where the time goes in v6:
time: 40.6 us; the launch traced here: 40.2 us
  Pallas kernels  14.1 us (35%)
  starting transfers between devices  13.5 us (33%)
  waiting for transfers between devices  10.5 us (26%)
  local copies, waits for them, and re-layouts  1.31 us (3%)
  between operations  0.78 us (2%)
    pallas_call x8, Pallas kernels, call(): pl.pallas_call(body, in_specs=specs, out_shape=tuple((pltpu.VMEM(*o) if i...  14.1 us
    all_to_all x2, starting transfers between devices, trade(): return lax.all_to_all(value, 'dp', split_axis=0, concat_axis=0, tiled=True)  9.2 us
    all_to_all x2, waiting for transfers between devices, trade(): return lax.all_to_all(value, 'dp', split_axis=0, concat_axis=0, tiled=True)  8.52 us
    ppermute x6, starting transfers between devices, send(): return lax.ppermute(value, 'space', pairs)  4.32 us
    ppermute x6, waiting for transfers between devices, send(): return lax.ppermute(value, 'space', pairs)  1.97 us
    unnamed x15, local copies, waits for them, and re-layouts  1.31 us
  transfers between devices with their start and end apart: 8, of which 4 were waited for; matrix products, arithmetic and copies ran while one was open for 0% of the time, Pallas kernels for 35%

profile of v6, /device:TPU:0, one launch (start us, length us, event | category | flops | bytes accessed | tf_op | source)
XLA Modules:
  0.0 40.2 jit_solution(16373065236201487057)
XLA Ops:
  0.6 3.0 %collective-permute-start = (bf16[1,4,32,768]{3,2,1,0:T(8,128)(2,1)}, bf16[1,4,32,768]{3,2,1,0:T(8,128)(2,1)S(1)}, u32[]{:S(2)}, u32[]{:S(2)}) collective-permute-start(bf16[1,4,32,768]{3,2,1,0:T(8,128)(2,1)} %refs_5_.3), channel_id=1, source_target_pairs={{0,2},{1,3},{2,0},{3,1},{4,6},{5,7},{6,4},{7,5},{8,10},{9,11},{10,... | collective-permute-start | bytes 589832 | tf_op jit(solution)/shard_map/ppermute | solution.py:333
  3.7 0.0 collective-permute-start.1
  3.7 5.8 %all-to-all-start = ((bf16[8,16,384]{2,1,0:T(8,128)(2,1)}), bf16[8,16,384]{2,1,0:T(8,128)(2,1)S(1)}, u32[]{:S(2)}, u32[]{:S(2)}) async-start(bf16[8,16,384]{2,1,0:T(8,128)(2,1)} %bitcast.9), calls=%async_computation | async-start | bytes 196608 | tf_op jit(solution)/shard_map/all_to_all | solution.py:336
  9.5 0.0 copy-start.6
  9.5 0.6 %copy-done.6 = s32[1,128,1]{1,2,0:T(1,128)S(1)} copy-done((s32[1,128,1]{1,2,0:T(1,128)S(1)}, s32[1,128,1]{1,2,0:T(1,128)}, u32[]{:S(2)}) %copy-start.6) | copy-done | bytes 536
  10.2 0.1 shard_map.125.refs_2_.refs_3_
  10.3 6.4 %all-to-all-done = bf16[8,16,384]{2,1,0:T(8,128)(2,1)S(1)} async-done(((bf16[8,16,384]{2,1,0:T(8,128)(2,1)}), bf16[8,16,384]{2,1,0:T(8,128)(2,1)S(1)}, u32[]{:S(2)}, u32[]{:S(2)}) %all-to-all-start) | async-done | bytes 98336 | tf_op jit(solution)/shard_map/all_to_all | solution.py:336
  16.7 0.0 copy-start
  16.7 0.0 copy-start.1
  16.7 0.0 copy-start.5
  16.7 2.7 %shard_map.126 = (bf16[2,32,3072]{2,1,0:T(8,128)(2,1)S(1)}, bf16[2,32,3072]{2,1,0:T(8,128)(2,1)S(1)}, bf16[3072,384]{1,0:T(8,128)(2,1)S(1)}, bf16[768,768]{1,0:T(8,128)(2,1)S(1)}) custom-call(s32[1]{0:T(128)} %bitcast.refs_0_, bf16[128,384]{1,0:T(8,128)(2,1)S(1)} %bitcast.6, bf16[128,128]{1,0:T(8,128)(2,1)S(1)} %shard_map.125.refs_2_.refs_3_, ...), custom_call_target="tpu_custom_call" | custom-call | flops 301989888 | bytes 4000000 | tf_op jit(solution)/shard_map/pallas_call | solution.py:39
  19.4 0.0 copy-start.2
  19.4 0.0 copy-start.3
  19.4 0.0 copy-start.4
  19.4 0.1 collective-permute-start.4
  19.5 0.0 collective-permute-done.refs_4_.refs_6_
  19.5 0.5 %collective-permute-start.2 = (bf16[1,4,32,768]{3,2,1,0:T(8,128)(2,1)S(1)}, bf16[1,4,32,768]{3,2,1,0:T(8,128)(2,1)S(1)}, u32[]{:S(2)}, u32[]{:S(2)}) collective-permute-start(bf16[1,4,32,768]{3,2,1,0:T(8,128)(2,1)S(1)} %collective-permute-done.refs_4_.refs_6_), channel_id=1, source_target_pairs={{0,1},{1,0},{2,3},{3,2},{4,5},{5,4},{6,7},{7,6},{8,9},{9,8},{10,11... | collective-permute-start | bytes 589832 | tf_op jit(solution)/shard_map/ppermute | solution.py:333
  20.0 0.0 copy-done
  20.0 0.0 copy-done.1
  20.0 0.0 copy-done.5
  20.0 2.4 %shard_map.123 = (f32[256,768]{1,0:T(8,128)S(1)}, bf16[768,1536]{1,0:T(8,128)(2,1)S(1)}, bf16[1536,768]{1,0:T(8,128)(2,1)S(1)}) custom-call(f32[7,7,768]{2,1,0:T(8,128)S(1)} %copy-done.1, f32[768]{0:T(1024)S(1)} %copy-done.5, f32[8,128]{1,0:T(8,128)S(1)} %shard_map.122.refs_2_, bf16[1,4,32,768]{3,2,1,0:T(8,128)(2,1)S(1)} %copy-done, ...), custom_call_target="tpu_custom_call" | custom-call | flops 4000000000 | bytes 6000000 | tf_op jit(solution)/shard_map/pallas_call | solution.py:39
  22.4 0.0 collective-permute-done.1.refs_3_
  22.4 0.0 collective-permute-done.2.refs_4_
  22.4 0.0 copy-done.2
  22.5 0.0 copy-done.3
  22.5 0.0 copy-done.4
  22.5 3.5 %shard_map.124 = (bf16[2,32,3072]{2,1,0:T(8,128)(2,1)S(1)}, bf16[128,1536]{1,0:T(8,128)(2,1)S(1)}, bf16[128,768]{1,0:T(8,128)(2,1)S(1)}, bf16[128,768]{1,0:T(8,128)(2,1)S(1)}, f32[128,256]{1,0:T(8,128)S(1)}) custom-call(s32[1]{0:T(128)} %bitcast.refs_0_, f32[256,768]{1,0:T(8,128)S(1)} %get-tuple-element.16.refs_1_, f32[7,7,768]{2,1,0:T(8,128)S(1)} %copy-done.1, ...), custom_call_target="tpu_custom_call" | custom-call | flops 1207959552 | bytes 9000000 | tf_op jit(solution)/shard_map/pallas_call | solution.py:39
  26.0 0.1 collective-permute-start.3
  26.1 0.0 collective-permute-done.4.refs_2_
  26.1 0.1 shard_map.128
  26.2 0.6 %collective-permute-start.5 = (bf16[32,3072]{1,0:T(8,128)(2,1)S(1)}, bf16[32,3072]{1,0:T(8,128)(2,1)S(1)}, u32[]{:S(2)}, u32[]{:S(2)}) collective-permute-start(bf16[32,3072]{1,0:T(8,128)(2,1)S(1)} %get-tuple-element.24), channel_id=1, source_target_pairs={{0,2},{1,3},{2,0},{3,1},{4,6},{5,7},{6,4},{7,5},{8,10},{9,11},{10,... | collective-permute-start | bytes 589832 | tf_op jit(solution)/shard_map/ppermute | solution.py:333
  26.8 1.0 %collective-permute-done.3.refs_2_ = bf16[2,32,3072]{2,1,0:T(8,128)(2,1)S(1)} collective-permute-done((bf16[2,32,3072]{2,1,0:T(8,128)(2,1)S(1)}, bf16[2,32,3072]{2,1,0:T(8,128)(2,1)S(1)}, u32[]{:S(2)}, u32[]{:S(2)}) %collective-permute-start.3) | collective-permute-done | bytes 393248 | tf_op jit(solution)/shard_map/ppermute | solution.py:333
  27.8 1.4 %shard_map.127 = bf16[128,384]{1,0:T(8,128)(2,1)} custom-call(s32[1]{0:T(128)} %bitcast.refs_0_, bf16[2,32,3072]{2,1,0:T(8,128)(2,1)S(1)} %get-tuple-element.19.refs_1_, bf16[2,32,3072]{2,1,0:T(8,128)(2,1)S(1)} %collective-permute-done.3.refs_2_, bf16[128,128]{1,0:T(8,128)(2,1)S(1)} %shard_map.125.refs_2_.refs_3_, ...), custom_call_target="tpu_custom_call" | custom-call | flops 301989888 | bytes 4000000 | tf_op jit(solution)/shard_map/pallas_call | solution.py:39
  29.2 3.4 %all-to-all-start.1 = ((bf16[8,16,384]{2,1,0:T(8,128)(2,1)}), bf16[8,16,384]{2,1,0:T(8,128)(2,1)S(1)}, u32[]{:S(2)}, u32[]{:S(2)}) async-start(bf16[8,16,384]{2,1,0:T(8,128)(2,1)} %bitcast.4), calls=%async_computation.1 | async-start | bytes 196608 | tf_op jit(solution)/shard_map/all_to_all | solution.py:336
  32.5 1.0 %collective-permute-done.5.refs_1_ = bf16[32,3072]{1,0:T(8,128)(2,1)S(1)} collective-permute-done((bf16[32,3072]{1,0:T(8,128)(2,1)S(1)}, bf16[32,3072]{1,0:T(8,128)(2,1)S(1)}, u32[]{:S(2)}, u32[]{:S(2)}) %collective-permute-start.5) | collective-permute-done | bytes 196640 | tf_op jit(solution)/shard_map/ppermute | solution.py:333
  33.5 3.9 %shard_map.129 = bf16[1,4,32,768]{3,2,1,0:T(8,128)(2,1)} custom-call(f32[32,3072]{1,0:T(8,128)S(1)} %get-tuple-element.23.refs_0_, bf16[32,3072]{1,0:T(8,128)(2,1)S(1)} %collective-permute-done.5.refs_1_, bf16[128,1536]{1,0:T(8,128)(2,1)S(1)} %get-tuple-element.25.refs_2_, bf16[128,768]{1,0:T(8,128)(2,1)S(1)} %get-tuple-element.26.refs_3_, ...), custom_call_target="tpu_custom_call" | custom-call | flops 603979776 | bytes 9000000 | tf_op jit(solution)/shard_map/pallas_call | solution.py:39
  37.4 2.2 %all-to-all-done.1 = bf16[8,16,384]{2,1,0:T(8,128)(2,1)S(1)} async-done(((bf16[8,16,384]{2,1,0:T(8,128)(2,1)}), bf16[8,16,384]{2,1,0:T(8,128)(2,1)S(1)}, u32[]{:S(2)}, u32[]{:S(2)}) %all-to-all-start.1) | async-done | bytes 98336 | tf_op jit(solution)/shard_map/all_to_all | solution.py:336
  39.6 0.6 %copy.14 = bf16[1,128,384]{2,1,0:T(8,128)(2,1)} copy(bf16[1,128,384]{2,1,0:T(8,128)(2,1)S(1)} %bitcast.8) | data formatting | bytes 196608
  (1 shorter events, 0.0 us)
Async XLA Ops:
  0.6 18.9 %collective-permute-start = (bf16[1,4,32,768]{3,2,1,0:T(8,128)(2,1)}, bf16[1,4,32,768]{3,2,1,0:T(8,128)(2,1)S(1)}, u32[]{:S(2)}, u32[]{:S(2)}) collective-permute-start(bf16[1,4,32,768]{3,2,1,0:T(8,128)(2,1)} %refs_5_.3), channel_id=1, source_target_pairs={{0,2},{1,3},{2,0},{3,1},{4,6},{5,7},{6,4},{7,5},{8,10},{9,11},{10,... | collective-permute-start | bytes 589832 | tf_op jit(solution)/shard_map/ppermute | solution.py:333
  3.7 18.8 %collective-permute-start.1 = (bf16[1,4,32,768]{3,2,1,0:T(8,128)(2,1)}, bf16[1,4,32,768]{3,2,1,0:T(8,128)(2,1)S(1)}, u32[]{:S(2)}, u32[]{:S(2)}) collective-permute-start(bf16[1,4,32,768]{3,2,1,0:T(8,128)(2,1)} %refs_5_.3), channel_id=1, source_target_pairs={{0,1},{1,0},{2,3},{3,2},{4,5},{5,4},{6,7},{7,6},{8,9},{9,8},{10,11... | collective-permute-start | bytes 589832 | tf_op jit(solution)/shard_map/ppermute | solution.py:333
  3.7 13.0 %all-to-all-start = ((bf16[8,16,384]{2,1,0:T(8,128)(2,1)}), bf16[8,16,384]{2,1,0:T(8,128)(2,1)S(1)}, u32[]{:S(2)}, u32[]{:S(2)}) async-start(bf16[8,16,384]{2,1,0:T(8,128)(2,1)} %bitcast.9), calls=%async_computation | async-start | bytes 196608 | tf_op jit(solution)/shard_map/all_to_all | solution.py:336
  9.5 0.7 %copy-start.6 = (s32[1,128,1]{1,2,0:T(1,128)S(1)}, s32[1,128,1]{1,2,0:T(1,128)}, u32[]{:S(2)}) copy-start(s32[1,128,1]{1,2,0:T(1,128)} %param.20) | copy-start | bytes 1540
  16.7 3.3 %copy-start = (bf16[1,4,32,768]{3,2,1,0:T(8,128)(2,1)S(1)}, bf16[1,4,32,768]{3,2,1,0:T(8,128)(2,1)}, u32[]{:S(2)}) copy-start(bf16[1,4,32,768]{3,2,1,0:T(8,128)(2,1)} %refs_5_.3) | copy-start | bytes 589828
  16.7 3.3 %copy-start.1 = (f32[7,7,768]{2,1,0:T(8,128)S(1)}, f32[7,7,768]{2,1,0:T(8,128)}, u32[]{:S(2)}) copy-start(f32[7,7,768]{2,1,0:T(8,128)} %refs_2_.1) | copy-start | bytes 451588
  16.7 3.4 %copy-start.5 = (f32[768]{0:T(1024)S(1)}, f32[768]{0:T(1024)}, u32[]{:S(2)}) copy-start(f32[768]{0:T(1024)} %refs_1_.1) | copy-start | bytes 9220
  19.4 3.0 %copy-start.2 = (f32[768]{0:T(1024)S(1)}, f32[768]{0:T(1024)}, u32[]{:S(2)}) copy-start(f32[768]{0:T(1024)} %refs_9_.3) | copy-start | bytes 9220
  19.4 3.0 %copy-start.3 = (f32[768]{0:T(1024)S(1)}, f32[768]{0:T(1024)}, u32[]{:S(2)}) copy-start(f32[768]{0:T(1024)} %refs_8_.3) | copy-start | bytes 9220
  19.4 3.0 %copy-start.4 = (f32[768]{0:T(1024)S(1)}, f32[768]{0:T(1024)}, u32[]{:S(2)}) copy-start(f32[768]{0:T(1024)} %refs_7_.3) | copy-start | bytes 9220
  19.4 6.7 %collective-permute-start.4 = (bf16[2,32,3072]{2,1,0:T(8,128)(2,1)S(1)}, bf16[2,32,3072]{2,1,0:T(8,128)(2,1)S(1)}, u32[]{:S(2)}, u32[]{:S(2)}) collective-permute-start(bf16[2,32,3072]{2,1,0:T(8,128)(2,1)S(1)} %get-tuple-element.22), channel_id=1, source_target_pairs={{0,1},{1,0},{2,3},{3,2},{4,5},{5,4},{6,7},{7,6},{8,9},{9,8},{10,11... | collective-permute-start | bytes 1179656 | tf_op jit(solution)/shard_map/ppermute | solution.py:333
  19.5 2.9 %collective-permute-start.2 = (bf16[1,4,32,768]{3,2,1,0:T(8,128)(2,1)S(1)}, bf16[1,4,32,768]{3,2,1,0:T(8,128)(2,1)S(1)}, u32[]{:S(2)}, u32[]{:S(2)}) collective-permute-start(bf16[1,4,32,768]{3,2,1,0:T(8,128)(2,1)S(1)} %collective-permute-done.refs_4_.refs_6_), channel_id=1, source_target_pairs={{0,1},{1,0},{2,3},{3,2},{4,5},{5,4},{6,7},{7,6},{8,9},{9,8},{10,11... | collective-permute-start | bytes 589832 | tf_op jit(solution)/shard_map/ppermute | solution.py:333
  26.0 1.8 %collective-permute-start.3 = (bf16[2,32,3072]{2,1,0:T(8,128)(2,1)S(1)}, bf16[2,32,3072]{2,1,0:T(8,128)(2,1)S(1)}, u32[]{:S(2)}, u32[]{:S(2)}) collective-permute-start(bf16[2,32,3072]{2,1,0:T(8,128)(2,1)S(1)} %get-tuple-element.19.refs_1_), channel_id=1, source_target_pairs={{0,1},{1,0},{2,3},{3,2},{4,5},{5,4},{6,7},{7,6},{8,9},{9,8},{10,11... | collective-permute-start | bytes 1179656 | tf_op jit(solution)/shard_map/ppermute | solution.py:333
  26.2 7.3 %collective-permute-start.5 = (bf16[32,3072]{1,0:T(8,128)(2,1)S(1)}, bf16[32,3072]{1,0:T(8,128)(2,1)S(1)}, u32[]{:S(2)}, u32[]{:S(2)}) collective-permute-start(bf16[32,3072]{1,0:T(8,128)(2,1)S(1)} %get-tuple-element.24), channel_id=1, source_target_pairs={{0,2},{1,3},{2,0},{3,1},{4,6},{5,7},{6,4},{7,5},{8,10},{9,11},{10,... | collective-permute-start | bytes 589832 | tf_op jit(solution)/shard_map/ppermute | solution.py:333
  29.2 10.4 %all-to-all-start.1 = ((bf16[8,16,384]{2,1,0:T(8,128)(2,1)}), bf16[8,16,384]{2,1,0:T(8,128)(2,1)S(1)}, u32[]{:S(2)}, u32[]{:S(2)}) async-start(bf16[8,16,384]{2,1,0:T(8,128)(2,1)} %bitcast.4), calls=%async_computation.1 | async-start | bytes 196608 | tf_op jit(solution)/shard_map/all_to_all | solution.py:336

commit v7 on v6

--- a/solution.py
+++ b/solution.py
@@ -119,10 +119,11 @@
 def forward_body(rows, width, channels, hidden, block, chips, place, part_ref, kernel_ref, *rest):
     mates, bands = rest[:chips], rest[chips : 2 * chips]
     (
-        gain_ref, scale_ref, down_gain_ref, w1_ref, w2_ref,
-        patch_ref, slope_ref, n1_ref, n2_ref, inv_ref,
-        padded, mixed, first, active, acc, grid,
+        gain_ref, scale_ref, down_gain_ref, w1_ref, w2_ref, w3_hbm,
+        patch_ref, slope_ref, n1_ref, n2_ref, inv_ref, w3_ref,
+        padded, mixed, first, active, acc, grid, sems,
     ) = rest[2 * chips :]
+    loads = fetch(((w3_hbm.at[pl.ds(0, w3_ref.shape[0])], w3_ref),), sems)
     chip, odd = place[0] // 2, place[0] % 2 == 1
     chunks = channels // LANES
     count = rows * width
@@ -187,6 +188,7 @@
                     patch_ref[q, r * half : (r + 1) * half, (2 * a + b) * channels : (2 * a + b + 1) * channels] = (
                         piece.astype(BF16)
                     )
+    wait(loads)
 
 
 def index_body(owners, capacity, table_ref, pick_ref):
@@ -206,14 +208,15 @@
 
 def pull_body(
     spaces, step,
-    place, returned_ref, pick_ref, w_hbm, w2_hbm,
-    keep_ref, send_ref, w_ref, w2_ref,
+    place, returned_ref, pick_ref, low_ref, w_hbm, w2_hbm,
+    keep_ref, send_ref, high_ref, w2_ref,
     wanted, both, sems,
 ):
-    depth = w_ref.shape[0]
-    low, high = pl.ds(0, depth // 2), pl.ds(depth // 2, depth // 2)
-    loads = fetch(((w_hbm.at[low], w_ref.at[low]), (w_hbm.at[high], w_ref.at[high])), sems)
+    third = low_ref.shape[0]
+    parts = [(pl.ds(i * third, third), pl.ds((i - 1) * third, third)) for i in (1, 2)]
+    loads = fetch([(w_hbm.at[a], high_ref.at[b]) for a, b in parts], sems)
     late = pltpu.make_async_copy(w2_hbm.at[pl.ds(0, w2_ref.shape[0])], w2_ref, sems.at[2])
+    late.start()
     core = place[0] % 2
     band = both.shape[0] // spaces
     wanted[...] = (
@@ -225,13 +228,13 @@
     for i in range(chips):
         both[i * band : (i + 1) * band, :] = wanted[2 * i + core]
         both[(chips + i) * band : (chips + i + 1) * band, :] = wanted[2 * i + 1 - core]
-    for d in range(0, depth, step):
-        if d == 0:
+    for d in range(0, 3 * third, step):
+        if d == third:
             loads[0].wait()
-            late.start()
-        if d == depth // 2:
+        if d == 2 * third:
             loads[1].wait()
-        part = nt(both[...], w_ref[d : d + step, :]).astype(BF16)
+        weight = low_ref[d : d + step, :] if d < third else high_ref[d - third : d - third + step, :]
+        part = nt(both[...], weight).astype(BF16)
         for i in range(chips):
             keep_ref[i, :, d : d + step] = part[i * band : (i + 1) * band]
             send_ref[i, :, d : d + step] = part[(chips + i) * band : (chips + i + 1) * band]
@@ -253,7 +256,7 @@
         out_hbm, out_ref, grid, scaled, active, acc, w1_ref, w2_far, in_sems, out_sems,
     ) = rest[chips - 1 :]
     split = w2_near.shape[0]
-    loads = fetch(((w2_hbm.at[pl.ds(split, split)], w2_far), (w1_hbm, w1_ref)), in_sems)
+    loads = fetch(((w2_hbm.at[pl.ds(split, hidden - split)], w2_far), (w1_hbm, w1_ref)), in_sems)
     half = width // 2
     chunks = channels // LANES
     for r in range(rows // 2):
@@ -293,13 +296,14 @@
     wait(stores)
 
 
-def push_body(chips, place, own_ref, mate_ref, pick_ref, w_ref, out_ref, patches, tokens):
+def push_body(chips, place, own_ref, mate_ref, pick_ref, low_ref, high_ref, out_ref, patches, tokens):
     chip, core = place[0] // 2, place[0] % 2
     band = own_ref.shape[1]
     for i in range(2 * chips):
         source_ref = own_ref if i % 2 == 0 else mate_ref
         patches[i * band : (i + 1) * band, :] = source_ref[i // 2]
-    result = nn(patches[...], w_ref[...]).astype(BF16)
+    third = low_ref.shape[0]
+    result = (nn(patches[:, :third], low_ref[...]) + nn(patches[:, third:], high_ref[...])).astype(BF16)
     for i in range(2 * chips):
         source = lax.rem(chip + chips - i // 2, chips)
         owner = 2 * source + (core if i % 2 == 0 else 1 - core)
@@ -325,7 +329,7 @@
     deep, narrow = w_down.shape
     place = lax.axis_index("space").astype(jnp.int32).reshape(1)
     lanes = channels // LANES
-    block, step = 256, 768
+    block, step = 256, 512
 
     swap = [(i, i ^ 1) for i in range(spaces)]
 
@@ -353,16 +357,17 @@
         [pltpu.VMEM((lanes, rows, width + 2 * LEFT, LANES), F32), pltpu.SemaphoreType.DMA((2,))],
         6, 4e9, 6e6,
     )
-    patches, slope, n1, n2, inv = call(
+    patches, slope, n1, n2, inv, w_low = call(
         lambda *refs: forward_body(rows, width, channels, hidden, block, chips, *refs),
-        (place, *close(part, dw_kernel, *mates, *bands, mix_gain, layer_scale, down_gain, w1_near, w2_whole)),
-        [SMEM] + [VMEM] * (7 + 2 * chips),
+        (place, *close(part, dw_kernel, *mates, *bands, mix_gain, layer_scale, down_gain, w1_near, w2_whole),
+         *far_off(w_down)),
+        [SMEM] + [VMEM] * (7 + 2 * chips) + [HBM],
         [((chips, band, 4 * channels), BF16), ((count, hidden), BF16), ((count, channels), BF16),
-         ((count, channels), BF16), ((count, 2 * LANES), F32)],
+         ((count, channels), BF16), ((count, 2 * LANES), F32), ((deep // 3, narrow), BF16)],
         [pltpu.VMEM((lanes, 2 * HALF, width + 2 * LEFT, LANES), F32),
          pltpu.VMEM((wide, channels), F32), pltpu.VMEM((wide, channels), BF16),
          pltpu.VMEM((wide, hidden), BF16), pltpu.VMEM((wide, channels), F32),
-         pltpu.VMEM((lanes, wide, LANES), F32)],
+         pltpu.VMEM((lanes, wide, LANES), F32), pltpu.SemaphoreType.DMA((1,))],
         20, 4 * wide * channels * hidden, 9e6,
     )
     mate_patches = send(patches, swap)
@@ -371,12 +376,12 @@
         close(owner_table.reshape(1, tokens)), [VMEM],
         [((slots, tokens), BF16)], [], 2, 1e7, 1e5,
     )
-    keep, give, w_near, w2_near = call(
+    keep, give, w_high, w2_near = call(
         lambda *refs: pull_body(spaces, step, *refs),
-        (place, *close(returned, pick), *far_off(w_down, w_reduce)),
-        [SMEM] + [VMEM] * 2 + [HBM] * 2,
-        [((chips, band, deep), BF16), ((chips, band, deep), BF16), (w_down.shape, BF16),
-         ((hidden // 2, channels), BF16)],
+        (place, *close(returned, pick, w_low), *far_off(w_down, w_reduce)),
+        [SMEM] + [VMEM] * 3 + [HBM] * 2,
+        [((chips, band, deep), BF16), ((chips, band, deep), BF16), ((deep - deep // 3, narrow), BF16),
+         ((hidden // 3, channels), BF16)],
         [pltpu.VMEM((spaces, band, narrow), BF16), pltpu.VMEM((tokens, narrow), BF16),
          pltpu.SemaphoreType.DMA((3,))],
         6, 2 * tokens * deep * narrow, 4e6,
@@ -390,8 +395,8 @@
     across = [send(sums[j - 1], onward(j)) for j in range(1, chips)]
     (buffer,) = call(
         lambda *refs: push_body(chips, *refs),
-        (place, *close(patches, mate_patches, pick, w_near)),
-        [SMEM] + [VMEM] * 4,
+        (place, *close(patches, mate_patches, pick, w_low, w_high)),
+        [SMEM] + [VMEM] * 5,
         [((slots, narrow), BF16)],
         [pltpu.VMEM((tokens, deep), BF16), pltpu.VMEM((spaces, band, narrow), BF16)],
         6, 2 * tokens * deep * narrow, 4e6,
@@ -406,7 +411,7 @@
         [pltpu.VMEM(section_three.shape, BF16), pltpu.VMEM((lanes, count, LANES), F32),
          pltpu.VMEM((count, channels), BF16), pltpu.VMEM((count, hidden), BF16),
          pltpu.VMEM((count, channels), F32),
-         pltpu.VMEM(w_expand.shape, BF16), pltpu.VMEM((hidden // 2, channels), BF16),
+         pltpu.VMEM(w_expand.shape, BF16), pltpu.VMEM((hidden - hidden // 3, channels), BF16),
          pltpu.SemaphoreType.DMA((2,)), pltpu.SemaphoreType.DMA((rows,))],
         16, 4 * count * channels * hidden, 9e6,
     )

time: 40.6 us -> 39.7 us (0.978)
  blocking collectives: 0 us -> 12.7 us
  waiting for transfers between devices: 10.5 us -> 1.34 us
  starting transfers between devices: 13.5 us -> 10.3 us
  Pallas kernels: 14.1 us -> 13 us
    all_to_all x0 -> x1, blocking collectives: none -> 12.7 us  [trade(): return lax.all_to_all(value, 'dp', split_axis=0, concat_axis=0, tiled=True)]
    all_to_all x2 -> x1, waiting for transfers between devices: 8.52 us -> 0.11 us  [trade(): return lax.all_to_all(value, 'dp', split_axis=0, concat_axis=0, tiled=True)]
    all_to_all x2 -> x1, starting transfers between devices: 9.2 us -> 5.83 us  [trade(): return lax.all_to_all(value, 'dp', split_axis=0, concat_axis=0, tiled=True)]
    pallas_call x8, Pallas kernels: 14.1 us -> 13 us  [call(): pl.pallas_call(body, in_specs=specs, out_shape=tuple((pltpu.VMEM(*o) if i...]
    ppermute x6, waiting for transfers between devices: 1.97 us -> 1.23 us  [send(): return lax.ppermute(value, 'space', pairs)]
  transfers between devices with their start and end apart: 8 -> 7, of which waited for: 4 -> 2; matrix products, arithmetic and copies ran while one was open for 0% -> 0% of each run, Pallas kernels for 35% -> 17%
where the time goes in v7:
time: 39.7 us; the launch traced here: 39.4 us
  Pallas kernels  13 us (33%)
  blocking collectives  12.7 us (32%)
  starting transfers between devices  10.3 us (26%)
  waiting for transfers between devices  1.34 us (3%)
  local copies, waits for them, and re-layouts  1.28 us (3%)
  between operations  0.8 us (2%)
    pallas_call x8, Pallas kernels, call(): pl.pallas_call(body, in_specs=specs, out_shape=tuple((pltpu.VMEM(*o) if i...  13 us
    all_to_all x1, blocking collectives, trade(): return lax.all_to_all(value, 'dp', split_axis=0, concat_axis=0, tiled=True)  12.7 us
    all_to_all x1, starting transfers between devices, trade(): return lax.all_to_all(value, 'dp', split_axis=0, concat_axis=0, tiled=True)  5.83 us
    ppermute x6, starting transfers between devices, send(): return lax.ppermute(value, 'space', pairs)  4.5 us
    unnamed x15, local copies, waits for them, and re-layouts  1.28 us
    ppermute x6, waiting for transfers between devices, send(): return lax.ppermute(value, 'space', pairs)  1.23 us
  transfers between devices with their start and end apart: 7, of which 2 were waited for; matrix products, arithmetic and copies ran while one was open for 0% of the time, Pallas kernels for 17%

profile of v7, /device:TPU:0, one launch (start us, length us, event | category | flops | bytes accessed | tf_op | source)
XLA Modules:
  0.0 39.4 jit_solution(12952238110810329549)
XLA Ops:
  0.6 3.0 %collective-permute-start = (bf16[1,4,32,768]{3,2,1,0:T(8,128)(2,1)}, bf16[1,4,32,768]{3,2,1,0:T(8,128)(2,1)S(1)}, u32[]{:S(2)}, u32[]{:S(2)}) collective-permute-start(bf16[1,4,32,768]{3,2,1,0:T(8,128)(2,1)} %refs_5_.4), channel_id=1, source_target_pairs={{0,2},{1,3},{2,0},{3,1},{4,6},{5,7},{6,4},{7,5},{8,10},{9,11},{10,... | collective-permute-start | bytes 589832 | tf_op jit(solution)/shard_map/ppermute | solution.py:337
  3.7 0.0 collective-permute-start.1
  3.7 5.8 %all-to-all-start = ((bf16[8,16,384]{2,1,0:T(8,128)(2,1)}), bf16[8,16,384]{2,1,0:T(8,128)(2,1)S(1)}, u32[]{:S(2)}, u32[]{:S(2)}) async-start(bf16[8,16,384]{2,1,0:T(8,128)(2,1)} %bitcast.10), calls=%async_computation | async-start | bytes 196608 | tf_op jit(solution)/shard_map/all_to_all | solution.py:340
  9.5 0.0 copy-start.6
  9.5 0.0 copy-start
  9.5 0.0 copy-start.1
  9.5 0.0 copy-start.5
  9.6 0.6 %copy-done.6 = s32[1,128,1]{1,2,0:T(1,128)S(1)} copy-done((s32[1,128,1]{1,2,0:T(1,128)S(1)}, s32[1,128,1]{1,2,0:T(1,128)}, u32[]{:S(2)}) %copy-start.6) | copy-done | bytes 536
  10.2 0.1 shard_map.125.refs_2_.refs_3_
  10.3 0.0 copy-start.2
  10.3 0.0 copy-start.3
  10.3 0.0 copy-start.4
  10.3 0.0 collective-permute-done.refs_4_.refs_6_
  10.4 0.3 collective-permute-start.2
  10.7 0.0 copy-done
  10.7 0.0 copy-done.1
  10.7 0.0 copy-done.5
  10.7 2.4 %shard_map.123 = (f32[256,768]{1,0:T(8,128)S(1)}, bf16[768,1536]{1,0:T(8,128)(2,1)S(1)}, bf16[1536,768]{1,0:T(8,128)(2,1)S(1)}) custom-call(f32[7,7,768]{2,1,0:T(8,128)S(1)} %copy-done.1, f32[768]{0:T(1024)S(1)} %copy-done.5, f32[8,128]{1,0:T(8,128)S(1)} %shard_map.122.refs_2_, bf16[1,4,32,768]{3,2,1,0:T(8,128)(2,1)S(1)} %copy-done, ...), custom_call_target="tpu_custom_call" | custom-call | flops 4000000000 | bytes 6000000 | tf_op jit(solution)/shard_map/pallas_call | solution.py:39
  13.1 0.0 collective-permute-done.1.refs_3_
  13.1 0.0 collective-permute-done.2.refs_4_
  13.1 0.0 copy-done.2
  13.1 0.0 copy-done.3
  13.1 0.0 copy-done.4
  13.1 3.4 %shard_map.124 = (bf16[2,32,3072]{2,1,0:T(8,128)(2,1)S(1)}, bf16[128,1536]{1,0:T(8,128)(2,1)S(1)}, bf16[128,768]{1,0:T(8,128)(2,1)S(1)}, bf16[128,768]{1,0:T(8,1...) custom-call(s32[1]{0:T(128)} %bitcast.refs_0_, f32[256,768]{1,0:T(8,128)S(1)} %get-tuple-element.17.refs_1_, ...), custom_call_target="tpu_custom_call" | custom-call | flops 1207959552 | bytes 9000000 | tf_op jit(solution)/shard_map/pallas_call | solution.py:39
  16.6 0.1 all-to-all-done
  16.7 2.0 %shard_map.126 = (bf16[2,32,3072]{2,1,0:T(8,128)(2,1)S(1)}, bf16[2,32,3072]{2,1,0:T(8,128)(2,1)S(1)}, bf16[2048,384]{1,0:T(8,128)(2,1)S(1)}, bf16[512,768]{1,0:T(8,128)(2,1)S(1)}) custom-call(s32[1]{0:T(128)} %bitcast.refs_0_, bf16[128,384]{1,0:T(8,128)(2,1)S(1)} %bitcast.7, bf16[128,128]{1,0:T(8,128)(2,1)S(1)} %shard_map.125.refs_2_.refs_3_, ...), custom_call_target="tpu_custom_call" | custom-call | flops 301989888 | bytes 4000000 | tf_op jit(solution)/shard_map/pallas_call | solution.py:39
  18.6 0.3 collective-permute-start.4
  18.9 0.3 collective-permute-start.3
  19.2 1.2 %collective-permute-done.4.refs_2_ = bf16[2,32,3072]{2,1,0:T(8,128)(2,1)S(1)} collective-permute-done((bf16[2,32,3072]{2,1,0:T(8,128)(2,1)S(1)}, bf16[2,32,3072]{2,1,0:T(8,128)(2,1)S(1)}, u32[]{:S(2)}, u32[]{:S(2)}) %collective-permute-start.4) | collective-permute-done | bytes 393248 | tf_op jit(solution)/shard_map/ppermute | solution.py:337
  20.4 0.1 shard_map.128
  20.5 0.6 %collective-permute-start.5 = (bf16[32,3072]{1,0:T(8,128)(2,1)S(1)}, bf16[32,3072]{1,0:T(8,128)(2,1)S(1)}, u32[]{:S(2)}, u32[]{:S(2)}) collective-permute-start(bf16[32,3072]{1,0:T(8,128)(2,1)S(1)} %get-tuple-element.26), channel_id=1, source_target_pairs={{0,2},{1,3},{2,0},{3,1},{4,6},{5,7},{6,4},{7,5},{8,10},{9,11},{10,... | collective-permute-start | bytes 589832 | tf_op jit(solution)/shard_map/ppermute | solution.py:337
  21.1 0.0 collective-permute-done.3.refs_2_
  21.1 0.8 %shard_map.127 = bf16[128,384]{1,0:T(8,128)(2,1)S(1)} custom-call(s32[1]{0:T(128)} %bitcast.refs_0_, bf16[2,32,3072]{2,1,0:T(8,128)(2,1)S(1)} %get-tuple-element.20.refs_1_, bf16[2,32,3072]{2,1,0:T(8,128)(2,1)S(1)} %collective-permute-done.3.refs_2_, bf16[128,128]{1,0:T(8,128)(2,1)S(1)} %shard_map.125.refs_2_.refs_3_, ...), custom_call_target="tpu_custom_call" | custom-call | flops 301989888 | bytes 4000000 | tf_op jit(solution)/shard_map/pallas_call | solution.py:39
  21.9 12.7 %all_to_all.20 = bf16[8,16,384]{2,1,0:T(8,128)(2,1)S(1)} all-to-all(bf16[8,16,384]{2,1,0:T(8,128)(2,1)S(1)} %bitcast.6), channel_id=1, replica_groups=mesh['dp'=8,'space'=4] {'dp'}, dimensions={0} | all-to-all | bytes 196608 | tf_op jit(solution)/shard_map/all_to_all | solution.py:340
  34.6 0.0 collective-permute-done.5.refs_1_
  34.6 4.2 %shard_map.129 = bf16[1,4,32,768]{3,2,1,0:T(8,128)(2,1)} custom-call(f32[32,3072]{1,0:T(8,128)S(1)} %get-tuple-element.25.refs_0_, bf16[32,3072]{1,0:T(8,128)(2,1)S(1)} %collective-permute-done.5.refs_1_, bf16[128,1536]{1,0:T(8,128)(2,1)S(1)} %get-tuple-element.27.refs_2_, bf16[128,768]{1,0:T(8,128)(2,1)S(1)} %get-tuple-element.28.refs_3_, ...), custom_call_target="tpu_custom_call" | custom-call | flops 603979776 | bytes 9000000 | tf_op jit(solution)/shard_map/pallas_call | solution.py:39
  38.8 0.6 %copy.14 = bf16[1,128,384]{2,1,0:T(8,128)(2,1)} copy(bf16[1,128,384]{2,1,0:T(8,128)(2,1)S(1)} %bitcast.9) | data formatting | bytes 196608
  (1 shorter events, 0.0 us)
Async XLA Ops:
  0.6 9.7 %collective-permute-start = (bf16[1,4,32,768]{3,2,1,0:T(8,128)(2,1)}, bf16[1,4,32,768]{3,2,1,0:T(8,128)(2,1)S(1)}, u32[]{:S(2)}, u32[]{:S(2)}) collective-permute-start(bf16[1,4,32,768]{3,2,1,0:T(8,128)(2,1)} %refs_5_.4), channel_id=1, source_target_pairs={{0,2},{1,3},{2,0},{3,1},{4,6},{5,7},{6,4},{7,5},{8,10},{9,11},{10,... | collective-permute-start | bytes 589832 | tf_op jit(solution)/shard_map/ppermute | solution.py:337
  3.7 9.4 %collective-permute-start.1 = (bf16[1,4,32,768]{3,2,1,0:T(8,128)(2,1)}, bf16[1,4,32,768]{3,2,1,0:T(8,128)(2,1)S(1)}, u32[]{:S(2)}, u32[]{:S(2)}) collective-permute-start(bf16[1,4,32,768]{3,2,1,0:T(8,128)(2,1)} %refs_5_.4), channel_id=1, source_target_pairs={{0,1},{1,0},{2,3},{3,2},{4,5},{5,4},{6,7},{7,6},{8,9},{9,8},{10,11... | collective-permute-start | bytes 589832 | tf_op jit(solution)/shard_map/ppermute | solution.py:337
  3.7 13.0 %all-to-all-start = ((bf16[8,16,384]{2,1,0:T(8,128)(2,1)}), bf16[8,16,384]{2,1,0:T(8,128)(2,1)S(1)}, u32[]{:S(2)}, u32[]{:S(2)}) async-start(bf16[8,16,384]{2,1,0:T(8,128)(2,1)} %bitcast.10), calls=%async_computation | async-start | bytes 196608 | tf_op jit(solution)/shard_map/all_to_all | solution.py:340
  9.5 0.7 %copy-start.6 = (s32[1,128,1]{1,2,0:T(1,128)S(1)}, s32[1,128,1]{1,2,0:T(1,128)}, u32[]{:S(2)}) copy-start(s32[1,128,1]{1,2,0:T(1,128)} %param.20) | copy-start | bytes 1540
  9.5 1.1 %copy-start = (bf16[1,4,32,768]{3,2,1,0:T(8,128)(2,1)S(1)}, bf16[1,4,32,768]{3,2,1,0:T(8,128)(2,1)}, u32[]{:S(2)}) copy-start(bf16[1,4,32,768]{3,2,1,0:T(8,128)(2,1)} %refs_5_.4) | copy-start | bytes 589828
  9.5 1.1 %copy-start.1 = (f32[7,7,768]{2,1,0:T(8,128)S(1)}, f32[7,7,768]{2,1,0:T(8,128)}, u32[]{:S(2)}) copy-start(f32[7,7,768]{2,1,0:T(8,128)} %refs_2_.1) | copy-start | bytes 451588
  9.5 1.1 %copy-start.5 = (f32[768]{0:T(1024)S(1)}, f32[768]{0:T(1024)}, u32[]{:S(2)}) copy-start(f32[768]{0:T(1024)} %refs_1_.1) | copy-start | bytes 9220
  10.3 2.8 %copy-start.2 = (f32[768]{0:T(1024)S(1)}, f32[768]{0:T(1024)}, u32[]{:S(2)}) copy-start(f32[768]{0:T(1024)} %refs_9_.3) | copy-start | bytes 9220
  10.3 2.8 %copy-start.3 = (f32[768]{0:T(1024)S(1)}, f32[768]{0:T(1024)}, u32[]{:S(2)}) copy-start(f32[768]{0:T(1024)} %refs_8_.3) | copy-start | bytes 9220
  10.3 2.8 %copy-start.4 = (f32[768]{0:T(1024)S(1)}, f32[768]{0:T(1024)}, u32[]{:S(2)}) copy-start(f32[768]{0:T(1024)} %refs_7_.3) | copy-start | bytes 9220
  10.4 2.7 %collective-permute-start.2 = (bf16[1,4,32,768]{3,2,1,0:T(8,128)(2,1)S(1)}, bf16[1,4,32,768]{3,2,1,0:T(8,128)(2,1)S(1)}, u32[]{:S(2)}, u32[]{:S(2)}) collective-permute-start(bf16[1,4,32,768]{3,2,1,0:T(8,128)(2,1)S(1)} %collective-permute-done.refs_4_.refs_6_), channel_id=1, source_target_pairs={{0,1},{1,0},{2,3},{3,2},{4,5},{5,4},{6,7},{7,6},{8,9},{9,8},{10,11... | collective-permute-start | bytes 589832 | tf_op jit(solution)/shard_map/ppermute | solution.py:337
  18.6 1.8 %collective-permute-start.4 = (bf16[2,32,3072]{2,1,0:T(8,128)(2,1)S(1)}, bf16[2,32,3072]{2,1,0:T(8,128)(2,1)S(1)}, u32[]{:S(2)}, u32[]{:S(2)}) collective-permute-start(bf16[2,32,3072]{2,1,0:T(8,128)(2,1)S(1)} %get-tuple-element.24), channel_id=1, source_target_pairs={{0,1},{1,0},{2,3},{3,2},{4,5},{5,4},{6,7},{7,6},{8,9},{9,8},{10,11... | collective-permute-start | bytes 1179656 | tf_op jit(solution)/shard_map/ppermute | solution.py:337
  18.9 2.2 %collective-permute-start.3 = (bf16[2,32,3072]{2,1,0:T(8,128)(2,1)S(1)}, bf16[2,32,3072]{2,1,0:T(8,128)(2,1)S(1)}, u32[]{:S(2)}, u32[]{:S(2)}) collective-permute-start(bf16[2,32,3072]{2,1,0:T(8,128)(2,1)S(1)} %get-tuple-element.20.refs_1_), channel_id=1, source_target_pairs={{0,1},{1,0},{2,3},{3,2},{4,5},{5,4},{6,7},{7,6},{8,9},{9,8},{10,11... | collective-permute-start | bytes 1179656 | tf_op jit(solution)/shard_map/ppermute | solution.py:337
  20.5 14.1 %collective-permute-start.5 = (bf16[32,3072]{1,0:T(8,128)(2,1)S(1)}, bf16[32,3072]{1,0:T(8,128)(2,1)S(1)}, u32[]{:S(2)}, u32[]{:S(2)}) collective-permute-start(bf16[32,3072]{1,0:T(8,128)(2,1)S(1)} %get-tuple-element.26), channel_id=1, source_target_pairs={{0,2},{1,3},{2,0},{3,1},{4,6},{5,7},{6,4},{7,5},{8,10},{9,11},{10,... | collective-permute-start | bytes 589832 | tf_op jit(solution)/shard_map/ppermute | solution.py:337

commit v8 on v7

--- a/solution.py
+++ b/solution.py
@@ -93,37 +93,41 @@
     return total
 
 
-def conv_body(rows, width, channels, chips, kernel_ref, bias_ref, ready, *rest):
-    bands, (w1_hbm, w2_hbm, part_ref, w1_ref, w2_ref, padded, sems) = rest[:chips], rest[chips:]
-    loads = fetch(((w1_hbm, w1_ref), (w2_hbm, w2_ref)), sems)
+def conv_body(rows, width, channels, kernel_ref, bias_ref, ready, band_ref, *rest):
+    if len(rest) > 2:
+        w1_hbm, part_ref, w1_ref, padded, sems = rest
+        loads = fetch(((w1_hbm, w1_ref),), sems)
+    else:
+        (part_ref, padded), loads = rest, []
     chunks = channels // LANES
     cols = pl.ds(LEFT, width)
     padded[:, :, 0:LEFT, :] = jnp.zeros((chunks, rows, LEFT, LANES), F32)
     padded[:, :, LEFT + width :, :] = jnp.zeros((chunks, rows, LEFT, LANES), F32)
-    for q, band_ref in enumerate(bands):
-
-        def own(c, _):
-            at = pl.ds(pl.multiple_of(c * LANES, LANES), LANES)
-            padded[c, :, cols, :] = band_ref[0, :, :, at].astype(F32)
-            bias = jnp.broadcast_to(bias_ref[at].reshape(1, LANES), (width, LANES))
-            lines = range(HALF, HALF + rows)
-            total = convolve(padded, c, lambda r: r - HALF, lines, [bias] * rows, kernel_ref, at, rows, width)
-            for out in range(rows):
-                part_ref[pl.ds((q * rows + out) * width, width), at] = total[out]
-            return 0
-
-        lax.fori_loop(0, chunks, own, 0)
+
+    def own(c, _):
+        at = pl.ds(pl.multiple_of(c * LANES, LANES), LANES)
+        padded[c, :, cols, :] = band_ref[0, :, :, at].astype(F32)
+        bias = jnp.broadcast_to(bias_ref[at].reshape(1, LANES), (width, LANES))
+        lines = range(HALF, HALF + rows)
+        total = convolve(padded, c, lambda r: r - HALF, lines, [bias] * rows, kernel_ref, at, rows, width)
+        for out in range(rows):
+            part_ref[pl.ds(out * width, width), at] = total[out]
+        return 0
+
+    lax.fori_loop(0, chunks, own, 0)
     wait(loads)
 
 
-def forward_body(rows, width, channels, hidden, block, chips, place, part_ref, kernel_ref, *rest):
-    mates, bands = rest[:chips], rest[chips : 2 * chips]
+def forward_body(rows, width, channels, hidden, block, chips, place, kernel_ref, *rest):
+    parts, mates, bands = rest[:chips], rest[chips : 2 * chips], rest[2 * chips : 3 * chips]
     (
-        gain_ref, scale_ref, down_gain_ref, w1_ref, w2_ref, w3_hbm,
+        gain_ref, scale_ref, down_gain_ref, w1_ref, w2_hbm, w3_hbm,
         patch_ref, slope_ref, n1_ref, n2_ref, inv_ref, w3_ref,
-        padded, mixed, first, active, acc, grid, sems,
-    ) = rest[2 * chips :]
-    loads = fetch(((w3_hbm.at[pl.ds(0, w3_ref.shape[0])], w3_ref),), sems)
+        padded, mixed, first, active, acc, grid, w2_ref, sems,
+    ) = rest[3 * chips :]
+    pairs = ((w2_hbm, w2_ref), (w3_hbm.at[pl.ds(0, w3_ref.shape[0])], w3_ref))
+    loads = [pltpu.make_async_copy(src, dst, sems.at[i]) for i, (src, dst) in enumerate(pairs)]
+    loads[0].start()
     chip, odd = place[0] // 2, place[0] % 2 == 1
     chunks = channels // LANES
     count = rows * width
@@ -142,9 +146,10 @@
             padded[c, 0:HALF, cols, :] = jnp.where(odd, same[0, high, :, at].astype(F32), above)
             padded[c, HALF:, cols, :] = jnp.where(odd, below, same[0, low, :, at].astype(F32))
             spots = [pl.ds((q * rows + out) * width, width) for out in range(rows)]
+            begun = [parts[q][pl.ds(out * width, width), at] for out in range(rows)]
             lines = [r for r in range(rows + 2 * HALF) if not HALF <= r < HALF + rows]
             total = convolve(
-                padded, c, lambda r: r if r < HALF else r - rows, lines, [part_ref[p, at] for p in spots],
+                padded, c, lambda r: r if r < HALF else r - rows, lines, begun,
                 kernel_ref, at, rows, width,
             )
             for p, value in zip(spots, total):
@@ -152,6 +157,7 @@
             return 0
 
         lax.fori_loop(0, chunks, outer, 0)
+    start(loads[1:])
     gain = gain_ref[...].reshape(1, channels)
     for r in range(0, chips * count, width):
         n1, inv1 = normalize(mixed[r : r + width, :])
@@ -166,6 +172,7 @@
         density = jnp.exp(-0.5 * mine * mine) * 0.3989422804014327
         slope_ref[:, b : b + block] = (cumulative[:count] + mine * density).astype(BF16)
         active[:, b : b + block] = (pre * cumulative).astype(BF16)
+    loads[0].wait()
     for b in range(0, channels, block):
         acc[:, b : b + block] = nn(active[...], w2_ref[:, b : b + block])
     scale, gain = scale_ref[...].reshape(1, channels), down_gain_ref[...].reshape(1, channels)
@@ -188,7 +195,7 @@
                     patch_ref[q, r * half : (r + 1) * half, (2 * a + b) * channels : (2 * a + b + 1) * channels] = (
                         piece.astype(BF16)
                     )
-    wait(loads)
+    loads[1].wait()
 
 
 def index_body(owners, capacity, table_ref, pick_ref):
@@ -349,25 +356,30 @@
 
     mates = [near] + [send(bands[j], swap) for j in range(1, chips)]
     wide = chips * count
-    part, w1_near, w2_whole = call(
-        lambda *refs: conv_body(rows, width, channels, chips, *refs),
-        (*close(dw_kernel, dw_bias, ready, *bands), *far_off(w_expand, w_reduce)),
-        [VMEM] * (3 + chips) + [HBM] * 2,
-        [((wide, channels), F32), (w_expand.shape, BF16), (w_reduce.shape, BF16)],
-        [pltpu.VMEM((lanes, rows, width + 2 * LEFT, LANES), F32), pltpu.SemaphoreType.DMA((2,))],
-        6, 4e9, 6e6,
-    )
+    parts = []
+    for q, value in enumerate(bands):
+        parts += call(
+            lambda *refs: conv_body(rows, width, channels, *refs),
+            close(dw_kernel, dw_bias, ready, value) + (far_off(w_expand) if q == chips - 1 else ()),
+            [VMEM] * 4 + [HBM] * (q == chips - 1),
+            [((count, channels), F32)] + [(w_expand.shape, BF16)] * (q == chips - 1),
+            [pltpu.VMEM((lanes, rows, width + 2 * LEFT, LANES), F32)]
+            + [pltpu.SemaphoreType.DMA((1,))] * (q == chips - 1),
+            4, 2e9, 2e6,
+        )
+    w1_near = parts.pop()
     patches, slope, n1, n2, inv, w_low = call(
         lambda *refs: forward_body(rows, width, channels, hidden, block, chips, *refs),
-        (place, *close(part, dw_kernel, *mates, *bands, mix_gain, layer_scale, down_gain, w1_near, w2_whole),
-         *far_off(w_down)),
-        [SMEM] + [VMEM] * (7 + 2 * chips) + [HBM],
+        (place, *close(dw_kernel, *parts, *mates, *bands, mix_gain, layer_scale, down_gain, w1_near),
+         *far_off(w_reduce, w_down)),
+        [SMEM] + [VMEM] * (5 + 3 * chips) + [HBM] * 2,
         [((chips, band, 4 * channels), BF16), ((count, hidden), BF16), ((count, channels), BF16),
          ((count, channels), BF16), ((count, 2 * LANES), F32), ((deep // 3, narrow), BF16)],
         [pltpu.VMEM((lanes, 2 * HALF, width + 2 * LEFT, LANES), F32),
          pltpu.VMEM((wide, channels), F32), pltpu.VMEM((wide, channels), BF16),
          pltpu.VMEM((wide, hidden), BF16), pltpu.VMEM((wide, channels), F32),
-         pltpu.VMEM((lanes, wide, LANES), F32), pltpu.SemaphoreType.DMA((1,))],
+         pltpu.VMEM((lanes, wide, LANES), F32),
+         pltpu.VMEM(w_reduce.shape, BF16), pltpu.SemaphoreType.DMA((2,))],
         20, 4 * wide * channels * hidden, 9e6,
     )
     mate_patches = send(patches, swap)

time: 39.7 us -> 41.4 us (1.043)
  local copies, waits for them, and re-layouts: 1.28 us -> 2.11 us
  Pallas kernels: 13 us -> 13.5 us
    unnamed x15 -> x23, local copies, waits for them, and re-layouts: 1.28 us -> 2.11 us
    pallas_call x8 -> x9, Pallas kernels: 13 us -> 13.5 us  [call(): pl.pallas_call(body, in_specs=specs, out_shape=tuple((pltpu.VMEM(*o) if i...]
  transfers between devices with their start and end apart: 7 -> 7, of which waited for: 2 -> 1; matrix products, arithmetic and copies ran while one was open for 0% -> 0% of each run, Pallas kernels for 17% -> 18%
where the time goes in v8:
time: 41.4 us; the launch traced here: 41 us
  Pallas kernels  13.5 us (33%)
  blocking collectives  12.9 us (31%)
  starting transfers between devices  10.3 us (25%)
  local copies, waits for them, and re-layouts  2.11 us (5%)
  waiting for transfers between devices  1.23 us (3%)
  between operations  0.85 us (2%)
    pallas_call x9, Pallas kernels, call(): pl.pallas_call(body, in_specs=specs, out_shape=tuple((pltpu.VMEM(*o) if i...  13.5 us
    all_to_all x1, blocking collectives, trade(): return lax.all_to_all(value, 'dp', split_axis=0, concat_axis=0, tiled=True)  12.9 us
    all_to_all x1, starting transfers between devices, trade(): return lax.all_to_all(value, 'dp', split_axis=0, concat_axis=0, tiled=True)  5.83 us
    ppermute x6, starting transfers between devices, send(): return lax.ppermute(value, 'space', pairs)  4.5 us
    unnamed x23, local copies, waits for them, and re-layouts  2.11 us
    ppermute x6, waiting for transfers between devices, send(): return lax.ppermute(value, 'space', pairs)  1.23 us
  transfers between devices with their start and end apart: 7, of which 1 were waited for; matrix products, arithmetic and copies ran while one was open for 0% of the time, Pallas kernels for 18%

profile of v8, /device:TPU:0, one launch (start us, length us, event | category | flops | bytes accessed | tf_op | source)
XLA Modules:
  0.0 41.0 jit_solution(3438371774034892780)
XLA Ops:
  0.6 3.0 %collective-permute-start = (bf16[1,4,32,768]{3,2,1,0:T(8,128)(2,1)}, bf16[1,4,32,768]{3,2,1,0:T(8,128)(2,1)S(1)}, u32[]{:S(2)}, u32[]{:S(2)}) collective-permute-start(bf16[1,4,32,768]{3,2,1,0:T(8,128)(2,1)} %refs_6_.1), channel_id=1, source_target_pairs={{0,2},{1,3},{2,0},{3,1},{4,6},{5,7},{6,4},{7,5},{8,10},{9,11},{10,... | collective-permute-start | bytes 589832 | tf_op jit(solution)/shard_map/ppermute | solution.py:344
  3.7 0.0 collective-permute-start.1
  3.7 5.8 %all-to-all-start = ((bf16[8,16,384]{2,1,0:T(8,128)(2,1)}), bf16[8,16,384]{2,1,0:T(8,128)(2,1)S(1)}, u32[]{:S(2)}, u32[]{:S(2)}) async-start(bf16[8,16,384]{2,1,0:T(8,128)(2,1)} %bitcast.10), calls=%async_computation | async-start | bytes 196608 | tf_op jit(solution)/shard_map/all_to_all | solution.py:347
  9.5 0.0 copy-start
  9.5 0.0 copy-start.1
  9.5 0.0 copy-start.9
  9.5 0.0 copy-start.10
  9.6 0.0 collective-permute-done.refs_3_.refs_7_
  9.6 0.3 collective-permute-start.2
  9.9 0.6 %copy-done = bf16[1,4,32,768]{3,2,1,0:T(8,128)(2,1)S(1)} copy-done((bf16[1,4,32,768]{3,2,1,0:T(8,128)(2,1)S(1)}, bf16[1,4,32,768]{3,2,1,0:T(8,128)(2,1)}, u32[]{:S(2)}) %copy-start) | copy-done | bytes 196632
  10.4 0.1 copy-done.1
  10.5 0.0 copy-done.9
  10.5 0.8 %shard_map.123.refs_2_ = f32[128,768]{1,0:T(8,128)S(1)} custom-call(f32[7,7,768]{2,1,0:T(8,128)S(1)} %copy-done.1, f32[768]{0:T(1024)S(1)} %copy-done.9, f32[8,128]{1,0:T(8,128)S(1)} %shard_map.122.refs_2_, bf16[1,4,32,768]{3,2,1,0:T(8,128)(2,1)S(1)} %copy-done), custom_call_target="tpu_custom_call" | custom-call | flops 2000000000 | bytes 2000000 | tf_op jit(solution)/shard_map/pallas_call | solution.py:39
  11.3 0.0 copy-done.10
  11.3 0.1 shard_map.126.refs_2_.refs_3_
  11.5 0.0 copy-start.2
  11.5 0.0 copy-start.5
  11.5 0.0 copy-start.6
  11.5 0.0 copy-start.7
  11.5 1.7 %shard_map.124 = (f32[128,768]{1,0:T(8,128)S(1)}, bf16[768,1536]{1,0:T(8,128)(2,1)S(1)}) custom-call(f32[7,7,768]{2,1,0:T(8,128)S(1)} %copy-done.1, f32[768]{0:T(1024)S(1)} %copy-done.9, f32[8,128]{1,0:T(8,128)S(1)} %shard_map.122.refs_2_, bf16[1,4,32,768]{3,2,1,0:T(8,128)(2,1)S(1)} %collective-permute-done.refs_3_.refs_7_, bf16[768,1536]{1,0:T(8,128)(2,1)} %refs_10_.3), custom_call_target="tpu_custom_call" | custom-call | flops 2000000000 | bytes 2000000 | tf_op jit(solution)/shard_map/pallas_call | solution.py:39
  13.2 0.0 copy-done.2
  13.2 0.0 collective-permute-done.1.refs_4_
  13.3 0.0 collective-permute-done.2.refs_5_
  13.3 0.0 copy-done.5
  13.3 0.0 copy-done.6
  13.3 0.0 copy-done.7
  13.3 3.9 %shard_map.125 = (bf16[2,32,3072]{2,1,0:T(8,128)(2,1)S(1)}, bf16[128,1536]{1,0:T(8,128)(2,1)S(1)}, bf16[128,768]{1,0:T(8,128)(2,1)S(1)}, bf16[128,768]{1,0:T(8,1...) custom-call(s32[1]{0:T(128)} %bitcast.refs_0_, f32[7,7,768]{2,1,0:T(8,128)S(1)} %copy-done.1, ...), custom_call_target="tpu_custom_call" | custom-call | flops 1207959552 | bytes 9000000 | tf_op jit(solution)/shard_map/pallas_call | solution.py:39
  17.2 0.0 all-to-all-done
  17.2 0.0 copy-start.3
  17.2 0.7 %copy-done.3 = bf16[128,128]{1,0:T(8,128)(2,1)S(1)} copy-done((bf16[128,128]{1,0:T(8,128)(2,1)S(1)}, bf16[128,128]{1,0:T(8,128)(2,1)}, u32[]{:S(2)}) %copy-start.3) | copy-done | bytes 32792
  18.0 0.0 copy-start.4
  18.0 1.9 %shard_map.127 = (bf16[2,32,3072]{2,1,0:T(8,128)(2,1)S(1)}, bf16[2,32,3072]{2,1,0:T(8,128)(2,1)S(1)}, bf16[2048,384]{1,0:T(8,128)(2,1)S(1)}, bf16[512,768]{1,0:T(8,128)(2,1)S(1)}) custom-call(s32[1]{0:T(128)} %bitcast.refs_0_, bf16[128,384]{1,0:T(8,128)(2,1)S(1)} %bitcast.7, bf16[128,128]{1,0:T(8,128)(2,1)S(1)} %copy-done.3, ...), custom_call_target="tpu_custom_call" | custom-call | flops 301989888 | bytes 4000000 | tf_op jit(solution)/shard_map/pallas_call | solution.py:39
  20.0 0.0 copy-start.8
  20.0 0.3 collective-permute-start.4
  20.3 0.3 collective-permute-start.3
  20.5 1.2 %collective-permute-done.4.refs_2_ = bf16[2,32,3072]{2,1,0:T(8,128)(2,1)S(1)} collective-permute-done((bf16[2,32,3072]{2,1,0:T(8,128)(2,1)S(1)}, bf16[2,32,3072]{2,1,0:T(8,128)(2,1)S(1)}, u32[]{:S(2)}, u32[]{:S(2)}) %collective-permute-start.4) | collective-permute-done | bytes 393248 | tf_op jit(solution)/shard_map/ppermute | solution.py:344
  21.8 0.1 shard_map.129
  21.8 0.6 %collective-permute-start.5 = (bf16[32,3072]{1,0:T(8,128)(2,1)S(1)}, bf16[32,3072]{1,0:T(8,128)(2,1)S(1)}, u32[]{:S(2)}, u32[]{:S(2)}) collective-permute-start(bf16[32,3072]{1,0:T(8,128)(2,1)S(1)} %get-tuple-element.24), channel_id=1, source_target_pairs={{0,2},{1,3},{2,0},{3,1},{4,6},{5,7},{6,4},{7,5},{8,10},{9,11},{10,... | collective-permute-start | bytes 589832 | tf_op jit(solution)/shard_map/ppermute | solution.py:344
  22.4 0.0 collective-permute-done.3.refs_2_
  22.4 0.0 copy-done.4
  22.5 0.7 %shard_map.128 = bf16[128,384]{1,0:T(8,128)(2,1)S(1)} custom-call(s32[1]{0:T(128)} %bitcast.refs_0_, bf16[2,32,3072]{2,1,0:T(8,128)(2,1)S(1)} %get-tuple-element.18.refs_1_, bf16[2,32,3072]{2,1,0:T(8,128)(2,1)S(1)} %collective-permute-done.3.refs_2_, bf16[128,128]{1,0:T(8,128)(2,1)S(1)} %copy-done.4, ...), custom_call_target="tpu_custom_call" | custom-call | flops 301989888 | bytes 4000000 | tf_op jit(solution)/shard_map/pallas_call | solution.py:39
  23.2 12.9 %all_to_all.20 = bf16[8,16,384]{2,1,0:T(8,128)(2,1)S(1)} all-to-all(bf16[8,16,384]{2,1,0:T(8,128)(2,1)S(1)} %bitcast.6), channel_id=1, replica_groups=mesh['dp'=8,'space'=4] {'dp'}, dimensions={0} | all-to-all | bytes 196608 | tf_op jit(solution)/shard_map/all_to_all | solution.py:347
  36.1 0.0 collective-permute-done.5.refs_1_
  36.1 0.0 copy-done.8
  36.1 4.2 %shard_map.130 = bf16[1,4,32,768]{3,2,1,0:T(8,128)(2,1)} custom-call(f32[32,3072]{1,0:T(8,128)S(1)} %get-tuple-element.23.refs_0_, bf16[32,3072]{1,0:T(8,128)(2,1)S(1)} %collective-permute-done.5.refs_1_, bf16[128,1536]{1,0:T(8,128)(2,1)S(1)} %get-tuple-element.25.refs_2_, bf16[128,768]{1,0:T(8,128)(2,1)S(1)} %get-tuple-element.26.refs_3_, ...), custom_call_target="tpu_custom_call" | custom-call | flops 603979776 | bytes 9000000 | tf_op jit(solution)/shard_map/pallas_call | solution.py:39
  40.3 0.6 %copy.14 = bf16[1,128,384]{2,1,0:T(8,128)(2,1)} copy(bf16[1,128,384]{2,1,0:T(8,128)(2,1)S(1)} %bitcast.9) | data formatting | bytes 196608
  (1 shorter events, 0.0 us)
Async XLA Ops:
  0.6 8.9 %collective-permute-start = (bf16[1,4,32,768]{3,2,1,0:T(8,128)(2,1)}, bf16[1,4,32,768]{3,2,1,0:T(8,128)(2,1)S(1)}, u32[]{:S(2)}, u32[]{:S(2)}) collective-permute-start(bf16[1,4,32,768]{3,2,1,0:T(8,128)(2,1)} %refs_6_.1), channel_id=1, source_target_pairs={{0,2},{1,3},{2,0},{3,1},{4,6},{5,7},{6,4},{7,5},{8,10},{9,11},{10,... | collective-permute-start | bytes 589832 | tf_op jit(solution)/shard_map/ppermute | solution.py:344
  3.7 9.6 %collective-permute-start.1 = (bf16[1,4,32,768]{3,2,1,0:T(8,128)(2,1)}, bf16[1,4,32,768]{3,2,1,0:T(8,128)(2,1)S(1)}, u32[]{:S(2)}, u32[]{:S(2)}) collective-permute-start(bf16[1,4,32,768]{3,2,1,0:T(8,128)(2,1)} %refs_6_.1), channel_id=1, source_target_pairs={{0,1},{1,0},{2,3},{3,2},{4,5},{5,4},{6,7},{7,6},{8,9},{9,8},{10,11... | collective-permute-start | bytes 589832 | tf_op jit(solution)/shard_map/ppermute | solution.py:344
  3.7 13.6 %all-to-all-start = ((bf16[8,16,384]{2,1,0:T(8,128)(2,1)}), bf16[8,16,384]{2,1,0:T(8,128)(2,1)S(1)}, u32[]{:S(2)}, u32[]{:S(2)}) async-start(bf16[8,16,384]{2,1,0:T(8,128)(2,1)} %bitcast.10), calls=%async_computation | async-start | bytes 196608 | tf_op jit(solution)/shard_map/all_to_all | solution.py:347
  9.5 0.9 %copy-start = (bf16[1,4,32,768]{3,2,1,0:T(8,128)(2,1)S(1)}, bf16[1,4,32,768]{3,2,1,0:T(8,128)(2,1)}, u32[]{:S(2)}) copy-start(bf16[1,4,32,768]{3,2,1,0:T(8,128)(2,1)} %refs_6_.1) | copy-start | bytes 589828
  9.5 1.0 %copy-start.1 = (f32[7,7,768]{2,1,0:T(8,128)S(1)}, f32[7,7,768]{2,1,0:T(8,128)}, u32[]{:S(2)}) copy-start(f32[7,7,768]{2,1,0:T(8,128)} %refs_1_.5) | copy-start | bytes 451588
  9.5 1.0 %copy-start.9 = (f32[768]{0:T(1024)S(1)}, f32[768]{0:T(1024)}, u32[]{:S(2)}) copy-start(f32[768]{0:T(1024)} %refs_1_.4) | copy-start | bytes 9220
  9.5 1.8 %copy-start.10 = (s32[1,128,1]{1,2,0:T(1,128)S(1)}, s32[1,128,1]{1,2,0:T(1,128)}, u32[]{:S(2)}) copy-start(s32[1,128,1]{1,2,0:T(1,128)} %param.20) | copy-start | bytes 1540
  9.6 3.7 %collective-permute-start.2 = (bf16[1,4,32,768]{3,2,1,0:T(8,128)(2,1)S(1)}, bf16[1,4,32,768]{3,2,1,0:T(8,128)(2,1)S(1)}, u32[]{:S(2)}, u32[]{:S(2)}) collective-permute-start(bf16[1,4,32,768]{3,2,1,0:T(8,128)(2,1)S(1)} %collective-permute-done.refs_3_.refs_7_), channel_id=1, source_target_pairs={{0,1},{1,0},{2,3},{3,2},{4,5},{5,4},{6,7},{7,6},{8,9},{9,8},{10,11... | collective-permute-start | bytes 589832 | tf_op jit(solution)/shard_map/ppermute | solution.py:344
  11.5 1.8 %copy-start.2 = (bf16[128,128]{1,0:T(8,128)(2,1)}, bf16[128,128]{1,0:T(8,128)(2,1)S(1)}, u32[]{:S(2)}) copy-start(bf16[128,128]{1,0:T(8,128)(2,1)S(1)} %shard_map.126.refs_2_.refs_3_) | copy-start | bytes 98308
  11.5 1.8 %copy-start.5 = (f32[768]{0:T(1024)S(1)}, f32[768]{0:T(1024)}, u32[]{:S(2)}) copy-start(f32[768]{0:T(1024)} %refs_9_.3) | copy-start | bytes 9220
  11.5 1.8 %copy-start.6 = (f32[768]{0:T(1024)S(1)}, f32[768]{0:T(1024)}, u32[]{:S(2)}) copy-start(f32[768]{0:T(1024)} %refs_8_.3) | copy-start | bytes 9220
  11.5 1.8 %copy-start.7 = (f32[768]{0:T(1024)S(1)}, f32[768]{0:T(1024)}, u32[]{:S(2)}) copy-start(f32[768]{0:T(1024)} %refs_7_.1) | copy-start | bytes 9220
  17.2 0.8 %copy-start.3 = (bf16[128,128]{1,0:T(8,128)(2,1)S(1)}, bf16[128,128]{1,0:T(8,128)(2,1)}, u32[]{:S(2)}) copy-start(bf16[128,128]{1,0:T(8,128)(2,1)} %copy-done.2) | copy-start | bytes 98308
  18.0 4.5 %copy-start.4 = (bf16[128,128]{1,0:T(8,128)(2,1)S(1)}, bf16[128,128]{1,0:T(8,128)(2,1)}, u32[]{:S(2)}) copy-start(bf16[128,128]{1,0:T(8,128)(2,1)} %copy-done.2) | copy-start | bytes 98308
  20.0 16.2 %copy-start.8 = (f32[768]{0:T(1024)S(1)}, f32[768]{0:T(1024)}, u32[]{:S(2)}) copy-start(f32[768]{0:T(1024)} %refs_7_.1) | copy-start | bytes 9220
  20.0 1.8 %collective-permute-start.4 = (bf16[2,32,3072]{2,1,0:T(8,128)(2,1)S(1)}, bf16[2,32,3072]{2,1,0:T(8,128)(2,1)S(1)}, u32[]{:S(2)}, u32[]{:S(2)}) collective-permute-start(bf16[2,32,3072]{2,1,0:T(8,128)(2,1)S(1)} %get-tuple-element.22), channel_id=1, source_target_pairs={{0,1},{1,0},{2,3},{3,2},{4,5},{5,4},{6,7},{7,6},{8,9},{9,8},{10,11... | collective-permute-start | bytes 1179656 | tf_op jit(solution)/shard_map/ppermute | solution.py:344
  20.3 2.2 %collective-permute-start.3 = (bf16[2,32,3072]{2,1,0:T(8,128)(2,1)S(1)}, bf16[2,32,3072]{2,1,0:T(8,128)(2,1)S(1)}, u32[]{:S(2)}, u32[]{:S(2)}) collective-permute-start(bf16[2,32,3072]{2,1,0:T(8,128)(2,1)S(1)} %get-tuple-element.18.refs_1_), channel_id=1, source_target_pairs={{0,1},{1,0},{2,3},{3,2},{4,5},{5,4},{6,7},{7,6},{8,9},{9,8},{10,11... | collective-permute-start | bytes 1179656 | tf_op jit(solution)/shard_map/ppermute | solution.py:344
  21.8 14.3 %collective-permute-start.5 = (bf16[32,3072]{1,0:T(8,128)(2,1)S(1)}, bf16[32,3072]{1,0:T(8,128)(2,1)S(1)}, u32[]{:S(2)}, u32[]{:S(2)}) collective-permute-start(bf16[32,3072]{1,0:T(8,128)(2,1)S(1)} %get-tuple-element.24), channel_id=1, source_target_pairs={{0,2},{1,3},{2,0},{3,1},{4,6},{5,7},{6,4},{7,5},{8,10},{9,11},{10,... | collective-permute-start | bytes 589832 | tf_op jit(solution)/shard_map/ppermute | solution.py:344
